TPU v7x, 32 devices: a whole 2x2x4 slice. The times are simulated.
32 devices in a mesh: replica: 4 (over y, x), shard: 8 (over z, core).
Axes of the slice: x: 2, y: 2, z: 4, core: 2. Of those that a mesh axis runs over, the one named last changes fastest.
Arguments:
- tokens: bfloat16 [8192, 2304], P(('replica', 'shard')), may hold values from -6 to 6
- w_query: bfloat16 [2304, 2048], P('shard'), may hold values from -0.375 to 0.375
- w_key: bfloat16 [2304, 1024], P('shard'), may hold values from -0.125 to 0.125
- w_value: bfloat16 [2304, 1024], P('shard'), may hold values from -0.125 to 0.125
- w_output: bfloat16 [2048, 2304], P('shard'), may hold values from -0.125 to 0.125
- gain_attn_in: bfloat16 [2304], P('shard'), may hold values from 0.25 to 1.75
- gain_attn_out: bfloat16 [2304], P('shard'), may hold values from 0.25 to 1.75
- gain_ffn_in: bfloat16 [2304], P('shard'), may hold values from 0.25 to 1.75
- gain_ffn_out: bfloat16 [2304], P('shard'), may hold values from 0.25 to 1.75
- w_gate: bfloat16 [9216, 2304], P('shard'), may hold values from -0.125 to 0.125
- w_up: bfloat16 [9216, 2304], P('shard'), may hold values from -0.125 to 0.125
- w_down: bfloat16 [9216, 2304], P('shard'), may hold values from -0.0625 to 0.0625
- segment_ids: int32 [4, 1024], P('replica'), may hold values from 0 to 3, never falling along the last dimension, each value on 1 to 384 neighbouring positions
- cotangent: bfloat16 [8192, 2304], P(('replica', 'shard')), may hold values from -6 to 6
Outputs:
- output: bfloat16 [8192, 2304], P(('replica', 'shard'))
- input_grad: float32 [8192, 2304], P(('replica', 'shard'))
- grad_query: float32 [2304, 2048], P('shard')
- grad_key: float32 [2304, 1024], P('shard')
- grad_value: float32 [2304, 1024], P('shard')
- grad_out_proj: float32 [2048, 2304], P('shard')
- grad_gain_attn_in: float32 [2304], P('shard')
- grad_gain_attn_out: float32 [2304], P('shard')
- grad_gain_ffn_in: float32 [2304], P('shard')
- grad_gain_ffn_out: float32 [2304], P('shard')
- grad_gate: float32 [9216, 2304], P('shard')
- grad_up: float32 [9216, 2304], P('shard')
- grad_down: float32 [9216, 2304], P('shard')
Inputs may be any that keep to these rules, and one draw needn't show every extreme that they name: `segment_ids`: along a row the ids never fall; every continuation 0 to 3 has one to 384 tokens, and one has exactly 384.
All inputs are finite; a program needn't handle non-finite values.
Results may differ from a plain program's by a relative error of at most 0.028.
Values may be sent and summed in bfloat16 or wider, within the bound.
A program may use at most 320 MiB of HBM per device.

v0:
```python
import jax
import jax.numpy as jnp
from jax import lax
from jax.sharding import PartitionSpec as P

H = 8
KV = 4
HD = 256
PROMPT = 1024


EPS = 1e-06
CAP = 50.0
THETA = 10000.0
NEGATIVE = -1e30


def inv_rms(values):
    return lax.rsqrt(jnp.mean(values * values, axis=-1, keepdims=True) + EPS)


def rms_scaled(values, gain):
    return values * inv_rms(values) * gain


def rotate(values, positions, head_count, head_dim, sign):
    tok_count = values.shape[0]
    half = head_dim // 2
    rates = THETA ** (-(jnp.arange(half, dtype=jnp.float32) * 2.0) / head_dim)
    angles = positions.astype(jnp.float32)[:, None] * rates[None, :]
    cosine = jnp.cos(angles)[:, None, :]
    sine = sign * jnp.sin(angles)[:, None, :]
    shaped = values.reshape(tok_count, head_count, head_dim)
    first = shaped[:, :, :half]
    second = shaped[:, :, half:]
    turned = jnp.concatenate(
        [first * cosine - second * sine, second * cosine + first * sine], axis=-1
    )
    return turned.reshape(tok_count, head_count * head_dim)


def glu_value(gate, up):
    return jax.nn.gelu(gate, approximate=True) * up


def on_device(
    tokens,
    w_query,
    w_key,
    w_value,
    w_output,
    gain_attn_in,
    gain_attn_out,
    gain_ffn_in,
    gain_ffn_out,
    w_gate,
    w_up,
    w_down,
    segment_ids,
    cotangent,
):
    tok_rows = tokens.shape[0]
    query_cols = w_query.shape[1]
    kv_cols = w_key.shape[1]
    group_rows = tok_rows * lax.axis_size("shard")
    head_group = H // KV
    shard_index = lax.axis_index("shard")
    start_row = shard_index * tok_rows
    segment_row = segment_ids[0]
    key_segments = jnp.concatenate([jnp.full((PROMPT,), -1, jnp.int32), segment_row])
    key_index = jnp.arange(group_rows, dtype=jnp.int32)
    query_index = start_row + jnp.arange(tok_rows, dtype=jnp.int32)
    query_segments = lax.dynamic_slice_in_dim(key_segments, start_row, tok_rows)
    earlier = jnp.sum((segment_row[None, :] < query_segments[:, None]).astype(jnp.int32), axis=1)
    positions = query_index - earlier
    visible = (key_index[None, :] <= query_index[:, None]) & (
        (key_index[None, :] < PROMPT) | (key_segments[None, :] == query_segments[:, None])
    )
    gain_stack = jnp.stack([gain_attn_in, gain_attn_out, gain_ffn_in, gain_ffn_out])
    full_query, full_key, full_value, full_out, gains = (
        lax.all_gather(w_query, "shard", axis=0, tiled=True),
        lax.all_gather(w_key, "shard", axis=0, tiled=True),
        lax.all_gather(w_value, "shard", axis=0, tiled=True),
        lax.all_gather(w_output, "shard", axis=0, tiled=True),
        lax.all_gather(gain_stack, "shard", axis=1, tiled=True),
    )
    gain_first = gains[0].astype(jnp.float32)
    gain_second = gains[1].astype(jnp.float32)
    gain_third = gains[2].astype(jnp.float32)
    gain_fourth = gains[3].astype(jnp.float32)
    x_float = tokens.astype(jnp.float32)
    normed = rms_scaled(x_float, gain_first).astype(jnp.bfloat16)
    query_lin = jnp.dot(normed, full_query, preferred_element_type=jnp.float32)
    key_lin = jnp.dot(normed, full_key, preferred_element_type=jnp.float32)
    value_lin = jnp.dot(normed, full_value, preferred_element_type=jnp.float32)
    query_scale = HD ** (-0.5)
    queries = (rotate(query_lin, positions, H, HD, 1.0) * query_scale).astype(jnp.bfloat16)
    keys = rotate(key_lin, positions, KV, HD, 1.0).astype(jnp.bfloat16)
    values = value_lin.astype(jnp.bfloat16)
    group_keys, group_values = (
        lax.all_gather(keys, "shard", axis=0, tiled=True),
        lax.all_gather(values, "shard", axis=0, tiled=True),
    )
    keys_shaped = group_keys.reshape(group_rows, KV, HD)
    values_shaped = group_values.reshape(group_rows, KV, HD)
    query_shaped = queries.reshape(tok_rows, KV, head_group, HD)

    def capped_scores():
        scores = jnp.einsum(
            "qkgd,pkd->kgqp", query_shaped, keys_shaped, preferred_element_type=jnp.float32
        )
        bent = jnp.tanh(scores / CAP)
        return (bent, jnp.where(visible[None, None], CAP * bent, NEGATIVE))

    bent, capped = capped_scores()
    highest = jnp.max(capped, axis=-1, keepdims=True)
    log_total = highest + jnp.log(jnp.sum(jnp.exp(capped - highest), axis=-1, keepdims=True))
    probs = jnp.exp(capped - log_total)
    probs_low = probs.astype(jnp.bfloat16)
    attended = jnp.einsum(
        "kgqp,pkd->qkgd", probs_low, values_shaped, preferred_element_type=jnp.float32
    )
    attended_low = attended.reshape(tok_rows, query_cols).astype(jnp.bfloat16)
    raw_attn = jnp.dot(attended_low, full_out, preferred_element_type=jnp.float32)
    hidden_state = x_float + rms_scaled(raw_attn, gain_second)
    normed_ffn = rms_scaled(hidden_state, gain_third).astype(jnp.bfloat16)
    group_normed = lax.all_gather(normed_ffn, "shard", axis=0, tiled=True)
    gate = jnp.einsum("td,fd->tf", group_normed, w_gate, preferred_element_type=jnp.float32)
    up = jnp.einsum("td,fd->tf", group_normed, w_up, preferred_element_type=jnp.float32)
    glu = glu_value(gate, up).astype(jnp.bfloat16)
    raw_ffn = lax.psum_scatter(
        jnp.dot(glu, w_down, preferred_element_type=jnp.float32).astype(jnp.bfloat16),
        "shard",
        scatter_dimension=0,
        tiled=True,
    ).astype(jnp.float32)
    output = (hidden_state + rms_scaled(raw_ffn, gain_fourth)).astype(jnp.bfloat16)
    grad_top = cotangent.astype(jnp.float32)
    _, pull_fourth = jax.vjp(rms_scaled, raw_ffn, gain_fourth)
    d_raw_ffn, grad_gain_fourth = pull_fourth(grad_top)
    d_raw_low = d_raw_ffn.astype(jnp.bfloat16)
    group_d_raw = lax.all_gather(d_raw_low, "shard", axis=0, tiled=True)
    grad_down = jnp.einsum("tf,td->fd", glu, group_d_raw, preferred_element_type=jnp.float32)
    d_glu = jnp.einsum("td,fd->tf", group_d_raw, w_down, preferred_element_type=jnp.float32)
    _, pull_glu = jax.vjp(glu_value, gate, up)
    d_gate, d_up = pull_glu(d_glu)
    d_gate_low = d_gate.astype(jnp.bfloat16)
    d_up_low = d_up.astype(jnp.bfloat16)
    grad_gate = jnp.einsum(
        "tf,td->fd", d_gate_low, group_normed, preferred_element_type=jnp.float32
    )
    grad_up = jnp.einsum("tf,td->fd", d_up_low, group_normed, preferred_element_type=jnp.float32)
    gate_part = jnp.dot(d_gate_low, w_gate, preferred_element_type=jnp.float32)
    up_part = jnp.dot(d_up_low, w_up, preferred_element_type=jnp.float32)
    d_normed_ffn = lax.psum_scatter(
        (gate_part + up_part).astype(jnp.bfloat16), "shard", scatter_dimension=0, tiled=True
    ).astype(jnp.float32)
    _, pull_third = jax.vjp(rms_scaled, hidden_state, gain_third)
    d_hidden_part, grad_gain_third = pull_third(d_normed_ffn)
    d_hidden = grad_top + d_hidden_part
    _, pull_second = jax.vjp(rms_scaled, raw_attn, gain_second)
    d_raw_attn, grad_gain_second = pull_second(d_hidden)
    d_raw_attn_low = d_raw_attn.astype(jnp.bfloat16)
    picked = attended_low
    grad_out_proj = lax.psum_scatter(
        jnp.einsum("tf,td->fd", picked, d_raw_attn_low, preferred_element_type=jnp.float32).astype(
            jnp.bfloat16
        ),
        "shard",
        scatter_dimension=0,
        tiled=True,
    ).astype(jnp.float32)
    d_attended_low = jnp.einsum(
        "td,fd->tf", d_raw_attn_low, full_out, preferred_element_type=jnp.float32
    ).astype(jnp.bfloat16)
    d_attended_shaped = d_attended_low.reshape(tok_rows, KV, head_group, HD)
    bent_again, capped_again = capped_scores()
    probs_again = jnp.exp(capped_again - log_total)
    probs_again_low = probs_again.astype(jnp.bfloat16)
    d_probs = jnp.einsum(
        "qkgd,pkd->kgqp", d_attended_shaped, values_shaped, preferred_element_type=jnp.float32
    )
    d_capped = probs_again * (d_probs - jnp.sum(probs_again * d_probs, axis=-1, keepdims=True))
    d_scores_low = (d_capped * (1.0 - bent_again * bent_again)).astype(jnp.bfloat16)
    d_queries = jnp.einsum(
        "kgqp,pkd->qkgd", d_scores_low, keys_shaped, preferred_element_type=jnp.float32
    ).reshape(tok_rows, query_cols)
    d_keys_group = jnp.einsum(
        "kgqp,qkgd->pkd", d_scores_low, query_shaped, preferred_element_type=jnp.float32
    ).reshape(group_rows, kv_cols)
    d_values_group = jnp.einsum(
        "kgqp,qkgd->pkd", probs_again_low, d_attended_shaped, preferred_element_type=jnp.float32
    ).reshape(group_rows, kv_cols)
    d_keys, d_values = (
        lax.psum_scatter(
            d_keys_group.astype(jnp.bfloat16), "shard", scatter_dimension=0, tiled=True
        ).astype(jnp.float32),
        lax.psum_scatter(
            d_values_group.astype(jnp.bfloat16), "shard", scatter_dimension=0, tiled=True
        ).astype(jnp.float32),
    )
    d_query_low = rotate(d_queries * query_scale, positions, H, HD, -1.0).astype(jnp.bfloat16)
    d_key_low = rotate(d_keys, positions, KV, HD, -1.0).astype(jnp.bfloat16)
    d_value_low = d_values.astype(jnp.bfloat16)
    d_normed = jnp.einsum("tf,df->td", d_query_low, full_query, preferred_element_type=jnp.float32)
    d_normed = d_normed + jnp.einsum(
        "tf,df->td", d_key_low, full_key, preferred_element_type=jnp.float32
    )
    d_normed = d_normed + jnp.einsum(
        "tf,df->td", d_value_low, full_value, preferred_element_type=jnp.float32
    )
    _, pull_first = jax.vjp(rms_scaled, x_float, gain_first)
    d_input_part, grad_gain_first = pull_first(d_normed)
    input_grad = d_hidden + d_input_part
    d_projected = jnp.concatenate([d_query_low, d_key_low, d_value_low], axis=1)
    picked = normed
    grad_projected = lax.psum_scatter(
        jnp.einsum("tc,tf->cf", picked, d_projected, preferred_element_type=jnp.float32).astype(
            jnp.bfloat16
        ),
        "shard",
        scatter_dimension=0,
        tiled=True,
    ).astype(jnp.float32)
    grad_query = grad_projected[:, :query_cols]
    grad_key = grad_projected[:, query_cols : query_cols + kv_cols]
    grad_value = grad_projected[:, query_cols + kv_cols :]
    gain_terms = jnp.stack([grad_gain_first, grad_gain_second, grad_gain_third, grad_gain_fourth])
    gain_shares = lax.psum_scatter(
        gain_terms.astype(jnp.bfloat16), "shard", scatter_dimension=1, tiled=True
    ).astype(jnp.float32)
    grad_query, grad_key, grad_value, grad_out_proj, gain_shares, grad_gate, grad_up, grad_down = (
        lax.psum(grad_query.astype(jnp.bfloat16), "replica").astype(jnp.float32),
        lax.psum(grad_key.astype(jnp.bfloat16), "replica").astype(jnp.float32),
        lax.psum(grad_value.astype(jnp.bfloat16), "replica").astype(jnp.float32),
        lax.psum(grad_out_proj.astype(jnp.bfloat16), "replica").astype(jnp.float32),
        lax.psum(gain_shares.astype(jnp.bfloat16), "replica").astype(jnp.float32),
        lax.psum(grad_gate.astype(jnp.bfloat16), "replica").astype(jnp.float32),
        lax.psum(grad_up.astype(jnp.bfloat16), "replica").astype(jnp.float32),
        lax.psum(grad_down.astype(jnp.bfloat16), "replica").astype(jnp.float32),
    )
    return (
        output,
        input_grad,
        grad_query,
        grad_key,
        grad_value,
        grad_out_proj,
        gain_shares[0],
        gain_shares[1],
        gain_shares[2],
        gain_shares[3],
        grad_gate,
        grad_up,
        grad_down,
    )


def solution(mesh):
    placed = (
        P(("replica", "shard"), None),
        P("shard", None),
        P("shard", None),
        P("shard", None),
        P("shard", None),
        P("shard"),
        P("shard"),
        P("shard"),
        P("shard"),
        P("shard", None),
        P("shard", None),
        P("shard", None),
        P("replica", None),
        P(("replica", "shard"), None),
    )
    return jax.shard_map(
        on_device,
        mesh=mesh,
        in_specs=placed,
        out_specs=(
            P(("replica", "shard"), None),
            P(("replica", "shard"), None),
            P("shard", None),
            P("shard", None),
            P("shard", None),
            P("shard", None),
            P("shard"),
            P("shard"),
            P("shard"),
            P("shard"),
            P("shard", None),
            P("shard", None),
            P("shard", None),
        ),
        check_vma=False,
    )
```

profile of v0, /device:TPU:0, one launch (start us, length us, event | category | flops | bytes accessed | tf_op | source)
XLA Modules:
  0.0 1786.2 jit_solution(15343301327467958355)
XLA Ops:
  11.5 15.7 all-gather
  29.5 34.6 %all-gather.10.cloned.1.call-done = bf16[2304,1024]{1,0:T(8,128)(2,1)} async-done(((bf16[288,1024]{1,0:T(8,128)(2,1)}), bf16[2304,1024]{1,0:T(8,128)(2,1)}) %all-gather.10.cloned.1.call-update) | async-done | bytes 4718608 | tf_op jit(solution)/shard_map/all_gather | solution.py:83
  71.4 45.0 %all-gather.14.cloned.1.call-done = bf16[2304,1024]{1,0:T(8,128)(2,1)} async-done(((bf16[288,1024]{1,0:T(8,128)(2,1)}), bf16[2304,1024]{1,0:T(8,128)(2,1)}) %all-gather.14.cloned.1.call-update) | async-done | bytes 4718608 | tf_op jit(solution)/shard_map/all_gather | solution.py:82
  126.9 37.6 %all-gather.12.cloned.1.call-done = bf16[2048,1024]{1,0:T(8,128)(2,1)} async-done(((bf16[256,1024]{1,0:T(8,128)(2,1)}), bf16[2048,1024]{1,0:T(8,128)(2,1)}) %all-gather.12.cloned.1.call-update) | async-done | bytes 4194320 | tf_op jit(solution)/shard_map/all_gather | solution.py:102
  172.4 83.0 %all-gather.18.cloned.1.call-done = bf16[2304,2048]{1,0:T(8,128)(2,1)} async-done(((bf16[288,2048]{1,0:T(8,128)(2,1)}), bf16[2304,2048]{1,0:T(8,128)(2,1)}) %all-gather.18.cloned.1.call-update) | async-done | bytes 9437200 | tf_op jit(solution)/shard_map/all_gather | solution.py:81
  262.3 41.5 %all-gather.16.cloned.1.call-done = bf16[2048,1024]{0,1:T(8,128)(2,1)} async-done(((bf16[256,1024]{0,1:T(8,128)(2,1)}), bf16[2048,1024]{0,1:T(8,128)(2,1)}) %all-gather.16.cloned.1.call-update) | async-done | bytes 4194320 | tf_op jit(solution)/shard_map/all_gather | solution.py:101
  317.8 10.0 fusion.43
  327.8 66.4 %all-gather.20.cloned.1.call-done = bf16[2048,2304]{1,0:T(8,128)(2,1)} async-done(((bf16[256,2304]{1,0:T(8,128)(2,1)}), bf16[2048,2304]{1,0:T(8,128)(2,1)}) %all-gather.20.cloned.1.call-update) | async-done | bytes 9437200 | tf_op jit(solution)/shard_map/all_gather | solution.py:84
  405.5 89.3 %all-gather.22.cloned.1.call-done = bf16[2048,2304]{1,0:T(8,128)(2,1)} async-done(((bf16[256,2304]{1,0:T(8,128)(2,1)}), bf16[2048,2304]{1,0:T(8,128)(2,1)}) %all-gather.22.cloned.1.call-update) | async-done | bytes 9437200 | tf_op jit(solution)/shard_map/all_gather | solution.py:127
  494.8 18.7 %fusion.83 = f32[2048,1152]{1,0:T(8,128)} fusion(bf16[2048,2304]{1,0:T(8,128)(2,1)} %all-gather.22.cloned.1.call-done, bf16[1152,2304]{1,0:T(8,128)(2,1)} %param.23), kind=kOutput, calls=%fused_computation.159 | convolution fusion | flops 10871635968 | bytes 24182784 | tf_op jit(solution)/shard_map/td,fd->tf/dot_general | solution.py:128
  513.5 21.7 %multiply_convert_fusion.1 = (bf16[2048,1152]{1,0:T(8,128)(2,1)}, f32[2048,1152]{1,0:T(8,128)}) fusion(f32[2048,1152]{1,0:T(8,128)} %fusion.83, bf16[2048,2304]{1,0:T(8,128)(2,1)} %all-gather.22.cloned.1.call-done, bf16[1152,2304]{1,0:T(8,128)(2,1)} %param.24), kind=kOutput, calls=%fused_computation.28 | convolution fusion | flops 10895228928 | bytes 38338560 | tf_op jit(solution)/shard_map/td,fd->tf/dot_general | solution.py:129
  535.2 16.9 convolution_convert_fusion.2
  552.3 97.9 %reduce-scatter.10.cloned.1.call-done = bf16[256,2304]{1,0:T(8,128)(2,1)} async-done(((bf16[2048,2304]{1,0:T(8,128)(2,1)}), bf16[256,2304]{1,0:T(8,128)(2,1)}) %reduce-scatter.10.cloned.1.call-update) | async-done | bytes 1179664 | tf_op jit(solution)/shard_map/reduce_scatter | solution.py:131
  658.0 89.2 %all-gather.24.cloned.1.call-done = bf16[2048,2304]{1,0:T(8,128)(2,1)} async-done(((bf16[256,2304]{1,0:T(8,128)(2,1)}), bf16[2048,2304]{1,0:T(8,128)(2,1)}) %all-gather.24.cloned.1.call-update) | async-done | bytes 9437200 | tf_op jit(solution)/shard_map/all_gather | solution.py:142
  747.1 29.1 %multiply_convert_fusion = (bf16[2048,1152]{1,0:T(8,128)(2,1)}, bf16[2048,1152]{1,0:T(8,128)(2,1)}) fusion(f32[2048,1152]{1,0:T(8,128)} %fusion.83, f32[2048,1152]{1,0:T(8,128)} %get-tuple-element.64, bf16[2048,2304]{1,0:T(8,128)(2,1)} %all-gather.24.cloned.1.call-done, bf16[1152,2304]{1,0:T(8,128)(2,1)} %param.25), kind=kOutput, calls=%fused_computation.27 | convolution fusion | flops 10928259072 | bytes 43057152 | tf_op jit(solution)/shard_map/td,fd->tf/dot_general | solution.py:144
  776.2 18.6 %fusion.84 = f32[2048,2304]{1,0:T(8,128)} fusion(bf16[2048,1152]{1,0:T(8,128)(2,1)} %get-tuple-element.40, bf16[1152,2304]{1,0:T(8,128)(2,1)} %param.23), kind=kOutput, calls=%fused_computation.160 | convolution fusion | flops 10871635968 | bytes 28901376 | tf_op jit(solution)/shard_map/dot_general | solution.py:153
  794.8 19.4 %add_convert_fusion = bf16[2048,2304]{1,0:T(8,128)(2,1)} fusion(f32[2048,2304]{1,0:T(8,128)} %fusion.84, bf16[2048,1152]{1,0:T(8,128)(2,1)S(1)} %copy-done.49, bf16[1152,2304]{1,0:T(8,128)(2,1)} %param.24), kind=kOutput, calls=%fused_computation.2 | convolution fusion | flops 10881073152 | bytes 38338560 | tf_op jit(solution)/shard_map/dot_general | solution.py:154
  814.3 98.1 %reduce-scatter.12.cloned.1.call-done = bf16[256,2304]{1,0:T(8,128)(2,1)} async-done(((bf16[2048,2304]{1,0:T(8,128)(2,1)}), bf16[256,2304]{1,0:T(8,128)(2,1)}) %reduce-scatter.12.cloned.1.call-update) | async-done | bytes 1179664 | tf_op jit(solution)/shard_map/reduce_scatter | solution.py:155
  926.4 10.4 fusion.14
  936.8 28.1 %bitcast_convert_fusion.1 = bf16[4,256,2048]{2,1,0:T(8,128)(2,1)} fusion(bf16[256,4,2,256]{3,0,2,1:T(8,128)(2,1)} %bitcast.175, f32[4,2048,256,2]{2,1,3,0:T(8,128)} %fusion.14, f32[4,2048,256,2]{2,1,3,0:T(8,128)} %copy-done.9, f32[4,2,256]{2,1,0:T(2,128)S(1)} %bitcast.184, pred[256,2048]{0,1:T(8,128)(4,1)S(1)} %copy-done.21), kind=kOutput, calls=%fused_computation.32 | convolution fusion | flops 2212499456 | bytes 39329792 | tf_op jit(solution)/shard_map/kgqp,qkgd->pkd/dot_general | solution.py:188
  964.9 11.6 bitcast_convert_fusion
  976.6 27.4 %convolution_multiply_fusion = f32[4,256,2,256]{3,1,2,0:T(8,128)} fusion(bf16[2048,4,256,1]{0,2,3,1:T(8,128)(2,1)} %bitcast.192, f32[4,2048,256,2]{2,1,3,0:T(8,128)} %fusion.14, f32[4,2048,256,2]{2,1,3,0:T(8,128)} %copy-done.9, f32[4,2,256]{2,1,0:T(2,128)S(1)} %bitcast.186, pred[256,2048]{0,1:T(8,128)(4,1)S(1)} %copy-done.21), kind=kOutput, calls=%fused_computation.92 | convolution fusion | flops 2210926592 | bytes 40378368 | tf_op jit(solution)/shard_map/kgqp,pkd->qkgd/dot_general | solution.py:185
  1020.5 43.8 %reduce-scatter.16.cloned.1.call-done = bf16[256,1024]{0,1:T(8,128)(2,1)} async-done(((bf16[2048,1024]{0,1:T(8,128)(2,1)}), bf16[256,1024]{0,1:T(8,128)(2,1)}) %reduce-scatter.16.cloned.1.call-update) | async-done | bytes 524304 | tf_op jit(solution)/shard_map/reduce_scatter | solution.py:198
  1065.6 10.5 convolution_convert_fusion
  1083.3 17.5 convolution_convert_fusion.3
  1100.7 17.3 convolution_convert_fusion.4
  1118.2 13.7 convolution_convert_fusion.5
  1145.0 117.3 %reduce-scatter.18.cloned.1.call-done = bf16[288,4096]{1,0:T(8,128)(2,1)} async-done(((bf16[2304,4096]{1,0:T(8,128)(2,1)}), bf16[288,4096]{1,0:T(8,128)(2,1)}) %reduce-scatter.18.cloned.1.call-update) | async-done | bytes 2359312 | tf_op jit(solution)/shard_map/reduce_scatter | solution.py:217
  1267.1 95.9 %reduce-scatter.20.cloned.1.call-done = bf16[256,2304]{1,0:T(8,128)(2,1)} async-done(((bf16[2048,2304]{1,0:T(8,128)(2,1)}), bf16[256,2304]{1,0:T(8,128)(2,1)}) %reduce-scatter.20.cloned.1.call-update) | async-done | bytes 1179664 | tf_op jit(solution)/shard_map/reduce_scatter | solution.py:165
  1368.4 26.3 %reduce-scatter.22.cloned.1.call-done = bf16[288,4]{1,0:T(8,128)(2,1)} async-done(((bf16[2304,4]{1,0:T(8,128)(2,1)}), bf16[288,4]{1,0:T(8,128)(2,1)}) %reduce-scatter.22.cloned.1.call-update) | async-done | bytes 2320
  1395.7 9.8 psum.60
  1406.1 349.2 %all-reduce.4.cloned.1.call-done = (bf16[288,2048]{1,0:T(8,128)(2,1)}, bf16[288,1024]{1,0:T(8,128)(2,1)}, bf16[288,1024]{1,0:T(8,128)(2,1)}, bf16[256,2304]{1,0:...) async-done(((bf16[288,2048]{1,0:T(8,128)(2,1)}, bf16[288,1024]{1,0:T(8,128)(2,1)}, bf16[288,1024]{1,0:T(8,128)(2,1)}, ...) | async-done | bytes 19464208 | tf_op jit(solution)/shard_map/psum | solution.py:233
  (265 shorter events, 159.6 us)
Async XLA Ops:
  7.2 56.9 %all-gather.10.cloned.1.call-start = ((), (), s32[]{:S(2)}) async-start(), calls=%async_computation.7 | async-start | bytes 5308416 | tf_op jit(solution)/shard_map/all_gather | solution.py:83
  7.9 108.5 %all-gather.14.cloned.1.call-start = ((), (), s32[]{:S(2)}) async-start(), calls=%async_computation.9 | async-start | bytes 5308416 | tf_op jit(solution)/shard_map/all_gather | solution.py:82
  8.7 155.9 %all-gather.12.cloned.1.call-start = ((), (), s32[]{:S(2)}) async-start(), calls=%async_computation.8 | async-start | bytes 4718592 | tf_op jit(solution)/shard_map/all_gather | solution.py:102
  27.4 228.1 %copy-start.27 = (f32[2304]{0:T(1024)}, f32[2304]{0:T(1024)S(1)}, u32[]{:S(2)}) copy-start(f32[2304]{0:T(1024)S(1)} %get-tuple-element.24) | copy-start | bytes 27652
  27.4 373.4 %copy-start.29 = (f32[2304]{0:T(1024)}, f32[2304]{0:T(1024)S(1)}, u32[]{:S(2)}) copy-start(f32[2304]{0:T(1024)S(1)} %get-tuple-element.23) | copy-start | bytes 27652
  27.4 375.4 %copy-start.32 = (f32[2304]{0:T(1024)}, f32[2304]{0:T(1024)S(1)}, u32[]{:S(2)}) copy-start(f32[2304]{0:T(1024)S(1)} %get-tuple-element.22) | copy-start | bytes 27652
  27.4 627.6 %copy-start.31 = (f32[2304]{0:T(1024)}, f32[2304]{0:T(1024)S(1)}, u32[]{:S(2)}) copy-start(f32[2304]{0:T(1024)S(1)} %get-tuple-element.21) | copy-start | bytes 27652
  29.5 225.9 %copy-start.33 = (f32[256]{0:T(256)}, f32[256]{0:T(256)S(1)}, u32[]{:S(2)}) copy-start(f32[256]{0:T(256)S(1)} %fusion.51) | copy-start | bytes 3076
  69.2 186.3 %all-gather.18.cloned.1.call-start = ((), (), s32[]{:S(2)}) async-start(), calls=%async_computation.11 | async-start | bytes 10616832 | tf_op jit(solution)/shard_map/all_gather | solution.py:81
  69.7 234.0 %all-gather.16.cloned.1.call-start = ((), (), s32[]{:S(2)}) async-start(), calls=%async_computation.10 | async-start | bytes 4718592 | tf_op jit(solution)/shard_map/all_gather | solution.py:101
  71.4 190.2 %copy-start.18 = (f32[256,128]{1,0:T(8,128)}, f32[256,128]{1,0:T(8,128)S(1)}, u32[]{:S(2)}) copy-start(f32[256,128]{1,0:T(8,128)S(1)} %get-tuple-element.58) | copy-start | bytes 393220
  124.6 269.7 %all-gather.20.cloned.1.call-start = ((), (), s32[]{:S(2)}) async-start(), calls=%async_computation.12 | async-start | bytes 10616832 | tf_op jit(solution)/shard_map/all_gather | solution.py:84
  125.1 369.7 %all-gather.22.cloned.1.call-start = ((), (), s32[]{:S(2)}) async-start(), calls=%async_computation.13 | async-start | bytes 10616832 | tf_op jit(solution)/shard_map/all_gather | solution.py:127
  126.9 190.8 %copy-start.20 = (pred[256,2048]{0,1:T(8,128)(4,1)}, pred[256,2048]{0,1:T(8,128)(4,1)S(1)}, u32[]{:S(2)}) copy-start(pred[256,2048]{0,1:T(8,128)(4,1)S(1)} %fusion.42) | copy-start | bytes 1572868
  327.8 72.9 %copy-start.12 = (bf16[4,256,2,256]{3,1,2,0:T(8,128)(2,1)}, bf16[4,256,2,256]{3,1,2,0:T(8,128)(2,1)S(1)}, u32[]{:S(2)}) copy-start(bf16[4,256,2,256]{3,1,2,0:T(8,128)(2,1)S(1)} %fusion.43) | copy-start | bytes 3145732
  402.8 110.7 %copy-start.45 = (f32[256]{0:T(256)}, f32[256]{0:T(256)S(1)}, u32[]{:S(2)}) copy-start(f32[256]{0:T(256)S(1)} %get-tuple-element.37) | copy-start | bytes 3076
  405.5 244.8 %reduce-scatter.10.cloned.1.call-start = ((), (), s32[]{:S(2)}) async-start(), calls=%async_computation.14 | async-start | bytes 10616832 | tf_op jit(solution)/shard_map/reduce_scatter | solution.py:131
  552.1 99.8 %copy-start.11 = (bf16[256,2304]{1,0:T(8,128)(2,1)S(1)}, bf16[256,2304]{1,0:T(8,128)(2,1)}, u32[]{:S(2)}) copy-start(bf16[256,2304]{1,0:T(8,128)(2,1)} %param.27) | copy-start | bytes 3538948
  552.1 195.0 %all-gather.24.cloned.1.call-start = ((), (), s32[]{:S(2)}) async-start(), calls=%async_computation.15 | async-start | bytes 10616832 | tf_op jit(solution)/shard_map/all_gather | solution.py:142
  651.8 124.4 %copy-start.42 = (f32[256]{0:T(256)}, f32[256]{0:T(256)S(1)}, u32[]{:S(2)}) copy-start(f32[256]{0:T(256)S(1)} %fusion.54) | copy-start | bytes 3076
  657.9 254.4 %reduce-scatter.12.cloned.1.call-start = ((), (), s32[]{:S(2)}) async-start(), calls=%async_computation.16 | async-start | bytes 10616832 | tf_op jit(solution)/shard_map/reduce_scatter | solution.py:155
  814.2 98.2 %copy-start.1 = (f32[256,2304]{1,0:T(8,128)S(1)}, f32[256,2304]{1,0:T(8,128)}, u32[]{:S(2)}) copy-start(f32[256,2304]{1,0:T(8,128)} %copy-done) | copy-start | bytes 7077892
  814.2 101.9 %copy-start.8 = (bf16[256,2304]{1,0:T(8,128)(2,1)S(1)}, bf16[256,2304]{1,0:T(8,128)(2,1)}, u32[]{:S(2)}) copy-start(bf16[256,2304]{1,0:T(8,128)(2,1)} %reduce-scatter.10.cloned.1.call-done) | copy-start | bytes 3538948
  814.2 101.9 %copy-start.30 = (f32[2304]{0:T(1024)S(1)}, f32[2304]{0:T(1024)}, u32[]{:S(2)}) copy-start(f32[2304]{0:T(1024)} %copy-done.29) | copy-start | bytes 27652
  814.2 101.9 %copy-start.40 = (f32[256]{0:T(256)S(1)}, f32[256]{0:T(256)}, u32[]{:S(2)}) copy-start(f32[256]{0:T(256)} %copy-done.39) | copy-start | bytes 3076
  814.2 199.2 %reduce-scatter.14.cloned.1.call-start = ((), (), s32[]{:S(2)}) async-start(), calls=%async_computation.17 | async-start | bytes 4718592 | tf_op jit(solution)/shard_map/reduce_scatter | solution.py:195
  964.9 99.4 %reduce-scatter.16.cloned.1.call-start = ((), (), s32[]{:S(2)}) async-start(), calls=%async_computation.18 | async-start | bytes 4718592 | tf_op jit(solution)/shard_map/reduce_scatter | solution.py:198
  976.5 285.8 %reduce-scatter.18.cloned.1.call-start = ((), (), s32[]{:S(2)}) async-start(), calls=%async_computation.19 | async-start | bytes 21233664 | tf_op jit(solution)/shard_map/reduce_scatter | solution.py:217
  1020.5 55.6 %copy-start.15 = (bf16[32,8,4,256]{3,1,2,0:T(8,128)(2,1)}, bf16[32,8,4,256]{3,1,2,0:T(8,128)(2,1)S(1)}, u32[]{:S(2)}) copy-start(bf16[32,8,4,256]{3,1,2,0:T(8,128)(2,1)S(1)} %copy.138) | copy-start | bytes 1572868
  1076.1 286.9 %reduce-scatter.20.cloned.1.call-start = ((), (), s32[]{:S(2)}) async-start(), calls=%async_computation.20 | async-start | bytes 10616832 | tf_op jit(solution)/shard_map/reduce_scatter | solution.py:165
  1082.6 312.1 %reduce-scatter.22.cloned.1.call-start = ((), (), s32[]{:S(2)}) async-start(), calls=%async_computation.21 | async-start | bytes 663552
  1145.0 610.3 %all-reduce.4.cloned.1.call-start = ((), (), s32[]{:S(2)}) async-start(), calls=%async_computation.22 | async-start | bytes 38928384 | tf_op jit(solution)/shard_map/psum | solution.py:233
  (52 other events, 811.1 us)
Sparse Core Ops, SparseCore 0:
  9.7 54.4 all-gather.9
  65.8 50.5 all-gather.13
  118.6 45.9 all-gather.11
  166.0 89.3 all-gather.17
  257.5 46.2 all-gather.15
  305.2 88.9 all-gather.19
  405.6 89.1 all-gather.21
  552.2 97.9 reduce-scatter.9
  658.0 89.0 all-gather.23
  814.3 97.9 reduce-scatter.11
  965.0 48.3 reduce-scatter.13
  1016.1 48.1 reduce-scatter.15
  1076.2 186.1 reduce-scatter.17
  1265.1 97.8 reduce-scatter.19
  1365.1 29.5 reduce-scatter.21
  1400.5 354.7 all-reduce.3
where the time goes:
time: 1790 us
  waiting for transfers between devices  1320 us (74%)
  matrix products  318 us (18%)
  other arithmetic  60.7 us (3%)
  local copies, waits for them, and re-layouts  44.5 us (2%)
  blocking collectives  25.5 us (1%)
    psum x1, waiting for transfers between devices, on_device(): lax.psum(grad_query.astype(jnp.bfloat16), 'replica').astype(jnp.float32)  349 us
    reduce_scatter x1, waiting for transfers between devices, on_device(): lax.psum_scatter(jnp.einsum('tc,tf->cf', picked, d_projected, preferred_e...  117 us
    reduce_scatter x1, waiting for transfers between devices, on_device(): lax.psum_scatter((gate_part + up_part).astype(jnp.bfloat16), 'shard', sca...  98.1 us
    reduce_scatter x1, waiting for transfers between devices, on_device(): lax.psum_scatter(jnp.dot(glu, w_down, preferred_element_type=jnp.float32)...  97.9 us
    reduce_scatter x1, waiting for transfers between devices, on_device(): lax.psum_scatter(jnp.einsum('tf,td->fd', picked, d_raw_attn_low, preferre...  95.9 us
    all_gather x1, waiting for transfers between devices, on_device(): group_normed = lax.all_gather(normed_ffn, 'shard', axis=0, tiled=True)  89.3 us
    all_gather x1, waiting for transfers between devices, on_device(): group_d_raw = lax.all_gather(d_raw_low, 'shard', axis=0, tiled=True)  89.2 us
    all_gather x1, waiting for transfers between devices, on_device(): lax.all_gather(w_query, 'shard', axis=0, tiled=True)  83 us
  transfers between devices with their start and end apart: 16, of which 16 were waited for; matrix products, arithmetic and copies ran while one was open for 11% of the time, Pallas kernels for 0%

commit v1 on v0

--- a/solution.py
+++ b/solution.py
@@ -1,6 +1,10 @@
+import functools
+
 import jax
 import jax.numpy as jnp
 from jax import lax
+from jax.experimental import pallas as pl
+from jax.experimental.pallas import tpu as pltpu
 from jax.sharding import PartitionSpec as P
 
 H = 8
@@ -256,6 +260,477 @@
     )
 
 
+BLOCK = 256
+HALF = HD // 2
+QUARTER = HD // 4
+NT = (((1,), (1,)), ((), ()))
+TN = (((0,), (0,)), ((), ()))
+F32 = jnp.float32
+BF16 = jnp.bfloat16
+
+
+def dot(a, b, dims=(((1,), (0,)), ((), ()))):
+    return lax.dot_general(a, b, dims, preferred_element_type=F32)
+
+
+def turn(x, cosine, sine):
+    return x * cosine + pltpu.roll(x, QUARTER, 1) * sine
+
+
+def qkv_kernel(x_ref, gain_ref, w_ref, tab_ref, normed_ref, q_ref, kv_ref):
+    core = lax.rem(lax.axis_index("shard"), 2)
+    x = x_ref[...].astype(F32)
+    normed = (x * inv_rms(x) * gain_ref[...]).astype(BF16)
+    normed_ref[...] = normed
+    lin = dot(normed, w_ref[...])
+    tab = tab_ref[...]
+    c0, s0, c1, s1 = (tab[:, i * HALF : (i + 1) * HALF] for i in range(4))
+    scale = HD ** (-0.5)
+    q_ref[:, :HALF] = (turn(lin[:, :HALF], c0, s0) * scale).astype(BF16)
+    q_ref[:, HALF:] = (turn(lin[:, HALF:HD], c1, s1) * scale).astype(BF16)
+    first = core == 0
+    ck = jnp.where(first, c0, c1)
+    sk = jnp.where(first, s0, s1)
+    kv_ref[:, :HALF] = turn(lin[:, HD : HD + HALF], ck, sk).astype(BF16)
+    kv_ref[:, HALF:] = lin[:, HD + HALF :].astype(BF16)
+
+
+def visible_block(low_row, i, j):
+    key = j * BLOCK + lax.broadcasted_iota(jnp.int32, (BLOCK, BLOCK), 0)
+    query = i * BLOCK + lax.broadcasted_iota(jnp.int32, (BLOCK, BLOCK), 1)
+    return (key <= query) & (key >= low_row)
+
+
+def block_ranges(i):
+    whole = PROMPT // BLOCK
+    full = jnp.minimum(i, whole)
+    return full, full, i + 1
+
+
+def attend_kernel(q_ref, k_ref, v_ref, low_ref, wo_ref, att_ref, lse_ref, part_ref):
+    i = pl.program_id(0)
+    q = q_ref[...]
+    low_row = low_ref[...]
+
+    def step(j, carry, masked):
+        acc, total = carry
+        rows = pl.ds(pl.multiple_of(j * BLOCK, BLOCK), BLOCK)
+        s = dot(k_ref[rows, :], q, NT)
+        p = jnp.exp(CAP * jnp.tanh(s * (1.0 / CAP)))
+        if masked:
+            p = jnp.where(visible_block(low_row, i, j), p, 0.0)
+        total = total + jnp.sum(p, axis=0, keepdims=True)
+        acc = acc + dot(v_ref[rows, :], p.astype(BF16), TN)
+        return acc, total
+
+    full, start, stop = block_ranges(i)
+    carry = (jnp.zeros((HD, BLOCK), F32), jnp.zeros((1, BLOCK), F32))
+    carry = lax.fori_loop(0, full, functools.partial(step, masked=False), carry)
+    acc, total = lax.fori_loop(start, stop, functools.partial(step, masked=True), carry)
+    lse_ref[...] = jnp.log(total)
+    att = (acc / total).T.astype(BF16)
+    att_ref[...] = att
+    part_ref[...] = dot(att, wo_ref[...]).astype(BF16)
+
+
+def attend_back_kernel(
+    q_ref, k_ref, v_ref, low_ref, lse_ref, att_ref, g_ref, wo_ref, tab_ref,
+    dq_ref, dk_ref, dv_ref, go_ref, dk_acc, dv_acc, go_acc,
+):
+    i = pl.program_id(0)
+
+    @pl.when(i == 0)
+    def _():
+        dk_acc[...] = jnp.zeros_like(dk_acc)
+        dv_acc[...] = jnp.zeros_like(dv_acc)
+        go_acc[...] = jnp.zeros_like(go_acc)
+
+    q = q_ref[...]
+    g = g_ref[...]
+    att = att_ref[...]
+    low_row = low_ref[...]
+    lse_row = lse_ref[...]
+    go_acc[...] += dot(att, g, TN)
+    da = dot(g, wo_ref[...], NT).astype(BF16)
+    weighted = da.astype(F32) * att.astype(F32)
+    d_row = jnp.sum(weighted.T, axis=0, keepdims=True)
+
+    def step(j, dq, masked):
+        rows = pl.ds(pl.multiple_of(j * BLOCK, BLOCK), BLOCK)
+        k = k_ref[rows, :]
+        bent = jnp.tanh(dot(k, q, NT) * (1.0 / CAP))
+        p = jnp.exp(CAP * bent - lse_row)
+        if masked:
+            p = jnp.where(visible_block(low_row, i, j), p, 0.0)
+        dp = dot(v_ref[rows, :], da, NT)
+        ds = (p * (dp - d_row) * (1.0 - bent * bent)).astype(BF16)
+        dk_acc[rows, :] += dot(ds, q)
+        dv_acc[rows, :] += dot(p.astype(BF16), da)
+        return dq + dot(ds, k, TN)
+
+    full, start, stop = block_ranges(i)
+    dq = jnp.zeros((BLOCK, HD), F32)
+    dq = lax.fori_loop(0, full, functools.partial(step, masked=False), dq)
+    dq = lax.fori_loop(start, stop, functools.partial(step, masked=True), dq)
+    dq = dq * HD ** (-0.5)
+    tab = tab_ref[...]
+    c0, s0, c1, s1 = (tab[:, n * HALF : (n + 1) * HALF] for n in range(4))
+    dq_ref[:, :HALF] = turn(dq[:, :HALF], c0, -s0).astype(BF16)
+    dq_ref[:, HALF:] = turn(dq[:, HALF:], c1, -s1).astype(BF16)
+
+    @pl.when(i == pl.num_programs(0) - 1)
+    def _():
+        dk_ref[...] = dk_acc[...].astype(BF16)
+        dv_ref[...] = dv_acc[...].astype(BF16)
+        go_ref[...] = go_acc[...].astype(BF16)
+
+
+def rows_spec(cols):
+    return pl.BlockSpec((BLOCK, cols), lambda i: (i, 0))
+
+
+def whole_spec(rows, cols):
+    return pl.BlockSpec((rows, cols), lambda i: (0, 0))
+
+
+def lane_spec():
+    return pl.BlockSpec((1, BLOCK), lambda i: (0, i))
+
+
+def kernel_params():
+    return pltpu.CompilerParams(
+        dimension_semantics=("arbitrary",), vmem_limit_bytes=48 * 1024 * 1024
+    )
+
+
+def qkv_call(x, gain, weights, table):
+    rows, width = x.shape
+    cols = weights.shape[1]
+    return pl.pallas_call(
+        qkv_kernel,
+        grid=(rows // BLOCK,),
+        in_specs=[rows_spec(width), whole_spec(1, width), whole_spec(width, cols), rows_spec(cols)],
+        out_specs=[rows_spec(width), rows_spec(HD), rows_spec(HD)],
+        out_shape=[
+            jax.ShapeDtypeStruct((rows, width), BF16),
+            jax.ShapeDtypeStruct((rows, HD), BF16),
+            jax.ShapeDtypeStruct((rows, HD), BF16),
+        ],
+        compiler_params=kernel_params(),
+        cost_estimate=pl.CostEstimate(
+            flops=2 * rows * width * cols, bytes_accessed=4 * rows * width, transcendentals=0
+        ),
+        name="qkv",
+    )(x, gain, weights, table)
+
+
+def attend_call(q, k, v, low_row, wo):
+    rows = q.shape[0]
+    width = wo.shape[1]
+    return pl.pallas_call(
+        attend_kernel,
+        grid=(rows // BLOCK,),
+        in_specs=[
+            rows_spec(HD), whole_spec(rows, HD), whole_spec(rows, HD), lane_spec(),
+            whole_spec(HD, width),
+        ],
+        out_specs=[rows_spec(HD), lane_spec(), rows_spec(width)],
+        out_shape=[
+            jax.ShapeDtypeStruct((rows, HD), BF16),
+            jax.ShapeDtypeStruct((1, rows), F32),
+            jax.ShapeDtypeStruct((rows, width), BF16),
+        ],
+        compiler_params=kernel_params(),
+        cost_estimate=pl.CostEstimate(
+            flops=3 * rows * rows * HD + 2 * rows * width * HD,
+            bytes_accessed=2 * rows * width,
+            transcendentals=rows * rows,
+        ),
+        name="attend",
+    )(q, k, v, low_row, wo)
+
+
+def attend_back_call(q, k, v, low_row, lse, att, g, wo, table):
+    rows = q.shape[0]
+    width = wo.shape[1]
+    return pl.pallas_call(
+        attend_back_kernel,
+        grid=(rows // BLOCK,),
+        in_specs=[
+            rows_spec(HD), whole_spec(rows, HD), whole_spec(rows, HD), lane_spec(), lane_spec(),
+            rows_spec(HD), rows_spec(width), whole_spec(HD, width), rows_spec(4 * HALF),
+        ],
+        out_specs=[
+            rows_spec(HD), whole_spec(rows, HD), whole_spec(rows, HD), whole_spec(HD, width),
+        ],
+        out_shape=[
+            jax.ShapeDtypeStruct((rows, HD), BF16),
+            jax.ShapeDtypeStruct((rows, HD), BF16),
+            jax.ShapeDtypeStruct((rows, HD), BF16),
+            jax.ShapeDtypeStruct((HD, width), BF16),
+        ],
+        scratch_shapes=[
+            pltpu.VMEM((rows, HD), F32),
+            pltpu.VMEM((rows, HD), F32),
+            pltpu.VMEM((HD, width), F32),
+        ],
+        compiler_params=kernel_params(),
+        cost_estimate=pl.CostEstimate(
+            flops=6 * rows * rows * HD + 4 * rows * width * HD,
+            bytes_accessed=2 * rows * width,
+            transcendentals=rows * rows,
+        ),
+        name="attend_back",
+    )(q, k, v, low_row, lse, att, g, wo, table)
+
+
+def swap_cores(x):
+    n = lax.axis_size("shard")
+    return lax.ppermute(x, "shard", [(s, s ^ 1) for s in range(n)])
+
+
+def gather(x, axis_name, axis):
+    return lax.all_gather(x, axis_name, axis=axis, tiled=True)
+
+
+def scatter(x, axis_name, axis):
+    return lax.psum_scatter(x, axis_name, scatter_dimension=axis, tiled=True)
+
+
+def partner(x, bit, after=None):
+    n = lax.axis_size("replica")
+    got = lax.ppermute(x, "replica", [(r, r ^ bit) for r in range(n)])
+    return got if after is None else lax.optimization_barrier((got, after))[0]
+
+
+def halve(x, axis, bit, after=None):
+    half = x.shape[axis] // 2
+    mine = lax.rem(lax.axis_index("replica") // bit, 2)
+    kept = lax.dynamic_slice_in_dim(x, mine * half, half, axis)
+    sent = lax.dynamic_slice_in_dim(x, (1 - mine) * half, half, axis)
+    return (kept.astype(F32) + partner(sent, bit, after).astype(F32)).astype(BF16)
+
+
+def double(x, axis, bit, after=None):
+    other = partner(x, bit, after)
+    mine = lax.rem(lax.axis_index("replica") // bit, 2) == 0
+    return jnp.concatenate(
+        [jnp.where(mine, x, other), jnp.where(mine, other, x)], axis=axis
+    )
+
+
+def sum_replicas(x, after=(None, None, None, None)):
+    half = x.shape[0] // 2
+    parts = []
+    for piece, first, second in ((x[:half], 1, 2), (x[half:], 2, 1)):
+        piece = halve(halve(piece, 0, first, after[0]), 0, second, after[1])
+        parts.append(double(double(piece, 0, second, after[2]), 0, first, after[3]))
+    return jnp.concatenate(parts).astype(F32)
+
+
+def exchange(x):
+    return lax.all_to_all(x, "shard", 0, 0, tiled=True)
+
+
+def fast_on_device(
+    tokens,
+    w_query,
+    w_key,
+    w_value,
+    w_output,
+    gain_attn_in,
+    gain_attn_out,
+    gain_ffn_in,
+    gain_ffn_out,
+    w_gate,
+    w_up,
+    w_down,
+    segment_ids,
+    cotangent,
+):
+    tok_rows, width = tokens.shape
+    w_rows = w_query.shape[0]
+    shards = lax.axis_size("shard")
+    replicas = lax.axis_size("replica")
+    group_rows = tok_rows * shards
+    shard_index = lax.axis_index("shard")
+    first_core = lax.rem(shard_index, 2) == 0
+    piece = w_rows // replicas
+
+    x_group = gather(tokens, "shard", 0)
+    gain_stack = jnp.stack([gain_attn_in, gain_attn_out, gain_ffn_in, gain_ffn_out])
+    gains = gather(gain_stack, "shard", 1).astype(F32)
+
+    start = lax.axis_index("replica") * piece
+    wq = lax.dynamic_slice_in_dim(w_query, start, piece)
+    wk = lax.dynamic_slice_in_dim(w_key, start, piece)
+    wv = lax.dynamic_slice_in_dim(w_value, start, piece)
+    sent = jnp.concatenate(
+        [
+            wq.reshape(piece, H, 2, 2, QUARTER).swapaxes(2, 3).reshape(piece, H, HD),
+            wk.reshape(piece, KV, 2, 2, QUARTER).swapaxes(2, 3).reshape(piece, H, HALF),
+            wv.reshape(piece, H, HALF),
+        ],
+        axis=2,
+    ).swapaxes(0, 1)
+    head_w = gather(exchange(sent), "replica", 1).reshape(width, 2 * HD)
+
+    segment_row = segment_ids[0]
+    smaller = jnp.sum((segment_row[:, None] < segment_row[None, :]).astype(jnp.int32), axis=0)
+    earlier = jnp.concatenate([jnp.zeros((PROMPT,), jnp.int32), PROMPT + smaller])
+    index = jnp.arange(group_rows, dtype=jnp.int32)
+    low_row = earlier[None, :]
+    positions = jnp.where(index < PROMPT, index, index - (earlier - PROMPT))
+    rates = THETA ** (-(jnp.arange(HALF, dtype=F32) * 2.0) / HD)
+    angles = positions.astype(F32)[:, None] * rates[None, :]
+    cosine = jnp.cos(angles)
+    sine = jnp.sin(angles)
+    table = jnp.concatenate(
+        [
+            cosine[:, :QUARTER], cosine[:, :QUARTER], -sine[:, :QUARTER], sine[:, :QUARTER],
+            cosine[:, QUARTER:], cosine[:, QUARTER:], -sine[:, QUARTER:], sine[:, QUARTER:],
+        ],
+        axis=1,
+    )
+
+    normed, queries, kv_own = qkv_call(x_group, gains[0:1], head_w, table)
+    kv_other = swap_cores(kv_own)
+    kv_low = jnp.where(first_core, kv_own, kv_other)
+    kv_high = jnp.where(first_core, kv_other, kv_own)
+    keys = jnp.concatenate([kv_low[:, :HALF], kv_high[:, :HALF]], axis=1)
+    values = jnp.concatenate([kv_low[:, HALF:], kv_high[:, HALF:]], axis=1)
+    attended, lse, raw_part = attend_call(queries, keys, values, low_row, w_output)
+    raw_attn = scatter(raw_part, "shard", 0).astype(F32)
+
+    x_float = tokens.astype(F32)
+    grad_top = cotangent.astype(F32)
+    chunks = 2
+    size = tok_rows // chunks
+
+    hidden_parts, normed_groups, raw_parts = [], [], []
+    glus, gates, ups = [], [], []
+    for c in range(chunks):
+        rows = slice(c * size, (c + 1) * size)
+        hidden = x_float[rows] + rms_scaled(raw_attn[rows], gains[1])
+        hidden_parts.append(hidden)
+        normed_groups.append(gather(rms_scaled(hidden, gains[2]).astype(BF16), "shard", 0))
+    for c in range(chunks):
+        gate = jnp.einsum("td,fd->tf", normed_groups[c], w_gate, preferred_element_type=F32)
+        up = jnp.einsum("td,fd->tf", normed_groups[c], w_up, preferred_element_type=F32)
+        glu = glu_value(gate, up).astype(BF16)
+        gates.append(gate)
+        ups.append(up)
+        glus.append(glu)
+        raw_parts.append(scatter(dot(glu, w_down).astype(BF16), "shard", 0).astype(F32))
+    outs, d_groups, gain_four = [], [], []
+    for c in range(chunks):
+        rows = slice(c * size, (c + 1) * size)
+        outs.append((hidden_parts[c] + rms_scaled(raw_parts[c], gains[3])).astype(BF16))
+        _, pull = jax.vjp(rms_scaled, raw_parts[c], gains[3])
+        d_raw, g4 = pull(grad_top[rows])
+        gain_four.append(g4)
+        d_groups.append(gather(d_raw.astype(BF16), "shard", 0))
+    d_normed_parts, d_gates, d_ups = [], [], []
+    for c in range(chunks):
+        d_glu = jnp.einsum("td,fd->tf", d_groups[c], w_down, preferred_element_type=F32)
+        _, pull = jax.vjp(glu_value, gates[c], ups[c])
+        d_gate, d_up = pull(d_glu)
+        d_gate, d_up = d_gate.astype(BF16), d_up.astype(BF16)
+        d_gates.append(d_gate)
+        d_ups.append(d_up)
+        part = (dot(d_gate, w_gate) + dot(d_up, w_up)).astype(BF16)
+        d_normed_parts.append(scatter(part, "shard", 0).astype(F32))
+
+    def over_tokens(left, right):
+        total = dot(left[0], right[0], TN)
+        for c in range(1, chunks):
+            total = total + dot(left[c], right[c], TN)
+        return total.astype(BF16)
+
+    sum_down = over_tokens(glus, d_groups)
+    sum_gate = over_tokens(d_gates, normed_groups)
+    sum_up = over_tokens(d_ups, normed_groups)
+    d_normed_parts[-1] = lax.optimization_barrier(
+        (d_normed_parts[-1], sum_down, sum_gate, sum_up)
+    )[0]
+
+    d_hiddens, d_raws, gain_two, gain_three = [], [], [], []
+    for c in range(chunks):
+        rows = slice(c * size, (c + 1) * size)
+        _, pull = jax.vjp(rms_scaled, hidden_parts[c], gains[2])
+        part, g3 = pull(d_normed_parts[c])
+        d_hidden = grad_top[rows] + part
+        _, pull = jax.vjp(rms_scaled, raw_attn[rows], gains[1])
+        d_raw, g2 = pull(d_hidden)
+        gain_two.append(g2)
+        gain_three.append(g3)
+        d_hiddens.append(d_hidden)
+        d_raws.append(d_raw.astype(BF16))
+    d_hidden = jnp.concatenate(d_hiddens)
+    d_raw_low = jnp.concatenate(d_raws)
+    d_raw_group = gather(d_raw_low, "shard", 0)
+
+    dq, dk, dv, grad_out = attend_back_call(
+        queries, keys, values, low_row, lse, attended, d_raw_group, w_output, table
+    )
+    grad_down = sum_replicas(sum_down, (d_raw_low, None, None, dq))
+    grad_gate = sum_replicas(sum_gate, (d_raw_low, None, None, dq))
+    grad_up = sum_replicas(sum_up, (d_raw_low, dq, None, None))
+    dkv_low = jnp.concatenate([dk[:, :HALF], dv[:, :HALF]], axis=1)
+    dkv_high = jnp.concatenate([dk[:, HALF:], dv[:, HALF:]], axis=1)
+    dkv_mine = jnp.where(first_core, dkv_low, dkv_high).astype(F32)
+    dkv = dkv_mine + swap_cores(jnp.where(first_core, dkv_high, dkv_low)).astype(F32)
+    dk_half = dkv[:, :HALF]
+    own = jnp.where(first_core, table[:, :HD], table[:, HD:])
+    turned = jnp.concatenate([dk_half[:, QUARTER:], dk_half[:, :QUARTER]], axis=1)
+    dk_lin = dk_half * own[:, :HALF] - turned * own[:, HALF:]
+    d_lin = jnp.concatenate([dq, dk_lin.astype(BF16), dkv[:, HALF:].astype(BF16)], axis=1)
+    part, d_lin = lax.optimization_barrier((dot(d_lin, head_w, NT).astype(BF16), d_lin))
+    d_normed = scatter(part, "shard", 0).astype(F32)
+    grad_head = dot(normed, d_lin, TN)
+    gain_one = jnp.sum(grad_head * head_w.astype(F32), axis=1) / gains[0]
+    _, pull = jax.vjp(rms_scaled, x_float, gains[0])
+    input_grad = d_hidden + pull(d_normed)[0]
+
+    gain_terms = jnp.stack([gain_one, sum(gain_two), sum(gain_three), sum(gain_four)], axis=1)
+    padded = jnp.pad(gain_terms, ((0, 0), (0, HALF - gain_terms.shape[1])))
+    moved = jnp.concatenate([grad_head, padded], axis=1).astype(BF16)
+    moved = moved.reshape(shards, w_rows, moved.shape[1])
+    cut = HD + HALF
+    left = halve(halve(moved[:, :, :cut], 1, 1), 1, 2)
+    right = halve(halve(moved[:, :, cut:], 1, 2), 1, 1)
+    traded = exchange(jnp.concatenate([left, right], axis=2))
+    left = double(double(traded[:, :, :cut], 1, 2), 1, 1).astype(F32)
+    right = double(double(traded[:, :, cut:], 1, 1), 1, 2).astype(F32)
+    grad_query = (
+        left[:, :, :HD].reshape(H, w_rows, 2, 2, QUARTER).transpose(1, 0, 3, 2, 4)
+    ).reshape(w_rows, H * HD)
+    grad_key = (
+        left[:, :, HD:]
+        .reshape(KV, 2, w_rows, 2, QUARTER)
+        .transpose(2, 0, 3, 1, 4)
+        .reshape(w_rows, KV * HD)
+    )
+    grad_value = right[:, :, :HALF].transpose(1, 0, 2).reshape(w_rows, KV * HD)
+    grad_out_proj = sum_replicas(grad_out)
+    gain_shares = jnp.sum(right[:, :, HALF : HALF + gain_terms.shape[1]], axis=0).T
+    return (
+        jnp.concatenate(outs),
+        input_grad,
+        grad_query,
+        grad_key,
+        grad_value,
+        grad_out_proj,
+        gain_shares[0],
+        gain_shares[1],
+        gain_shares[2],
+        gain_shares[3],
+        grad_gate,
+        grad_up,
+        grad_down,
+    )
+
+
 def solution(mesh):
     placed = (
         P(("replica", "shard"), None),
@@ -273,8 +748,10 @@
         P("replica", None),
         P(("replica", "shard"), None),
     )
+    heads_fit = mesh.shape["shard"] == H and H == 2 * KV and mesh.shape["replica"] == 4
+    body = fast_on_device if heads_fit else on_device
     return jax.shard_map(
-        on_device,
+        body,
         mesh=mesh,
         in_specs=placed,
         out_specs=(

time: 1790 us -> 1160 us (0.65)
  waiting for transfers between devices: 1320 us -> 594 us
  matrix products: 318 us -> 195 us
  Pallas kernels: 0 us -> 68.3 us
  other arithmetic: 60.7 us -> 120 us
  starting transfers between devices: 1.05 us -> 49.1 us
  local copies, waits for them, and re-layouts: 44.5 us -> 71.2 us
    psum x1 -> x0, waiting for transfers between devices: 349 us -> none  [on_device(): lax.psum(grad_query.astype(jnp.bfloat16), 'replica').astype(jnp.float32)]
    reduce_scatter x6, waiting for transfers between devices: 456 us -> 186 us  [scatter(): return lax.psum_scatter(x, axis_name, scatter_dimension=axis, tiled=True)]
    all_gather x8 -> x7, waiting for transfers between devices: 487 us -> 227 us  [gather(): return lax.all_gather(x, axis_name, axis=axis, tiled=True)]
    ppermute x0 -> x42, waiting for transfers between devices: none -> 165 us  [the longest x40 163 us: partner(): got = lax.ppermute(x, 'replica', [(r, r ^ bit) for r in range(n)])]
    dot_general x25 -> x20, matrix products: 318 us -> 195 us  [the longest x14 120 us: dot(): return lax.dot_general(a, b, dims, preferred_element_type=F32)]
    pallas_call x0 -> x3, Pallas kernels: none -> 68.3 us  [the longest x1 33.6 us: attend_back_call(): pl.pallas_call(attend_back_kernel, grid=(rows // BLOCK,), in_specs=[rows_...]
    ppermute x0 -> x42, starting transfers between devices: none -> 43.2 us  [the longest x40 42.9 us: partner(): got = lax.ppermute(x, 'replica', [(r, r ^ bit) for r in range(n)])]
    select_n x0 -> x23, other arithmetic: none -> 28.8 us  [the longest x20 21.3 us: double(): jnp.where(mine, x, other)]
  transfers between devices with their start and end apart: 16 -> 56, of which waited for: 16 -> 31; matrix products, arithmetic and copies ran while one was open for 11% -> 30% of each run, Pallas kernels for 0% -> 3%
where the time goes in v1:
time: 1160 us; the launch traced here: 1150 us
  waiting for transfers between devices  594 us (51%)
  matrix products  195 us (17%)
  other arithmetic  120 us (10%)
  local copies, waits for them, and re-layouts  71.2 us (6%)
  Pallas kernels  68.3 us (6%)
  starting transfers between devices  49.1 us (4%)
  blocking collectives  37.1 us (3%)
  between operations  16.6 us (1%)
    all_gather x7, waiting for transfers between devices, gather(): return lax.all_gather(x, axis_name, axis=axis, tiled=True)  227 us
    reduce_scatter x6, waiting for transfers between devices, scatter(): return lax.psum_scatter(x, axis_name, scatter_dimension=axis, tiled=True)  186 us
    ppermute x40, waiting for transfers between devices, partner(): got = lax.ppermute(x, 'replica', [(r, r ^ bit) for r in range(n)])  163 us
    dot_general x14, matrix products, dot(): return lax.dot_general(a, b, dims, preferred_element_type=F32)  120 us
    ppermute x40, starting transfers between devices, partner(): got = lax.ppermute(x, 'replica', [(r, r ^ bit) for r in range(n)])  42.9 us
    pallas_call x1, Pallas kernels, attend_back_call(): pl.pallas_call(attend_back_kernel, grid=(rows // BLOCK,), in_specs=[rows_...  33.6 us
    dot_general x2, matrix products, fast_on_device(): jnp.einsum('td,fd->tf', d_groups[c], w_down, preferred_element_type=F32)  30.4 us
    unnamed x314, local copies, waits for them, and re-layouts  28.9 us
  transfers between devices with their start and end apart: 56, of which 31 were waited for; matrix products, arithmetic and copies ran while one was open for 30% of the time, Pallas kernels for 3%

profile of v1, /device:TPU:0, one launch (start us, length us, event | category | flops | bytes accessed | tf_op | source)
XLA Modules:
  0.0 1151.7 jit_solution(6930840940688092380)
XLA Ops:
  12.7 23.0 %all_to_all.10 = bf16[8,72,512]{2,1,0:T(8,128)(2,1)S(1)} all-to-all(bf16[8,72,512]{2,1,0:T(8,128)(2,1)S(1)} %copy.133), channel_id=1, replica_groups=mesh['replica'=4,'shard'=8] {'shard'}, dimensions={0} | all-to-all | bytes 1179648 | tf_op jit(solution)/shard_map/all_to_all | solution.py:532
  37.6 14.1 %all-gather = bf16[8,288,4]{1,2,0:T(4,128)(2,1)S(1)} all-gather(bf16[1,288,4]{1,2,0:T(4,128)(2,1)S(1)} %maximum_bitcast_fusion.1), channel_id=1, replica_groups=mesh['replica'=4,'shard'=8] {'shard'}, dimensions={0}, use_global_device_ids=true | all-gather | bytes 20736 | tf_op jit(solution)/shard_map/all_gather | solution.py:493
  75.7 90.0 %all-gather.9.cloned.1.call-done.x_ref = bf16[2048,2304]{1,0:T(8,128)(2,1)} async-done(((bf16[256,2304]{1,0:T(8,128)(2,1)}), bf16[2048,2304]{1,0:T(8,128)(2,1)}) %all-gather.9.cloned.1.call-update) | async-done | bytes 9437200 | tf_op jit(solution)/shard_map/all_gather | solution.py:493
  165.7 12.1 %qkv.1 = (bf16[2048,2304]{1,0:T(8,128)(2,1)}, bf16[2048,256]{1,0:T(8,128)(2,1)S(1)}, bf16[2048,256]{1,0:T(8,128)(2,1)S(1)}) custom-call(bf16[2048,2304]{1,0:T(8,128)(2,1)} %all-gather.9.cloned.1.call-done.x_ref, f32[1,2304]{1,0:T(1,128)S(1)} %get-tuple-element.268.gain_ref, bf16[2304,512]{1,0:T(8,128)(2,1)S(1)} %bitcast.78, f32[2048,512]{1,0:T(8,128)} %concatenate.104.tab_ref), custom_call_target="tpu_custom_call" | custom-call | flops 4831838208 | bytes 18874368 | tf_op jit(solution)/shard_map/qkv/pallas_call | solution.py:409
  185.4 22.7 %attend.1 = (bf16[2048,256]{1,0:T(8,128)(2,1)S(1)}, f32[1,2048]{1,0:T(1,128)S(1)}, bf16[2048,2304]{1,0:T(8,128)(2,1)}) custom-call(bf16[2048,256]{1,0:T(8,128)(2,1)S(1)} %copy-done.8, bf16[2048,256]{1,0:T(8,128)(2,1)S(1)} %pad_maximum_fusion.10.k_ref, bf16[2048,256]{1,0:T(8,128)(2,1)S(1)} %pad_maximum_fusion.11.v_ref, s32[1,2048]{1,0:T(1,128)S(1)} %bitcast.80, ...), custom_call_target="tpu_custom_call" | custom-call | flops 5637144576 | bytes 9437184 | tf_op jit(solution)/shard_map/attend/pallas_call | solution.py:430
  211.9 95.3 %reduce-scatter.7.cloned.1.call-done = bf16[256,2304]{1,0:T(8,128)(2,1)} async-done(((bf16[2048,2304]{1,0:T(8,128)(2,1)}), bf16[256,2304]{1,0:T(8,128)(2,1)}) %reduce-scatter.7.cloned.1.call-update) | async-done | bytes 1179664 | tf_op jit(solution)/shard_map/reduce_scatter | solution.py:497
  313.8 49.2 %all-gather.13.cloned.1.call-done = bf16[1024,2304]{1,0:T(8,128)(2,1)} async-done(((bf16[128,2304]{1,0:T(8,128)(2,1)}), bf16[1024,2304]{1,0:T(8,128)(2,1)}) %all-gather.13.cloned.1.call-update) | async-done | bytes 4718608 | tf_op jit(solution)/shard_map/all_gather | solution.py:493
  363.0 9.9 fusion.69
  372.9 12.5 %multiply_convert_fusion.3 = (bf16[1024,1152]{1,0:T(8,128)(2,1)S(1)}, f32[1024,1152]{1,0:T(8,128)}) fusion(f32[1024,1152]{1,0:T(8,128)S(1)} %fusion.69, bf16[1024,2304]{1,0:T(8,128)(2,1)S(1)} %copy-done.128, bf16[1152,2304]{1,0:T(8,128)(2,1)} %param.24), kind=kOutput, calls=%fused_computation.36 | convolution fusion | flops 5447614464 | bytes 21823488 | tf_op jit(solution)/shard_map/td,fd->tf/dot_general | solution.py:619
  394.7 20.9 %all-gather.15.cloned.1.call-done = bf16[1024,2304]{1,0:T(8,128)(2,1)} async-done(((bf16[128,2304]{1,0:T(8,128)(2,1)}), bf16[1024,2304]{1,0:T(8,128)(2,1)}) %all-gather.15.cloned.1.call-update) | async-done | bytes 4718608 | tf_op jit(solution)/shard_map/all_gather | solution.py:493
  415.6 9.9 fusion.70
  425.5 12.5 %multiply_convert_fusion.2 = (bf16[1024,1152]{1,0:T(8,128)(2,1)S(1)}, f32[1024,1152]{1,0:T(8,128)}) fusion(f32[1024,1152]{1,0:T(8,128)S(1)} %fusion.70, bf16[1024,2304]{1,0:T(8,128)(2,1)S(1)} %copy-done.129, bf16[1152,2304]{1,0:T(8,128)(2,1)} %param.24), kind=kOutput, calls=%fused_computation.35 | convolution fusion | flops 5447614464 | bytes 21823488 | tf_op jit(solution)/shard_map/td,fd->tf/dot_general | solution.py:619
  450.3 21.3 %reduce-scatter.9.cloned.1.call-done = bf16[128,2304]{1,0:T(8,128)(2,1)} async-done(((bf16[1024,2304]{1,0:T(8,128)(2,1)}), bf16[128,2304]{1,0:T(8,128)(2,1)}) %reduce-scatter.9.cloned.1.call-update) | async-done | bytes 589840 | tf_op jit(solution)/shard_map/reduce_scatter | solution.py:497
  472.8 54.4 %reduce-scatter.11.cloned.1.call-done = bf16[128,2304]{1,0:T(8,128)(2,1)} async-done(((bf16[1024,2304]{1,0:T(8,128)(2,1)}), bf16[128,2304]{1,0:T(8,128)(2,1)}) %reduce-scatter.11.cloned.1.call-update) | async-done | bytes 589840 | tf_op jit(solution)/shard_map/reduce_scatter | solution.py:497
  540.5 42.9 %all-gather.19.cloned.1.call-done = bf16[1024,2304]{1,0:T(8,128)(2,1)} async-done(((bf16[128,2304]{1,0:T(8,128)(2,1)}), bf16[1024,2304]{1,0:T(8,128)(2,1)}) %all-gather.19.cloned.1.call-update) | async-done | bytes 4718608 | tf_op jit(solution)/shard_map/all_gather | solution.py:493
  583.4 15.0 %multiply_convert_fusion = (bf16[1024,1152]{1,0:T(8,128)(2,1)S(1)}, bf16[1024,1152]{1,0:T(8,128)(2,1)S(1)}) fusion(f32[1024,1152]{1,0:T(8,128)} %copy-done.134, f32[1024,1152]{1,0:T(8,128)} %get-tuple-element.281, bf16[1024,2304]{1,0:T(8,128)(2,1)} %all-gather.19.cloned.1.call-done, bf16[1152,2304]{1,0:T(8,128)(2,1)} %param.25), kind=kOutput, calls=%fused_computation.33 | convolution fusion | flops 5464129536 | bytes 24182784 | tf_op jit(solution)/shard_map/td,fd->tf/dot_general | solution.py:635
  598.5 10.6 fusion.72
  617.5 18.1 %all-gather.17.cloned.1.call-done = bf16[1024,2304]{1,0:T(8,128)(2,1)} async-done(((bf16[128,2304]{1,0:T(8,128)(2,1)}), bf16[1024,2304]{1,0:T(8,128)(2,1)}) %all-gather.17.cloned.1.call-update) | async-done | bytes 4718608 | tf_op jit(solution)/shard_map/all_gather | solution.py:493
  644.7 9.3 fusion
  659.9 15.4 %multiply_convert_fusion.1 = (bf16[1024,1152]{1,0:T(8,128)(2,1)}, bf16[1024,1152]{1,0:T(8,128)(2,1)}) fusion(f32[1024,1152]{1,0:T(8,128)} %copy-done.133, f32[1024,1152]{1,0:T(8,128)} %get-tuple-element.283, bf16[1024,2304]{1,0:T(8,128)(2,1)} %all-gather.17.cloned.1.call-done, bf16[1152,2304]{1,0:T(8,128)(2,1)S(1)} %bitcast.103), kind=kOutput, calls=%fused_computation.34 | convolution fusion | flops 5464129536 | bytes 24182784 | tf_op jit(solution)/shard_map/td,fd->tf/dot_general | solution.py:635
  700.8 9.3 fusion.2
  720.8 9.8 fusion.1
  732.9 14.9 %reduce-scatter.13.cloned.1.call-done = bf16[128,2304]{1,0:T(8,128)(2,1)} async-done(((bf16[1024,2304]{1,0:T(8,128)(2,1)}), bf16[128,2304]{1,0:T(8,128)(2,1)}) %reduce-scatter.13.cloned.1.call-update) | async-done | bytes 589840 | tf_op jit(solution)/shard_map/reduce_scatter | solution.py:497
  778.5 16.7 %collective-permute-done.18 = bf16[288,2304]{1,0:T(8,128)(2,1)S(1)} collective-permute-done((bf16[288,2304]{1,0:T(8,128)(2,1)S(1)}, bf16[288,2304]{1,0:T(8,128)(2,1)S(1)}, u32[]{:S(2)}, u32[]{:S(2)}) %collective-permute-start.18) | collective-permute-done | bytes 1327136 | tf_op jit(solution)/shard_map/ppermute | solution.py:502
  801.1 10.0 collective-permute-done.35
  813.5 26.0 %collective-permute-done.19 = bf16[144,2304]{1,0:T(8,128)(2,1)S(1)} collective-permute-done((bf16[144,2304]{1,0:T(8,128)(2,1)S(1)}, bf16[144,2304]{1,0:T(8,128)(2,1)S(1)}, u32[]{:S(2)}, u32[]{:S(2)}) %collective-permute-start.19) | collective-permute-done | bytes 663584 | tf_op jit(solution)/shard_map/ppermute | solution.py:502
  842.0 11.8 %collective-permute-done.36 = bf16[144,2304]{1,0:T(8,128)(2,1)S(1)} collective-permute-done((bf16[144,2304]{1,0:T(8,128)(2,1)S(1)}, bf16[144,2304]{1,0:T(8,128)(2,1)S(1)}, u32[]{:S(2)}, u32[]{:S(2)}) %collective-permute-start.36) | collective-permute-done | bytes 663584 | tf_op jit(solution)/shard_map/ppermute | solution.py:502
  875.8 33.6 %attend_back.1 = (bf16[2048,256]{1,0:T(8,128)(2,1)S(1)}, bf16[2048,256]{1,0:T(8,128)(2,1)S(1)}, bf16[2048,256]{1,0:T(8,128)(2,1)S(1)}, bf16[256,2304]{1,0:T(8,128)(2,1)}) custom-call(bf16[2048,256]{1,0:T(8,128)(2,1)S(1)} %copy-done.9, bf16[2048,256]{1,0:T(8,128)(2,1)S(1)} %copy-done.4, bf16[2048,256]{1,0:T(8,128)(2,1)} %copy-done.2, s32[1,2048]{1,0:T(1,128)S(1)} %bitcast.81, ...), custom_call_target="tpu_custom_call" | custom-call | flops 11274289152 | bytes 9437184 | tf_op jit(solution)/shard_map/attend_back/pallas_call | solution.py:456
  918.4 10.2 collective-permute-done.21
  989.7 9.8 fusion.59
  1019.1 20.2 %collective-permute-done.2 = bf16[8,144,384]{2,1,0:T(8,128)(2,1)} collective-permute-done((bf16[8,144,384]{2,1,0:T(8,128)(2,1)}, bf16[8,144,384]{2,1,0:T(8,128)(2,1)}, u32[]{:S(2)}, u32[]{:S(2)}) %collective-permute-start.2) | collective-permute-done | bytes 884768 | tf_op jit(solution)/shard_map/ppermute | solution.py:502
  1067.3 13.8 %all-to-all-done.1 = bf16[8,72,640]{2,1,0:T(8,128)(2,1)} async-done(((bf16[8,72,640]{2,1,0:T(8,128)(2,1)}), bf16[8,72,640]{2,1,0:T(8,128)(2,1)}, u32[]{:S(2)}, u32[]{:S(2)}) %all-to-all-start.1) | async-done | bytes 737312 | tf_op jit(solution)/shard_map/all_to_all | solution.py:532
  (615 shorter events, 390.2 us)
Async XLA Ops:
  7.2 66.1 %all-gather.11.cloned.1.call-start = ((), (), s32[]{:S(2)}) async-start(), calls=%async_computation.9 | async-start | bytes 2949120 | tf_op jit(solution)/shard_map/all_gather | solution.py:493
  36.7 129.0 %all-gather.9.cloned.1.call-start = ((), (), s32[]{:S(2)}) async-start(), calls=%async_computation.8 | async-start | bytes 10616832 | tf_op jit(solution)/shard_map/all_gather | solution.py:493
  37.5 269.7 %reduce-scatter.7.cloned.1.call-start = ((), (), s32[]{:S(2)}) async-start(), calls=%async_computation.10 | async-start | bytes 10616832 | tf_op jit(solution)/shard_map/reduce_scatter | solution.py:497
  209.1 153.9 %all-gather.13.cloned.1.call-start = ((), (), s32[]{:S(2)}) async-start(), calls=%async_computation.11 | async-start | bytes 5308416 | tf_op jit(solution)/shard_map/all_gather | solution.py:493
  312.8 102.8 %all-gather.15.cloned.1.call-start = ((), (), s32[]{:S(2)}) async-start(), calls=%async_computation.13 | async-start | bytes 5308416 | tf_op jit(solution)/shard_map/all_gather | solution.py:493
  313.4 158.2 %reduce-scatter.9.cloned.1.call-start = ((), (), s32[]{:S(2)}) async-start(), calls=%async_computation.12 | async-start | bytes 5308416 | tf_op jit(solution)/shard_map/reduce_scatter | solution.py:497
  394.7 132.5 %reduce-scatter.11.cloned.1.call-start = ((), (), s32[]{:S(2)}) async-start(), calls=%async_computation.14 | async-start | bytes 5308416 | tf_op jit(solution)/shard_map/reduce_scatter | solution.py:497
  447.4 136.0 %all-gather.19.cloned.1.call-start = ((), (), s32[]{:S(2)}) async-start(), calls=%async_computation.17 | async-start | bytes 5308416 | tf_op jit(solution)/shard_map/all_gather | solution.py:493
  533.2 102.4 %all-gather.17.cloned.1.call-start = ((), (), s32[]{:S(2)}) async-start(), calls=%async_computation.15 | async-start | bytes 5308416 | tf_op jit(solution)/shard_map/all_gather | solution.py:493
  533.9 196.7 %reduce-scatter.15.cloned.1.call-start = ((), (), s32[]{:S(2)}) async-start(), calls=%async_computation.18 | async-start | bytes 5308416 | tf_op jit(solution)/shard_map/reduce_scatter | solution.py:497
  617.0 130.8 %reduce-scatter.13.cloned.1.call-start = ((), (), s32[]{:S(2)}) async-start(), calls=%async_computation.16 | async-start | bytes 5308416 | tf_op jit(solution)/shard_map/reduce_scatter | solution.py:497
  655.6 109.1 %collective-permute-start.34 = (bf16[288,2304]{1,0:T(8,128)(2,1)}, bf16[288,2304]{1,0:T(8,128)(2,1)}, u32[]{:S(2)}, u32[]{:S(2)}) collective-permute-start(bf16[288,2304]{1,0:T(8,128)(2,1)} %constant_dynamic-slice_fusion.3), channel_id=1, source_target_pairs={{0,8},{8,0},{16,24},{24,16},{1,9},{9,1},{17,25},{25,17},{2,10},{10... | collective-permute-start | bytes 3981320 | tf_op jit(solution)/shard_map/ppermute | solution.py:502
  658.4 109.7 %collective-permute-start.38 = (bf16[288,2304]{1,0:T(8,128)(2,1)}, bf16[288,2304]{1,0:T(8,128)(2,1)}, u32[]{:S(2)}, u32[]{:S(2)}) collective-permute-start(bf16[288,2304]{1,0:T(8,128)(2,1)} %constant_dynamic-slice_fusion.1), channel_id=1, source_target_pairs={{0,16},{8,24},{16,0},{24,8},{1,17},{9,25},{17,1},{25,9},{2,18},{10... | collective-permute-start | bytes 3981320 | tf_op jit(solution)/shard_map/ppermute | solution.py:502
  691.5 183.1 %all-gather.21.cloned.1.call-start = ((), (), s32[]{:S(2)}) async-start(), calls=%async_computation.19 | async-start | bytes 10616832 | tf_op jit(solution)/shard_map/all_gather | solution.py:493
  711.7 59.3 %collective-permute-start.26 = (bf16[288,2304]{1,0:T(8,128)(2,1)}, bf16[288,2304]{1,0:T(8,128)(2,1)}, u32[]{:S(2)}, u32[]{:S(2)}) collective-permute-start(bf16[288,2304]{1,0:T(8,128)(2,1)} %constant_dynamic-slice_fusion.7), channel_id=1, source_target_pairs={{0,8},{8,0},{16,24},{24,16},{1,9},{9,1},{17,25},{25,17},{2,10},{10... | collective-permute-start | bytes 3981320 | tf_op jit(solution)/shard_map/ppermute | solution.py:502
  714.4 60.4 %collective-permute-start.30 = (bf16[288,2304]{1,0:T(8,128)(2,1)}, bf16[288,2304]{1,0:T(8,128)(2,1)}, u32[]{:S(2)}, u32[]{:S(2)}) collective-permute-start(bf16[288,2304]{1,0:T(8,128)(2,1)} %constant_dynamic-slice_fusion.5), channel_id=1, source_target_pairs={{0,16},{8,24},{16,0},{24,8},{1,17},{9,25},{17,1},{25,9},{2,18},{10... | collective-permute-start | bytes 3981320 | tf_op jit(solution)/shard_map/ppermute | solution.py:502
  760.0 379.4 %reduce-scatter.17.cloned.1.call-start = ((), (), s32[]{:S(2)}) async-start(), calls=%async_computation.20 | async-start | bytes 10616832 | tf_op jit(solution)/shard_map/reduce_scatter | solution.py:497
  768.1 42.9 %collective-permute-start.35 = (bf16[144,2304]{1,0:T(8,128)(2,1)S(1)}, bf16[144,2304]{1,0:T(8,128)(2,1)S(1)}, u32[]{:S(2)}, u32[]{:S(2)}) collective-permute-start(bf16[144,2304]{1,0:T(8,128)(2,1)S(1)} %constant_dynamic-slice_fusion.2), channel_id=1, source_target_pairs={{0,16},{8,24},{16,0},{24,8},{1,17},{9,25},{17,1},{25,9},{2,18},{10... | collective-permute-start | bytes 1990664 | tf_op jit(solution)/shard_map/ppermute | solution.py:502
  770.9 40.9 %collective-permute-start.39 = (bf16[144,2304]{1,0:T(8,128)(2,1)S(1)}, bf16[144,2304]{1,0:T(8,128)(2,1)S(1)}, u32[]{:S(2)}, u32[]{:S(2)}) collective-permute-start(bf16[144,2304]{1,0:T(8,128)(2,1)S(1)} %constant_dynamic-slice_fusion), channel_id=1, source_target_pairs={{0,8},{8,0},{16,24},{24,16},{1,9},{9,1},{17,25},{25,17},{2,10},{10... | collective-permute-start | bytes 1990664 | tf_op jit(solution)/shard_map/ppermute | solution.py:502
  774.8 136.2 %collective-permute-start.27 = (bf16[144,2304]{1,0:T(8,128)(2,1)}, bf16[144,2304]{1,0:T(8,128)(2,1)}, u32[]{:S(2)}, u32[]{:S(2)}) collective-permute-start(bf16[144,2304]{1,0:T(8,128)(2,1)} %constant_dynamic-slice_fusion.6), channel_id=1, source_target_pairs={{0,16},{8,24},{16,0},{24,8},{1,17},{9,25},{17,1},{25,9},{2,18},{10... | collective-permute-start | bytes 1990664 | tf_op jit(solution)/shard_map/ppermute | solution.py:502
  795.2 117.8 %collective-permute-start.31 = (bf16[144,2304]{1,0:T(8,128)(2,1)}, bf16[144,2304]{1,0:T(8,128)(2,1)}, u32[]{:S(2)}, u32[]{:S(2)}) collective-permute-start(bf16[144,2304]{1,0:T(8,128)(2,1)} %constant_dynamic-slice_fusion.4), channel_id=1, source_target_pairs={{0,8},{8,0},{16,24},{24,16},{1,9},{9,1},{17,25},{25,17},{2,10},{10... | collective-permute-start | bytes 1990664 | tf_op jit(solution)/shard_map/ppermute | solution.py:502
  797.1 42.4 %collective-permute-start.19 = (bf16[144,2304]{1,0:T(8,128)(2,1)S(1)}, bf16[144,2304]{1,0:T(8,128)(2,1)S(1)}, u32[]{:S(2)}, u32[]{:S(2)}) collective-permute-start(bf16[144,2304]{1,0:T(8,128)(2,1)S(1)} %constant_dynamic-slice_fusion.10), channel_id=1, source_target_pairs={{0,16},{8,24},{16,0},{24,8},{1,17},{9,25},{17,1},{25,9},{2,18},{10... | collective-permute-start | bytes 1990664 | tf_op jit(solution)/shard_map/ppermute | solution.py:502
  811.8 41.9 %collective-permute-start.36 = (bf16[144,2304]{1,0:T(8,128)(2,1)S(1)}, bf16[144,2304]{1,0:T(8,128)(2,1)S(1)}, u32[]{:S(2)}, u32[]{:S(2)}) collective-permute-start(bf16[144,2304]{1,0:T(8,128)(2,1)S(1)} %add_convert_fusion.10), channel_id=1, source_target_pairs={{0,16},{8,24},{16,0},{24,8},{1,17},{9,25},{17,1},{25,9},{2,18},{10... | collective-permute-start | bytes 1990664 | tf_op jit(solution)/shard_map/ppermute | solution.py:502
  855.6 53.8 %collective-permute-start.37 = (bf16[288,2304]{1,0:T(8,128)(2,1)}, bf16[288,2304]{1,0:T(8,128)(2,1)}, u32[]{:S(2)}, u32[]{:S(2)}) collective-permute-start(bf16[288,2304]{1,0:T(8,128)(2,1)} %pad_maximum_fusion.6), channel_id=1, source_target_pairs={{0,8},{8,0},{16,24},{24,16},{1,9},{9,1},{17,25},{25,17},{2,10},{10... | collective-permute-start | bytes 3981320 | tf_op jit(solution)/shard_map/ppermute | solution.py:502
  865.0 46.0 %collective-permute-start.41 = (bf16[288,2304]{1,0:T(8,128)(2,1)}, bf16[288,2304]{1,0:T(8,128)(2,1)}, u32[]{:S(2)}, u32[]{:S(2)}) collective-permute-start(bf16[288,2304]{1,0:T(8,128)(2,1)} %pad_maximum_fusion.7), channel_id=1, source_target_pairs={{0,16},{8,24},{16,0},{24,8},{1,17},{9,25},{17,1},{25,9},{2,18},{10... | collective-permute-start | bytes 3981320 | tf_op jit(solution)/shard_map/ppermute | solution.py:502
  871.6 57.0 %collective-permute-start.21 = (bf16[288,2304]{1,0:T(8,128)(2,1)}, bf16[288,2304]{1,0:T(8,128)(2,1)}, u32[]{:S(2)}, u32[]{:S(2)}) collective-permute-start(bf16[288,2304]{1,0:T(8,128)(2,1)} %pad_maximum_fusion.2), channel_id=1, source_target_pairs={{0,8},{8,0},{16,24},{24,16},{1,9},{9,1},{17,25},{25,17},{2,10},{10... | collective-permute-start | bytes 3981320 | tf_op jit(solution)/shard_map/ppermute | solution.py:502
  912.2 74.0 %collective-permute-start.28 = (bf16[144,2304]{1,0:T(8,128)(2,1)S(1)}, bf16[144,2304]{1,0:T(8,128)(2,1)}, u32[]{:S(2)}, u32[]{:S(2)}) collective-permute-start(bf16[144,2304]{1,0:T(8,128)(2,1)S(1)} %add_convert_fusion.12), channel_id=1, source_target_pairs={{0,16},{8,24},{16,0},{24,8},{1,17},{9,25},{17,1},{25,9},{2,18},{10... | collective-permute-start | bytes 1990664 | tf_op jit(solution)/shard_map/ppermute | solution.py:502
  915.1 89.8 %collective-permute-start.32 = (bf16[144,2304]{1,0:T(8,128)(2,1)}, bf16[144,2304]{1,0:T(8,128)(2,1)}, u32[]{:S(2)}, u32[]{:S(2)}) collective-permute-start(bf16[144,2304]{1,0:T(8,128)(2,1)} %add_convert_fusion.11), channel_id=1, source_target_pairs={{0,8},{8,0},{16,24},{24,16},{1,9},{9,1},{17,25},{25,17},{2,10},{10... | collective-permute-start | bytes 1990664 | tf_op jit(solution)/shard_map/ppermute | solution.py:502
  983.7 57.4 %collective-permute-start.13 = (bf16[64,2304]{1,0:T(8,128)(2,1)}, bf16[64,2304]{1,0:T(8,128)(2,1)}, u32[]{:S(2)}, u32[]{:S(2)}) collective-permute-start(bf16[64,2304]{1,0:T(8,128)(2,1)} %pad_maximum_fusion.16), channel_id=1, source_target_pairs={{0,8},{8,0},{16,24},{24,16},{1,9},{9,1},{17,25},{25,17},{2,10},{10... | collective-permute-start | bytes 884744 | tf_op jit(solution)/shard_map/ppermute | solution.py:502
  985.0 76.2 %collective-permute-start.17 = (bf16[64,2304]{1,0:T(8,128)(2,1)}, bf16[64,2304]{1,0:T(8,128)(2,1)}, u32[]{:S(2)}, u32[]{:S(2)}) collective-permute-start(bf16[64,2304]{1,0:T(8,128)(2,1)} %pad_maximum_fusion.17), channel_id=1, source_target_pairs={{0,16},{8,24},{16,0},{24,8},{1,17},{9,25},{17,1},{25,9},{2,18},{10... | collective-permute-start | bytes 884744 | tf_op jit(solution)/shard_map/ppermute | solution.py:502
  988.8 75.1 %collective-permute-start.29 = (bf16[288,2304]{1,0:T(8,128)(2,1)}, bf16[288,2304]{1,0:T(8,128)(2,1)}, u32[]{:S(2)}, u32[]{:S(2)}) collective-permute-start(bf16[288,2304]{1,0:T(8,128)(2,1)} %pad_maximum_fusion.4), channel_id=1, source_target_pairs={{0,8},{8,0},{16,24},{24,16},{1,9},{9,1},{17,25},{25,17},{2,10},{10... | collective-permute-start | bytes 3981320 | tf_op jit(solution)/shard_map/ppermute | solution.py:502
  1018.1 65.1 %collective-permute-start.33 = (bf16[288,2304]{1,0:T(8,128)(2,1)}, bf16[288,2304]{1,0:T(8,128)(2,1)}, u32[]{:S(2)}, u32[]{:S(2)}) collective-permute-start(bf16[288,2304]{1,0:T(8,128)(2,1)} %pad_maximum_fusion.5), channel_id=1, source_target_pairs={{0,16},{8,24},{16,0},{24,8},{1,17},{9,25},{17,1},{25,9},{2,18},{10... | collective-permute-start | bytes 3981320 | tf_op jit(solution)/shard_map/ppermute | solution.py:502
  (178 other events, 2046.7 us)
Sparse Core Ops, SparseCore 0:
  36.8 36.3 all-gather.10
  74.9 90.7 all-gather.8
  209.2 97.9 reduce-scatter.6
  312.9 50.0 all-gather.12
  365.0 50.5 all-gather.14
  417.7 53.7 reduce-scatter.8
  473.9 53.3 reduce-scatter.10
  533.3 50.0 all-gather.18
  585.1 50.5 all-gather.16
  638.3 53.7 reduce-scatter.14
  694.4 53.3 reduce-scatter.12
  760.1 89.0 all-gather.20
  969.9 96.3 reduce-scatter.16

commit v2 on v1

--- a/solution.py
+++ b/solution.py
@@ -307,7 +307,7 @@
     return full, full, i + 1
 
 
-def attend_kernel(q_ref, k_ref, v_ref, low_ref, wo_ref, att_ref, lse_ref, part_ref):
+def attend_kernel(q_ref, k_ref, v_ref, low_ref, wo_ref, att_ref, lse_ref, top_ref, end_ref):
     i = pl.program_id(0)
     q = q_ref[...]
     low_row = low_ref[...]
@@ -330,23 +330,53 @@
     lse_ref[...] = jnp.log(total)
     att = (acc / total).T.astype(BF16)
     att_ref[...] = att
-    part_ref[...] = dot(att, wo_ref[...]).astype(BF16)
+    part = dot(att, wo_ref[...]).astype(BF16)
+    top_ref[...] = part[: BLOCK // 2]
+    end_ref[...] = part[BLOCK // 2 :]
+
+
+def swap_copies(sources, targets, bits, sems):
+    return [
+        pltpu.make_async_remote_copy(
+            src_ref=src,
+            dst_ref=dst,
+            send_sem=sems.at[0, n],
+            recv_sem=sems.at[1, n],
+            device_id={"replica": flipped(bit)},
+            device_id_type=pl.DeviceIdType.MESH,
+        )
+        for n, (src, dst, bit) in enumerate(zip(sources, targets, bits))
+    ]
 
 
 def attend_back_kernel(
-    q_ref, k_ref, v_ref, low_ref, lse_ref, att_ref, g_ref, wo_ref, tab_ref,
-    dq_ref, dk_ref, dv_ref, go_ref, dk_acc, dv_acc, go_acc,
+    bits,
+    q_ref, k_ref, v_ref, low_ref, lse_ref, att_ref, top_ref, end_ref, wo_ref, tab_ref,
+    swap_a, swap_b,
+    dq_ref, dk_ref, dv_ref, go_ref, got_a, got_b, dk_acc, dv_acc, go_acc, swap_sem,
 ):
     i = pl.program_id(0)
+    swaps = swap_copies((swap_a, swap_b), (got_a, got_b), bits, swap_sem)
 
     @pl.when(i == 0)
     def _():
+        barrier = pltpu.get_barrier_semaphore()
+        for bit in bits:
+            pl.semaphore_signal(
+                barrier,
+                inc=1,
+                device_id={"replica": flipped(bit)},
+                device_id_type=pl.DeviceIdType.MESH,
+            )
+        pl.semaphore_wait(barrier, len(bits))
+        for swap in swaps:
+            swap.start()
         dk_acc[...] = jnp.zeros_like(dk_acc)
         dv_acc[...] = jnp.zeros_like(dv_acc)
         go_acc[...] = jnp.zeros_like(go_acc)
 
     q = q_ref[...]
-    g = g_ref[...]
+    g = jnp.concatenate([top_ref[...], end_ref[...]])
     att = att_ref[...]
     low_row = low_ref[...]
     lse_row = lse_ref[...]
@@ -383,10 +413,19 @@
         dk_ref[...] = dk_acc[...].astype(BF16)
         dv_ref[...] = dv_acc[...].astype(BF16)
         go_ref[...] = go_acc[...].astype(BF16)
+        for swap in swaps:
+            swap.wait()
+
+
+ANYWHERE = pl.BlockSpec(memory_space=pl.ANY)
 
 
 def rows_spec(cols):
     return pl.BlockSpec((BLOCK, cols), lambda i: (i, 0))
+
+
+def half_spec(cols):
+    return pl.BlockSpec((BLOCK // 2, cols), lambda i: (i, 0))
 
 
 def whole_spec(rows, cols):
@@ -434,11 +473,12 @@
             rows_spec(HD), whole_spec(rows, HD), whole_spec(rows, HD), lane_spec(),
             whole_spec(HD, width),
         ],
-        out_specs=[rows_spec(HD), lane_spec(), rows_spec(width)],
+        out_specs=[rows_spec(HD), lane_spec(), half_spec(width), half_spec(width)],
         out_shape=[
             jax.ShapeDtypeStruct((rows, HD), BF16),
             jax.ShapeDtypeStruct((1, rows), F32),
-            jax.ShapeDtypeStruct((rows, width), BF16),
+            jax.ShapeDtypeStruct((rows // 2, width), BF16),
+            jax.ShapeDtypeStruct((rows // 2, width), BF16),
         ],
         compiler_params=kernel_params(),
         cost_estimate=pl.CostEstimate(
@@ -450,38 +490,612 @@
     )(q, k, v, low_row, wo)
 
 
-def attend_back_call(q, k, v, low_row, lse, att, g, wo, table):
+def attend_back_call(number, q, k, v, low_row, lse, att, top, end, wo, table, swaps):
     rows = q.shape[0]
     width = wo.shape[1]
+    bits = tuple(bit for _, bit in swaps)
+    sent = [x for x, _ in swaps]
     return pl.pallas_call(
-        attend_back_kernel,
+        functools.partial(attend_back_kernel, bits),
         grid=(rows // BLOCK,),
         in_specs=[
             rows_spec(HD), whole_spec(rows, HD), whole_spec(rows, HD), lane_spec(), lane_spec(),
-            rows_spec(HD), rows_spec(width), whole_spec(HD, width), rows_spec(4 * HALF),
+            rows_spec(HD), half_spec(width), half_spec(width), whole_spec(HD, width),
+            rows_spec(4 * HALF), ANYWHERE, ANYWHERE,
         ],
         out_specs=[
             rows_spec(HD), whole_spec(rows, HD), whole_spec(rows, HD), whole_spec(HD, width),
+            ANYWHERE, ANYWHERE,
         ],
         out_shape=[
             jax.ShapeDtypeStruct((rows, HD), BF16),
             jax.ShapeDtypeStruct((rows, HD), BF16),
             jax.ShapeDtypeStruct((rows, HD), BF16),
             jax.ShapeDtypeStruct((HD, width), BF16),
-        ],
+        ]
+        + [jax.ShapeDtypeStruct(x.shape, x.dtype) for x in sent],
         scratch_shapes=[
             pltpu.VMEM((rows, HD), F32),
             pltpu.VMEM((rows, HD), F32),
             pltpu.VMEM((HD, width), F32),
+            pltpu.SemaphoreType.DMA((2, len(bits))),
         ],
-        compiler_params=kernel_params(),
+        compiler_params=pltpu.CompilerParams(
+            dimension_semantics=("arbitrary",),
+            vmem_limit_bytes=48 * 1024 * 1024,
+            collective_id=number,
+            has_side_effects=True,
+        ),
         cost_estimate=pl.CostEstimate(
             flops=6 * rows * rows * HD + 4 * rows * width * HD,
             bytes_accessed=2 * rows * width,
             transcendentals=rows * rows,
         ),
         name="attend_back",
-    )(q, k, v, low_row, lse, att, g, wo, table)
+    )(q, k, v, low_row, lse, att, top, end, wo, table, *sent)
+
+
+def gelu_parts(v):
+    k = (2.0 / jnp.pi) ** 0.5
+    square = v * v
+    bent = jnp.tanh(k * v * (1.0 + 0.044715 * square))
+    half = 0.5 * (1.0 + bent)
+    slope = half + 0.5 * v * (1.0 - bent * bent) * k * (1.0 + 3 * 0.044715 * square)
+    return v * half, slope
+
+
+def flipped(bit):
+    r = lax.axis_index("replica")
+    return r + bit * (1 - 2 * lax.rem(r // bit, 2))
+
+
+def greet_neighbours(chips, bits=()):
+    barrier = pltpu.get_barrier_semaphore()
+    for bit in bits:
+        pl.semaphore_signal(
+            barrier,
+            inc=1,
+            device_id={"replica": flipped(bit)},
+            device_id_type=pl.DeviceIdType.MESH,
+        )
+    me = lax.axis_index("shard")
+    z, core, last = me // 2, lax.rem(me, 2), chips - 1
+
+    def greet(chip, other):
+        pl.semaphore_signal(
+            barrier,
+            inc=1,
+            device_id={"shard": chip * 2 + other},
+            device_id_type=pl.DeviceIdType.MESH,
+        )
+
+    greet(z, 1 - core)
+
+    @pl.when(z > 0)
+    def _():
+        greet(z - 1, core)
+
+    @pl.when(z < last)
+    def _():
+        greet(z + 1, core)
+
+    pl.semaphore_wait(barrier, 1 + len(bits) + jnp.minimum(z, 1) + jnp.minimum(last - z, 1))
+
+
+class Line:
+    def __init__(self, own, buf, sems, chips):
+        self.own, self.buf, self.chips = own, buf, chips
+        self.right, self.left, self.side, self.got, self.got_side = sems
+        me = lax.axis_index("shard")
+        self.z, self.core = me // 2, lax.rem(me, 2)
+        self.rows = own.shape[0]
+
+    def place(self, chip, core):
+        first = pl.multiple_of((chip * 2 + core) * self.rows, self.rows)
+        return self.buf.at[pl.ds(first, self.rows)]
+
+    def move(self, chip, src, send, got, target_chip, target_core):
+        return pltpu.make_async_remote_copy(
+            src_ref=src,
+            dst_ref=self.place(chip, self.core),
+            send_sem=send.at[chip],
+            recv_sem=got.at[chip],
+            device_id={"shard": target_chip * 2 + target_core},
+            device_id_type=pl.DeviceIdType.MESH,
+        )
+
+    def to_right(self, chip, src):
+        return self.move(chip, src, self.right, self.got, self.z + 1, self.core)
+
+    def to_left(self, chip, src):
+        return self.move(chip, src, self.left, self.got, self.z - 1, self.core)
+
+    def to_side(self, chip, src):
+        return self.move(chip, src, self.side, self.got_side, self.z, 1 - self.core)
+
+    def start(self):
+        z, last = self.z, self.chips - 1
+
+        @pl.when(z > 0)
+        def _():
+            self.to_left(z, self.own).start()
+
+        @pl.when(z < last)
+        def _():
+            self.to_right(z, self.own).start()
+
+        self.to_side(z, self.own).start()
+
+    def pass_on(self, hop):
+        z, last = self.z, self.chips - 1
+
+        @pl.when((hop > 0) & (z >= hop))
+        def _():
+            chip = z - hop
+            block = self.place(chip, self.core)
+            self.to_right(chip, block).wait_recv()
+
+            @pl.when(z < last)
+            def _():
+                self.to_right(chip, block).start()
+
+            self.to_side(chip, block).start()
+
+        @pl.when((hop > 0) & (z + hop <= last))
+        def _():
+            chip = z + hop
+            block = self.place(chip, self.core)
+            self.to_left(chip, block).wait_recv()
+
+            @pl.when(z > 0)
+            def _():
+                self.to_left(chip, block).start()
+
+            self.to_side(chip, block).start()
+
+    def chip_at(self, step):
+        z = self.z
+        near = z + 1 - 2 * lax.rem(z, 2)
+        high = z // 2
+        by_step = (z, near, 2 - high, 3 - 3 * high)
+        chip = by_step[0]
+        for n in range(1, 4):
+            chip = jnp.where(step == n, by_step[n], chip)
+        return chip
+
+    def wait_side(self, chip):
+        pltpu.make_async_remote_copy(
+            src_ref=self.place(chip, self.core),
+            dst_ref=self.place(chip, 1 - self.core),
+            send_sem=self.side.at[chip],
+            recv_sem=self.got_side.at[chip],
+            device_id={"shard": self.z * 2 + 1 - self.core},
+            device_id_type=pl.DeviceIdType.MESH,
+        ).wait_recv()
+
+    def finish(self):
+        z, last = self.z, self.chips - 1
+
+        def done(chip, carry):
+            @pl.when((z < last) & (chip <= z))
+            def _():
+                self.to_right(chip, self.place(chip, self.core)).wait_send()
+
+            @pl.when((z > 0) & (chip >= z))
+            def _():
+                self.to_left(chip, self.place(chip, self.core)).wait_send()
+
+            self.to_side(chip, self.place(chip, self.core)).wait_send()
+            return carry
+
+        lax.fori_loop(0, self.chips, done, 0)
+
+
+class Chain:
+    def __init__(self, part, total, total_hbm, bufs, sems, chips):
+        self.part, self.total, self.total_hbm, self.chips = part, total, total_hbm, chips
+        self.mine, self.side, self.from_left, self.from_right, self.stage = bufs
+        (
+            self.mine_sem, self.side_send, self.side_got, self.sent, self.left_got,
+            self.right_got, self.total_sem,
+        ) = sems
+        me = lax.axis_index("shard")
+        self.z, self.core = me // 2, lax.rem(me, 2)
+        self.rows = self.mine.shape[1]
+
+    def block(self, chip, core):
+        first = pl.multiple_of((chip * 2 + core) * self.rows, self.rows)
+        return self.part.at[pl.ds(first, self.rows)]
+
+    def load(self, chip):
+        return pltpu.make_async_copy(
+            self.block(chip, self.core), self.mine.at[chip], self.mine_sem.at[chip]
+        )
+
+    def hand(self, chip):
+        return pltpu.make_async_remote_copy(
+            src_ref=self.block(chip, 1 - self.core),
+            dst_ref=self.side.at[chip],
+            send_sem=self.side_send.at[chip],
+            recv_sem=self.side_got.at[chip],
+            device_id={"shard": self.z * 2 + 1 - self.core},
+            device_id_type=pl.DeviceIdType.MESH,
+        )
+
+    def send(self, chip, dst, got, step):
+        return pltpu.make_async_remote_copy(
+            src_ref=self.stage.at[chip],
+            dst_ref=dst.at[chip],
+            send_sem=self.sent.at[chip],
+            recv_sem=got.at[chip],
+            device_id={"shard": (self.z + step) * 2 + self.core},
+            device_id_type=pl.DeviceIdType.MESH,
+        )
+
+    def to_right(self, chip):
+        return self.send(chip, self.from_left, self.left_got, 1)
+
+    def to_left(self, chip):
+        return self.send(chip, self.from_right, self.right_got, -1)
+
+    def start(self):
+        z, last = self.z, self.chips - 1
+
+        def begin(n, carry):
+            chip = jnp.where(z * 2 <= last, last - n, n)
+            self.hand(chip).start()
+            self.load(chip).start()
+            return carry
+
+        lax.fori_loop(0, self.chips, begin, 0)
+
+    def add(self, dst, chip, others):
+        size = 32
+
+        def some(n, carry):
+            rows = pl.ds(pl.multiple_of(n * size, size), size)
+            value = self.mine[chip, rows, :].astype(F32) + self.side[chip, rows, :].astype(F32)
+            for other in others:
+                value = value + other[chip, rows, :].astype(F32)
+            if dst is self.total:
+                dst[rows, :] = value
+            else:
+                dst[chip, rows, :] = value.astype(BF16)
+            return carry
+
+        lax.fori_loop(0, self.rows // size, some, 0)
+
+    def ready(self, chip):
+        self.load(chip).wait()
+        self.hand(chip).wait_recv()
+
+    def step(self, n):
+        z, last = self.z, self.chips - 1
+
+        @pl.when((n < last) & (z <= n))
+        def _():
+            chip = last - n + z
+            self.ready(chip)
+
+            @pl.when(z == 0)
+            def _():
+                self.add(self.stage, chip, ())
+
+            @pl.when(z > 0)
+            def _():
+                self.to_right(chip).wait_recv()
+                self.add(self.stage, chip, (self.from_left,))
+
+            self.to_right(chip).start()
+
+        @pl.when((n < last) & (last - z <= n))
+        def _():
+            chip = n - last + z
+            self.ready(chip)
+
+            @pl.when(z == last)
+            def _():
+                self.add(self.stage, chip, ())
+
+            @pl.when(z < last)
+            def _():
+                self.to_left(chip).wait_recv()
+                self.add(self.stage, chip, (self.from_right,))
+
+            self.to_left(chip).start()
+
+        @pl.when(n == last)
+        def _():
+            self.ready(z)
+
+            @pl.when(z == 0)
+            def _():
+                self.to_left(z).wait_recv()
+                self.add(self.total, z, (self.from_right,))
+
+            @pl.when(z == last)
+            def _():
+                self.to_right(z).wait_recv()
+                self.add(self.total, z, (self.from_left,))
+
+            @pl.when((z > 0) & (z < last))
+            def _():
+                self.to_left(z).wait_recv()
+                self.to_right(z).wait_recv()
+                self.add(self.total, z, (self.from_left, self.from_right))
+
+            pltpu.make_async_copy(self.total, self.total_hbm, self.total_sem).start()
+
+    def finish(self):
+        z = self.z
+
+        def done(chip, carry):
+            self.hand(chip).wait_send()
+
+            @pl.when(chip != z)
+            def _():
+                self.to_right(chip).wait_send()
+
+            return carry
+
+        lax.fori_loop(0, self.chips, done, 0)
+        pltpu.make_async_copy(self.total, self.total_hbm, self.total_sem).wait()
+
+
+FF_TILE = 384
+
+
+def forward_tiles(rows, buf, weights, ins, outs, acc, part):
+    wg, wu, wd = weights
+    gate, up, glu = outs
+    tiles = wg.shape[0] // FF_TILE
+    for t in range(tiles):
+        cols = slice(t * FF_TILE, (t + 1) * FF_TILE)
+        g = dot(buf[rows, :], wg[cols, :], NT)
+        u = dot(buf[rows, :], wu[cols, :], NT)
+        act = (gelu_parts(g)[0] * u).astype(BF16)
+        gate[rows, cols] = g.astype(BF16)
+        up[rows, cols] = u.astype(BF16)
+        glu[rows, cols] = act
+        more = dot(act, wd[cols, :])
+        add_tile(t, tiles, rows, more, acc, part)
+
+
+def backward_tiles(rows, buf, weights, ins, outs, acc, part):
+    wg, wu, wd = weights
+    gate, up = ins
+    dgate, dup = outs
+    tiles = wg.shape[0] // FF_TILE
+    for t in range(tiles):
+        cols = slice(t * FF_TILE, (t + 1) * FF_TILE)
+        d_act = dot(buf[rows, :], wd[cols, :], NT)
+        value, slope = gelu_parts(gate[rows, cols].astype(F32))
+        dg = (d_act * up[rows, cols].astype(F32) * slope).astype(BF16)
+        du = (d_act * value).astype(BF16)
+        dgate[rows, cols] = dg
+        dup[rows, cols] = du
+        more = dot(dg, wg[cols, :]) + dot(du, wu[cols, :])
+        add_tile(t, tiles, rows, more, acc, part)
+
+
+def add_tile(t, tiles, rows, more, acc, part):
+    if t == 0:
+        acc[...] = more
+    elif t < tiles - 1:
+        acc[...] += more
+    else:
+        part[rows, :] = (acc[...] + more).astype(BF16)
+
+
+def comm_kernel(tiles_of, n_saved, n_made, gathers, sums, bits, *refs):
+    refs = list(refs)
+
+    def take(n):
+        out = refs[:n]
+        del refs[:n]
+        return out
+
+    heavy = tiles_of is not None
+    own_hbm = take(1)[0] if gathers else None
+    loads_from = take(3 + n_saved) if heavy else []
+    part_in = take(1)[0] if sums else None
+    swap_from = take(len(bits))
+    all_hbm = take(1)[0] if gathers else None
+    made_hbm = take(n_made + 1) if heavy else []
+    total_hbm = take(1)[0] if sums else None
+    swap_to = take(len(bits))
+    buf = take(1)[0] if gathers else None
+    loads_to = take(3 + n_saved) if heavy else []
+    made = take(n_made + 1) if heavy else []
+    acc = take(1)[0] if heavy else None
+    total = take(1)[0] if sums else None
+    chain_bufs = take(5) if sums else None
+    line_sems = take(6) if gathers else None
+    chain_sems = take(7) if sums else None
+    out_sem = take(1)[0] if gathers else None
+    load_sem = take(1)[0] if heavy else None
+    swap_sem = take(1)[0] if bits else None
+
+    chips = lax.axis_size("shard") // 2
+    greet_neighbours(chips, sorted(set(bits)))
+    swaps = swap_copies(swap_from, swap_to, bits, swap_sem)
+    line = chain = None
+    if gathers:
+        line = Line(own_hbm, buf, line_sems[:5], chips)
+        line.start()
+        keep = pltpu.make_async_copy(own_hbm, line.place(line.z, line.core), line_sems[5])
+        keep.start()
+        pair = 2 * own_hbm.shape[0]
+    if sums:
+        chain = Chain(part_in, total, total_hbm, chain_bufs, chain_sems, chips)
+        chain.start()
+    for swap in swaps:
+        swap.start()
+    loads = [
+        pltpu.make_async_copy(src, dst, load_sem.at[n])
+        for n, (src, dst) in enumerate(zip(loads_from, loads_to))
+    ]
+    for load in loads:
+        load.start()
+    if gathers:
+        keep.wait()
+
+    def outs(chip):
+        rows = pl.ds(pl.multiple_of(chip * pair, pair), pair)
+        return [
+            pltpu.make_async_copy(src.at[rows], dst.at[rows], out_sem.at[n, chip])
+            for n, (src, dst) in enumerate(zip([buf] + made, [all_hbm] + made_hbm))
+        ]
+
+    def step(n, carry):
+        if gathers:
+            line.pass_on(n)
+        if sums and gathers:
+
+            @pl.when(n > 0)
+            def _():
+                chain.step(n - 1)
+
+        elif sums:
+            chain.step(n)
+        if gathers:
+            chip = line.chip_at(n)
+            line.wait_side(chip)
+            rows = pl.ds(pl.multiple_of(chip * pair, pair), pair)
+            if heavy:
+
+                @pl.when(n == 0)
+                def _():
+                    for load in loads:
+                        load.wait()
+
+                tiles_of(rows, buf, loads_to[:3], loads_to[3:], made[:-1], acc, made[-1])
+            for copy in outs(chip):
+                copy.start()
+        return carry
+
+    lax.fori_loop(0, chips, step, 0)
+    if sums and gathers:
+        chain.step(chips - 1)
+    if sums:
+        chain.finish()
+    if gathers:
+        line.finish()
+
+        def drain(chip, carry):
+            for copy in outs(chip):
+                copy.wait()
+            return carry
+
+        lax.fori_loop(0, chips, drain, 0)
+    for swap in swaps:
+        swap.wait()
+
+
+def comm_call(
+    number, own=None, part=None, tiles_of=None, weights=(), saved=(), n_made=0, swaps=()
+):
+    shards = lax.axis_size("shard")
+    chips = shards // 2
+    gathers, sums, heavy = own is not None, part is not None, tiles_of is not None
+    ins, outs, scratch, sems = [], [], [], []
+    width = own.shape[1] if gathers else part.shape[1]
+    flops = 0
+    moved = 0
+    if gathers:
+        rows = own.shape[0] * shards
+        wide = jax.ShapeDtypeStruct((rows, width), BF16)
+        ins.append(own)
+        outs.append(wide)
+        scratch.append(pltpu.VMEM((rows, width), BF16))
+        moved += 30 * rows * width
+    if heavy:
+        ins += list(weights) + list(saved)
+        units = weights[0].shape[0]
+        thin = jax.ShapeDtypeStruct((rows, units), BF16)
+        outs += [thin] * n_made + [wide]
+        scratch += [pltpu.VMEM(x.shape, BF16) for x in ins[1:]]
+        scratch += [pltpu.VMEM((rows, units), BF16)] * n_made
+        scratch += [pltpu.VMEM((rows, width), BF16)]
+        scratch += [pltpu.VMEM((2 * own.shape[0], width), F32)]
+        flops = 6 * rows * units * width
+    if sums:
+        ins.append(part)
+        size = part.shape[0] // shards
+        outs.append(jax.ShapeDtypeStruct((size, width), F32))
+        scratch.append(pltpu.VMEM((size, width), F32))
+        scratch += [pltpu.VMEM((chips, size, width), BF16)] * 5
+        moved += 30 * part.shape[0] * width
+    dma = pltpu.SemaphoreType.DMA
+    bits = tuple(bit for _, bit in swaps)
+    ins += [x for x, _ in swaps]
+    outs += [jax.ShapeDtypeStruct(x.shape, x.dtype) for x, _ in swaps]
+    if gathers:
+        sems += [dma((chips,))] * 5 + [dma]
+    if sums:
+        sems += [dma((chips,))] * 6 + [dma]
+    if gathers:
+        sems.append(dma((n_made + 2 if heavy else 1, chips)))
+    if heavy:
+        sems.append(dma((3 + len(saved),)))
+    if bits:
+        sems.append(dma((2, len(bits))))
+    kernel = functools.partial(comm_kernel, tiles_of, len(saved), n_made, gathers, sums, bits)
+    return pl.pallas_call(
+        kernel,
+        in_specs=[ANYWHERE] * len(ins),
+        out_specs=[ANYWHERE] * len(outs),
+        out_shape=outs,
+        scratch_shapes=scratch + sems,
+        compiler_params=pltpu.CompilerParams(
+            collective_id=number, has_side_effects=True, vmem_limit_bytes=58 * 1024 * 1024
+        ),
+        cost_estimate=pl.CostEstimate(flops=flops, bytes_accessed=moved, transcendentals=0),
+        name="comm%d" % number,
+    )(*ins)
+
+
+def over_tokens_kernel(a0, a1, b0, b1, c0, c1, x0, x1, g0, g1, out_ref):
+    i = pl.program_id(0)
+    tiles = pl.num_programs(0) // 3
+
+    def product(l0, l1, r0, r1):
+        out_ref[...] = (dot(l0[...], r0[...], TN) + dot(l1[...], r1[...], TN)).astype(BF16)
+
+    @pl.when(i < tiles)
+    def _():
+        product(a0, a1, x0, x1)
+
+    @pl.when((i >= tiles) & (i < 2 * tiles))
+    def _():
+        product(b0, b1, x0, x1)
+
+    @pl.when(i >= 2 * tiles)
+    def _():
+        product(c0, c1, g0, g1)
+
+
+def over_tokens(gates, ups, glus, xs, gs):
+    rows, units = glus[0].shape
+    width = xs[0].shape[1]
+    tiles = units // FF_TILE
+    whole = pl.BlockSpec((rows, width), lambda i: (0, 0), pipeline_mode=pl.Buffered(1))
+
+    def some(n):
+        return pl.BlockSpec((rows, FF_TILE), lambda i: (0, jnp.clip(i - n * tiles, 0, tiles - 1)))
+
+    return pl.pallas_call(
+        over_tokens_kernel,
+        grid=(3 * tiles,),
+        in_specs=[some(0), some(0), some(1), some(1), some(2), some(2)] + [whole] * 4,
+        out_specs=pl.BlockSpec((FF_TILE, width), lambda i: (i, 0)),
+        out_shape=jax.ShapeDtypeStruct((3 * units, width), BF16),
+        compiler_params=kernel_params(),
+        cost_estimate=pl.CostEstimate(
+            flops=12 * rows * units * width, bytes_accessed=16 * rows * width, transcendentals=0
+        ),
+        name="over_tokens",
+    )(*gates, *ups, *glus, *xs, *gs)
 
 
 def swap_cores(x):
@@ -497,35 +1111,95 @@
     return lax.psum_scatter(x, axis_name, scatter_dimension=axis, tiled=True)
 
 
-def partner(x, bit, after=None):
+def partner(x, bit):
     n = lax.axis_size("replica")
-    got = lax.ppermute(x, "replica", [(r, r ^ bit) for r in range(n)])
-    return got if after is None else lax.optimization_barrier((got, after))[0]
-
-
-def halve(x, axis, bit, after=None):
+    return lax.ppermute(x, "replica", [(r, r ^ bit) for r in range(n)])
+
+
+def halve_send(x, axis, bit):
     half = x.shape[axis] // 2
     mine = lax.rem(lax.axis_index("replica") // bit, 2)
     kept = lax.dynamic_slice_in_dim(x, mine * half, half, axis)
     sent = lax.dynamic_slice_in_dim(x, (1 - mine) * half, half, axis)
-    return (kept.astype(F32) + partner(sent, bit, after).astype(F32)).astype(BF16)
-
-
-def double(x, axis, bit, after=None):
-    other = partner(x, bit, after)
+    return kept, partner(sent, bit)
+
+
+def halve_sum(kept, got):
+    return (kept.astype(F32) + got.astype(F32)).astype(BF16)
+
+
+def halve(x, axis, bit):
+    return halve_sum(*halve_send(x, axis, bit))
+
+
+def join(x, other, axis, bit):
     mine = lax.rem(lax.axis_index("replica") // bit, 2) == 0
     return jnp.concatenate(
         [jnp.where(mine, x, other), jnp.where(mine, other, x)], axis=axis
     )
 
 
-def sum_replicas(x, after=(None, None, None, None)):
-    half = x.shape[0] // 2
-    parts = []
-    for piece, first, second in ((x[:half], 1, 2), (x[half:], 2, 1)):
-        piece = halve(halve(piece, 0, first, after[0]), 0, second, after[1])
-        parts.append(double(double(piece, 0, second, after[2]), 0, first, after[3]))
-    return jnp.concatenate(parts).astype(F32)
+def double(x, axis, bit):
+    return join(x, partner(x, bit), axis, bit)
+
+
+class ReplicaSum:
+    def __init__(self, x):
+        half = x.shape[0] // 2
+        self.kept = [x[:half], x[half:]]
+        self.stage = 0
+
+    def bits(self):
+        return (1, 2) if self.stage in (0, 3) else (2, 1)
+
+    def sends(self):
+        pairs = []
+        for n, bit in enumerate(self.bits()):
+            x = self.kept[n]
+            if self.stage < 2:
+                half = x.shape[0] // 2
+                mine = lax.rem(lax.axis_index("replica") // bit, 2)
+                self.kept[n] = lax.dynamic_slice_in_dim(x, mine * half, half)
+                x = lax.dynamic_slice_in_dim(x, (1 - mine) * half, half)
+            pairs.append((x, bit))
+        return pairs
+
+    def receive(self, got):
+        for n, (bit, other) in enumerate(zip(self.bits(), got)):
+            if self.stage < 2:
+                self.kept[n] = halve_sum(self.kept[n], other)
+            else:
+                self.kept[n] = join(self.kept[n], other, 0, bit)
+        self.stage += 1
+
+    def permute(self):
+        self.receive([partner(x, bit) for x, bit in self.sends()])
+
+    def result(self):
+        return jnp.concatenate(self.kept).astype(F32)
+
+    def thirds(self):
+        first, second = self.kept
+        third = (first.shape[0] + second.shape[0]) // 3
+        rest = first.shape[0] - third
+        middle = jnp.concatenate([first[third:], second[:rest]])
+        return first[:third].astype(F32), middle.astype(F32), second[rest:].astype(F32)
+
+
+def all_sends(sums):
+    return [pair for one in sums for pair in one.sends()]
+
+
+def all_receive(sums, got):
+    for n, one in enumerate(sums):
+        one.receive(got[2 * n : 2 * n + 2])
+
+
+def sum_replicas(x):
+    one = ReplicaSum(x)
+    for _ in range(4):
+        one.permute()
+    return one.result()
 
 
 def exchange(x):
@@ -599,83 +1273,72 @@
     kv_high = jnp.where(first_core, kv_other, kv_own)
     keys = jnp.concatenate([kv_low[:, :HALF], kv_high[:, :HALF]], axis=1)
     values = jnp.concatenate([kv_low[:, HALF:], kv_high[:, HALF:]], axis=1)
-    attended, lse, raw_part = attend_call(queries, keys, values, low_row, w_output)
-    raw_attn = scatter(raw_part, "shard", 0).astype(F32)
-
+    attended, lse, raw_top, raw_end = attend_call(queries, keys, values, low_row, w_output)
     x_float = tokens.astype(F32)
     grad_top = cotangent.astype(F32)
     chunks = 2
     size = tok_rows // chunks
 
-    hidden_parts, normed_groups, raw_parts = [], [], []
-    glus, gates, ups = [], [], []
-    for c in range(chunks):
-        rows = slice(c * size, (c + 1) * size)
-        hidden = x_float[rows] + rms_scaled(raw_attn[rows], gains[1])
-        hidden_parts.append(hidden)
-        normed_groups.append(gather(rms_scaled(hidden, gains[2]).astype(BF16), "shard", 0))
-    for c in range(chunks):
-        gate = jnp.einsum("td,fd->tf", normed_groups[c], w_gate, preferred_element_type=F32)
-        up = jnp.einsum("td,fd->tf", normed_groups[c], w_up, preferred_element_type=F32)
-        glu = glu_value(gate, up).astype(BF16)
-        gates.append(gate)
-        ups.append(up)
-        glus.append(glu)
-        raw_parts.append(scatter(dot(glu, w_down).astype(BF16), "shard", 0).astype(F32))
-    outs, d_groups, gain_four = [], [], []
-    for c in range(chunks):
-        rows = slice(c * size, (c + 1) * size)
-        outs.append((hidden_parts[c] + rms_scaled(raw_parts[c], gains[3])).astype(BF16))
-        _, pull = jax.vjp(rms_scaled, raw_parts[c], gains[3])
-        d_raw, g4 = pull(grad_top[rows])
-        gain_four.append(g4)
-        d_groups.append(gather(d_raw.astype(BF16), "shard", 0))
-    d_normed_parts, d_gates, d_ups = [], [], []
-    for c in range(chunks):
-        d_glu = jnp.einsum("td,fd->tf", d_groups[c], w_down, preferred_element_type=F32)
-        _, pull = jax.vjp(glu_value, gates[c], ups[c])
-        d_gate, d_up = pull(d_glu)
-        d_gate, d_up = d_gate.astype(BF16), d_up.astype(BF16)
-        d_gates.append(d_gate)
-        d_ups.append(d_up)
-        part = (dot(d_gate, w_gate) + dot(d_up, w_up)).astype(BF16)
-        d_normed_parts.append(scatter(part, "shard", 0).astype(F32))
-
-    def over_tokens(left, right):
-        total = dot(left[0], right[0], TN)
-        for c in range(1, chunks):
-            total = total + dot(left[c], right[c], TN)
-        return total.astype(BF16)
-
-    sum_down = over_tokens(glus, d_groups)
-    sum_gate = over_tokens(d_gates, normed_groups)
-    sum_up = over_tokens(d_ups, normed_groups)
-    d_normed_parts[-1] = lax.optimization_barrier(
-        (d_normed_parts[-1], sum_down, sum_gate, sum_up)
-    )[0]
-
-    d_hiddens, d_raws, gain_two, gain_three = [], [], [], []
-    for c in range(chunks):
+    weights = (w_gate, w_up, w_down)
+    (raw_first,) = comm_call(0, part=raw_top)
+
+    def enter(raw, c):
+        hidden = x_float[c * size : (c + 1) * size] + rms_scaled(raw, gains[1])
+        return hidden, rms_scaled(hidden, gains[2]).astype(BF16)
+
+    def leave(raw, hidden, c):
+        out = (hidden + rms_scaled(raw, gains[3])).astype(BF16)
+        _, pull = jax.vjp(rms_scaled, raw, gains[3])
+        d_raw, gain_term = pull(grad_top[c * size : (c + 1) * size])
+        return out, d_raw.astype(BF16), gain_term
+
+    hidden_first, low_first = enter(raw_first, 0)
+    normed_0, gate_0, up_0, glu_0, part_0, raw_second = comm_call(
+        1, low_first, raw_end, forward_tiles, weights, n_made=3
+    )
+    hidden_second, low_second = enter(raw_second, 1)
+    normed_1, gate_1, up_1, glu_1, part_1, ffn_first = comm_call(
+        1, low_second, part_0, forward_tiles, weights, n_made=3
+    )
+    out_first, d_first, g4_first = leave(ffn_first, hidden_first, 0)
+    d_all_0, d_gate_0, d_up_0, d_part_0, ffn_second = comm_call(
+        2, d_first, part_1, backward_tiles, weights, (gate_0, up_0), n_made=2
+    )
+    out_second, d_second, g4_second = leave(ffn_second, hidden_second, 1)
+    d_all_1, d_gate_1, d_up_1, d_part_1, d_normed_first = comm_call(
+        2, d_second, d_part_0, backward_tiles, weights, (gate_1, up_1), n_made=2
+    )
+    glus, d_groups = (glu_0, glu_1), (d_all_0, d_all_1)
+    d_gates, d_ups, normed_groups = (d_gate_0, d_gate_1), (d_up_0, d_up_1), (normed_0, normed_1)
+    hidden_parts, raw_parts = (hidden_first, hidden_second), (raw_first, raw_second)
+    outs, gain_four = (out_first, out_second), (g4_first, g4_second)
+
+    sums = [ReplicaSum(over_tokens(d_gates, d_ups, glus, normed_groups, d_groups))]
+
+    def back(d_normed, c):
         rows = slice(c * size, (c + 1) * size)
         _, pull = jax.vjp(rms_scaled, hidden_parts[c], gains[2])
-        part, g3 = pull(d_normed_parts[c])
+        part, g3 = pull(d_normed)
         d_hidden = grad_top[rows] + part
-        _, pull = jax.vjp(rms_scaled, raw_attn[rows], gains[1])
+        _, pull = jax.vjp(rms_scaled, raw_parts[c], gains[1])
         d_raw, g2 = pull(d_hidden)
-        gain_two.append(g2)
-        gain_three.append(g3)
-        d_hiddens.append(d_hidden)
-        d_raws.append(d_raw.astype(BF16))
-    d_hidden = jnp.concatenate(d_hiddens)
-    d_raw_low = jnp.concatenate(d_raws)
-    d_raw_group = gather(d_raw_low, "shard", 0)
-
-    dq, dk, dv, grad_out = attend_back_call(
-        queries, keys, values, low_row, lse, attended, d_raw_group, w_output, table
-    )
-    grad_down = sum_replicas(sum_down, (d_raw_low, None, None, dq))
-    grad_gate = sum_replicas(sum_gate, (d_raw_low, None, None, dq))
-    grad_up = sum_replicas(sum_up, (d_raw_low, dq, None, None))
+        return d_hidden, d_raw.astype(BF16), g2, g3
+
+    d_hidden_first, d_attn_first, g2_first, g3_first = back(d_normed_first, 0)
+    d_attn_0, d_normed_second, *got = comm_call(
+        3, d_attn_first, d_part_1, swaps=all_sends(sums)
+    )
+    all_receive(sums, got)
+    d_hidden_second, d_attn_second, g2_second, g3_second = back(d_normed_second, 1)
+    d_attn_1, *got = comm_call(4, d_attn_second, swaps=all_sends(sums))
+    all_receive(sums, got)
+    d_hidden = jnp.concatenate([d_hidden_first, d_hidden_second])
+    gain_two, gain_three = (g2_first, g2_second), (g3_first, g3_second)
+    dq, dk, dv, grad_out, *got = attend_back_call(
+        6, queries, keys, values, low_row, lse, attended, d_attn_0, d_attn_1, w_output, table,
+        all_sends(sums),
+    )
+    all_receive(sums, got)
     dkv_low = jnp.concatenate([dk[:, :HALF], dv[:, :HALF]], axis=1)
     dkv_high = jnp.concatenate([dk[:, HALF:], dv[:, HALF:]], axis=1)
     dkv_mine = jnp.where(first_core, dkv_low, dkv_high).astype(F32)
@@ -686,7 +1349,8 @@
     dk_lin = dk_half * own[:, :HALF] - turned * own[:, HALF:]
     d_lin = jnp.concatenate([dq, dk_lin.astype(BF16), dkv[:, HALF:].astype(BF16)], axis=1)
     part, d_lin = lax.optimization_barrier((dot(d_lin, head_w, NT).astype(BF16), d_lin))
-    d_normed = scatter(part, "shard", 0).astype(F32)
+    d_normed, *got = comm_call(5, part=part, swaps=all_sends(sums))
+    all_receive(sums, got)
     grad_head = dot(normed, d_lin, TN)
     gain_one = jnp.sum(grad_head * head_w.astype(F32), axis=1) / gains[0]
     _, pull = jax.vjp(rms_scaled, x_float, gains[0])
@@ -713,6 +1377,7 @@
     )
     grad_value = right[:, :, :HALF].transpose(1, 0, 2).reshape(w_rows, KV * HD)
     grad_out_proj = sum_replicas(grad_out)
+    grad_gate, grad_up, grad_down = sums[0].thirds()
     gain_shares = jnp.sum(right[:, :, HALF : HALF + gain_terms.shape[1]], axis=0).T
     return (
         jnp.concatenate(outs),

time: 1160 us -> 1070 us (0.922)
  Pallas kernels: 68.3 us -> 647 us
  waiting for transfers between devices: 594 us -> 142 us
  matrix products: 195 us -> 14.2 us
  starting transfers between devices: 49.1 us -> 21.7 us
    pallas_call x1 -> x10, Pallas kernels: 33.6 us -> 612 us  [the longest x8 519 us: comm_call(): pl.pallas_call(kernel, in_specs=[ANYWHERE] * len(ins), out_specs=[ANYWHER...]
    reduce_scatter x6 -> x0, waiting for transfers between devices: 186 us -> none  [scatter(): return lax.psum_scatter(x, axis_name, scatter_dimension=axis, tiled=True)]
    all_gather x7 -> x2, waiting for transfers between devices: 227 us -> 96.4 us  [gather(): return lax.all_gather(x, axis_name, axis=axis, tiled=True)]
    ppermute x40 -> x16, waiting for transfers between devices: 163 us -> 32.9 us  [partner(): return lax.ppermute(x, 'replica', [(r, r ^ bit) for r in range(n)])]
    dot_general x14 -> x2, matrix products: 120 us -> 14.2 us  [dot(): return lax.dot_general(a, b, dims, preferred_element_type=F32)]
    dot_general x6 -> x0, matrix products: 75.2 us -> none  [the longest x2 30.4 us: fast_on_device(): jnp.einsum('td,fd->tf', d_groups[c], w_down, preferred_element_type=F32)]
    ppermute x40 -> x16, starting transfers between devices: 42.9 us -> 16.8 us  [partner(): return lax.ppermute(x, 'replica', [(r, r ^ bit) for r in range(n)])]
    convert_element_type x29 -> x22, other arithmetic: 37.7 us -> 44.4 us  [the longest x12 15 us: halve_sum(): return (kept.astype(F32) + got.astype(F32)).astype(BF16)]
  transfers between devices with their start and end apart: 56 -> 21, of which waited for: 31 -> 13; matrix products, arithmetic and copies ran while one was open for 30% -> 8% of each run, Pallas kernels for 3% -> 10%
where the time goes in v2:
time: 1070 us
  Pallas kernels  647 us (60%)
  waiting for transfers between devices  142 us (13%)
  other arithmetic  112 us (10%)
  local copies, waits for them, and re-layouts  75.9 us (7%)
  blocking collectives  37.2 us (3%)
  starting transfers between devices  21.7 us (2%)
  between operations  15.6 us (1%)
  matrix products  14.2 us (1%)
    pallas_call x8, Pallas kernels, comm_call(): pl.pallas_call(kernel, in_specs=[ANYWHERE] * len(ins), out_specs=[ANYWHER...  519 us
    all_gather x2, waiting for transfers between devices, gather(): return lax.all_gather(x, axis_name, axis=axis, tiled=True)  96.4 us
    pallas_call x1, Pallas kernels, attend_back_call(): pl.pallas_call(functools.partial(attend_back_kernel, bits), grid=(rows //...  48.4 us
    pallas_call x1, Pallas kernels, over_tokens(): pl.pallas_call(over_tokens_kernel, grid=(3 * tiles,), in_specs=[some(0),...  44.3 us
    ppermute x16, waiting for transfers between devices, partner(): return lax.ppermute(x, 'replica', [(r, r ^ bit) for r in range(n)])  32.9 us
    unnamed x148, local copies, waits for them, and re-layouts  26 us
    all_to_all x1, blocking collectives, exchange(): return lax.all_to_all(x, 'shard', 0, 0, tiled=True)  23 us
    pallas_call x1, Pallas kernels, attend_call(): pl.pallas_call(attend_kernel, grid=(rows // BLOCK,), in_specs=[rows_spec(...  22.6 us
  transfers between devices with their start and end apart: 21, of which 13 were waited for; matrix products, arithmetic and copies ran while one was open for 8% of the time, Pallas kernels for 10%

profile of v2, /device:TPU:0, one launch (start us, length us, event | category | flops | bytes accessed | tf_op | source)
XLA Modules:
  0.0 1065.5 jit_solution(3510365544491567605)
XLA Ops:
  11.6 23.0 %all_to_all.10 = bf16[8,72,512]{2,1,0:T(8,128)(2,1)S(1)} all-to-all(bf16[8,72,512]{2,1,0:T(8,128)(2,1)S(1)} %copy.133), channel_id=1, replica_groups=mesh['replica'=4,'shard'=8] {'shard'}, dimensions={0} | all-to-all | bytes 1179648 | tf_op jit(solution)/shard_map/all_to_all | solution.py:1206
  36.5 14.2 %all-gather = bf16[8,288,4]{1,2,0:T(4,128)(2,1)S(1)} all-gather(bf16[1,288,4]{1,2,0:T(4,128)(2,1)S(1)} %maximum_bitcast_fusion.1), channel_id=1, replica_groups=mesh['replica'=4,'shard'=8] {'shard'}, dimensions={0}, use_global_device_ids=true | all-gather | bytes 20736 | tf_op jit(solution)/shard_map/all_gather | solution.py:1107
  57.3 7.7 concatenate.89.tab_ref
  65.8 6.4 all-gather.6.cloned.1.call-done
  74.6 90.0 %all-gather.4.cloned.1.call-done.x_ref = bf16[2048,2304]{1,0:T(8,128)(2,1)} async-done(((bf16[256,2304]{1,0:T(8,128)(2,1)}), bf16[2048,2304]{1,0:T(8,128)(2,1)}) %all-gather.4.cloned.1.call-update) | async-done | bytes 9437200 | tf_op jit(solution)/shard_map/all_gather | solution.py:1107
  164.6 12.1 %qkv.1 = (bf16[2048,2304]{1,0:T(8,128)(2,1)}, bf16[2048,256]{1,0:T(8,128)(2,1)S(1)}, bf16[2048,256]{1,0:T(8,128)(2,1)S(1)}) custom-call(bf16[2048,2304]{1,0:T(8,128)(2,1)} %all-gather.4.cloned.1.call-done.x_ref, f32[1,2304]{1,0:T(1,128)S(1)} %get-tuple-element.278.gain_ref, bf16[2304,512]{1,0:T(8,128)(2,1)S(1)} %bitcast.42, f32[2048,512]{1,0:T(8,128)} %concatenate.89.tab_ref), custom_call_target="tpu_custom_call" | custom-call | flops 4831838208 | bytes 18874368 | tf_op jit(solution)/shard_map/qkv/pallas_call | solution.py:448
  183.5 6.4 maximum_select_fusion
  193.5 22.6 %attend.1 = (bf16[2048,256]{1,0:T(8,128)(2,1)S(1)}, f32[1,2048]{1,0:T(1,128)S(1)}, bf16[1024,2304]{1,0:T(8,128)(2,1)}, bf16[1024,2304]{1,0:T(8,128)(2,1)}) custom-call(bf16[2048,256]{1,0:T(8,128)(2,1)S(1)} %copy-done.5, bf16[2048,256]{1,0:T(8,128)(2,1)S(1)} %pad_maximum_fusion.7.k_ref, bf16[2048,256]{1,0:T(8,128)(2,1)S(1)} %pad_maximum_fusion.8.v_ref, ...), custom_call_target="tpu_custom_call" | custom-call | flops 5637144576 | bytes 9437184 | tf_op jit(solution)/shard_map/attend/pallas_call | solution.py:469
  217.1 47.4 %comm0.1 = f32[128,2304]{1,0:T(8,128)} custom-call(bf16[1024,2304]{1,0:T(8,128)(2,1)} %get-tuple-element.62.refs_0_), custom_call_target="tpu_custom_call" | custom-call | bytes 70778880 | tf_op jit(solution)/shard_map/comm0/pallas_call | solution.py:1044
  269.1 56.8 %comm1.2 = (bf16[1024,2304]{1,0:T(8,128)(2,1)}, bf16[1024,1152]{1,0:T(8,128)(2,1)}, bf16[1024,1152]{1,0:T(8,128)(2,1)}, bf16[1024,1152]{1,0:T(8,128)(2,1)}, bf16...) custom-call(bf16[128,2304]{1,0:T(8,128)(2,1)} %multiply_convert_fusion.1.refs_0_, bf16[1152,2304]{1,0:T(8,128)(2,1)} %refs_1_.7, ...), custom_call_target="tpu_custom_call" | custom-call | flops 16307453952 | bytes 141557760 | tf_op jit(solution)/shard_map/comm1/pallas_call | solution.py:1044
  330.4 58.4 %comm1.3 = (bf16[1024,2304]{1,0:T(8,128)(2,1)}, bf16[1024,1152]{1,0:T(8,128)(2,1)}, bf16[1024,1152]{1,0:T(8,128)(2,1)}, bf16[1024,1152]{1,0:T(8,128)(2,1)}, bf16...) custom-call(bf16[128,2304]{1,0:T(8,128)(2,1)} %multiply_convert_fusion.refs_0_, bf16[1152,2304]{1,0:T(8,128)(2,1)} %refs_1_.7, ...), custom_call_target="tpu_custom_call" | custom-call | flops 16307453952 | bytes 141557760 | tf_op jit(solution)/shard_map/comm1/pallas_call | solution.py:1044
  395.5 58.6 %comm2.2 = (bf16[1024,2304]{1,0:T(8,128)(2,1)}, bf16[1024,1152]{1,0:T(8,128)(2,1)}, bf16[1024,1152]{1,0:T(8,128)(2,1)}, bf16[1024,2304]{1,0:T(8,128)(2,1)}, f32[128,2304]{1,0:T(8,128)}) custom-call(bf16[128,2304]{1,0:T(8,128)(2,1)} %get-tuple-element.249.refs_0_, bf16[1152,2304]{1,0:T(8,128)(2,1)} %refs_1_.7, bf16[1152,2304]{1,0:T(8,128)(2,1)} %refs_2_.7, ...), custom_call_target="tpu_custom_call" | custom-call | flops 16307453952 | bytes 141557760 | tf_op jit(solution)/shard_map/comm2/pallas_call | solution.py:1044
  459.5 61.3 %comm2.3 = (bf16[1024,2304]{1,0:T(8,128)(2,1)}, bf16[1024,1152]{1,0:T(8,128)(2,1)}, bf16[1024,1152]{1,0:T(8,128)(2,1)}, bf16[1024,2304]{1,0:T(8,128)(2,1)}, f32[128,2304]{1,0:T(8,128)}) custom-call(bf16[128,2304]{1,0:T(8,128)(2,1)} %get-tuple-element.246.refs_0_, bf16[1152,2304]{1,0:T(8,128)(2,1)} %refs_1_.7, bf16[1152,2304]{1,0:T(8,128)(2,1)} %refs_2_.7, ...), custom_call_target="tpu_custom_call" | custom-call | flops 16307453952 | bytes 141557760 | tf_op jit(solution)/shard_map/comm2/pallas_call | solution.py:1044
  524.1 44.3 %over_tokens.1 = bf16[3456,2304]{1,0:T(8,128)(2,1)} custom-call(bf16[1024,1152]{1,0:T(8,128)(2,1)S(1)} %copy-done.7, bf16[1024,1152]{1,0:T(8,128)(2,1)S(1)} %copy-done.8, bf16[1024,1152]{1,0:T(8,128)(2,1)} %get-tuple-element.78.b0, bf16[1024,1152]{1,0:T(8,128)(2,1)} %get-tuple-element.79.b1, bf16[1024,1152]{1,0:T(8,128)(2,1)} %get-tuple-element.80.c0, ...), custom_call_target="tpu_custom_call" | custom-call | flops 32614907904 | bytes 37748736 | tf_op jit(solution)/shard_map/over_tokens/pallas_call | solution.py:1087
  568.5 7.0 fusion.23
  586.0 89.0 %comm3.1 = (bf16[1024,2304]{1,0:T(8,128)(2,1)}, f32[128,2304]{1,0:T(8,128)}, bf16[864,2304]{1,0:T(8,128)(2,1)}, bf16[864,2304]{1,0:T(8,128)(2,1)}) custom-call(bf16[128,2304]{1,0:T(8,128)(2,1)} %fusion.6.refs_0_, bf16[1024,2304]{1,0:T(8,128)(2,1)} %get-tuple-element.75.refs_1_, bf16[864,2304]{1,0:T(8,128)(2,1)} %constant_dynamic-slice_fusion.10.refs_2_, ...), custom_call_target="tpu_custom_call" | custom-call | bytes 141557760 | tf_op jit(solution)/shard_map/comm3/pallas_call | solution.py:1044
  679.7 3.8 add_convert_fusion
  683.7 4.6 add_convert_fusion.1
  692.5 46.0 %comm4.1 = (bf16[1024,2304]{1,0:T(8,128)(2,1)}, bf16[432,2304]{1,0:T(8,128)(2,1)}, bf16[432,2304]{1,0:T(8,128)(2,1)}) custom-call(bf16[128,2304]{1,0:T(8,128)(2,1)} %fusion.8.refs_0_, bf16[432,2304]{1,0:T(8,128)(2,1)} %constant_dynamic-slice_fusion.8.refs_1_, bf16[432,2304]{1,0:T(8,128)(2,1)} %constant_dynamic-slice_fusion.7.refs_2_), custom_call_target="tpu_custom_call" | custom-call | bytes 70778880 | tf_op jit(solution)/shard_map/comm4/pallas_call | solution.py:1044
  738.5 4.0 add_convert_fusion.2.swap_b
  744.6 48.4 %attend_back.1 = (bf16[2048,256]{1,0:T(8,128)(2,1)S(1)}, bf16[2048,256]{1,0:T(8,128)(2,1)S(1)}, bf16[2048,256]{1,0:T(8,128)(2,1)S(1)}, bf16[256,2304]{1,0:T(8,12...) custom-call(bf16[2048,256]{1,0:T(8,128)(2,1)S(1)} %copy-done.5, ...), custom_call_target="tpu_custom_call" | custom-call | flops 11274289152 | bytes 9437184 | tf_op jit(solution)/shard_map/attend_back/pallas_call | solution.py:498
  831.9 7.5 convolution_convert_fusion.refs_0_
  839.4 6.7 fusion.24
  853.6 101.4 %comm5.1 = (f32[256,2304]{1,0:T(8,128)}, bf16[864,2304]{1,0:T(8,128)(2,1)}, bf16[864,2304]{1,0:T(8,128)(2,1)}) custom-call(bf16[2048,2304]{1,0:T(8,128)(2,1)} %convolution_convert_fusion.refs_0_, bf16[864,2304]{1,0:T(8,128)(2,1)} %pad_maximum_fusion.2.refs_1_, bf16[864,2304]{1,0:T(8,128)(2,1)} %pad_maximum_fusion.3.refs_2_), custom_call_target="tpu_custom_call" | custom-call | bytes 141557760 | tf_op jit(solution)/shard_map/comm5/pallas_call | solution.py:1044
  958.2 4.9 fusion
  969.2 4.9 fusion.1
  978.6 4.5 all-to-all-start.1
  983.1 7.6 maximum_convert_fusion
  990.8 12.3 %all-to-all-done.1 = bf16[8,72,640]{2,1,0:T(8,128)(2,1)} async-done(((bf16[8,72,640]{2,1,0:T(8,128)(2,1)}), bf16[8,72,640]{2,1,0:T(8,128)(2,1)}, u32[]{:S(2)}, u32[]{:S(2)}) %all-to-all-start.1) | async-done | bytes 737312 | tf_op jit(solution)/shard_map/all_to_all | solution.py:1206
  1008.7 4.0 collective-permute-done.8
  1025.7 6.4 collective-permute-done.9
  1036.0 7.8 collective-permute-done.7
  (331 shorter events, 169.7 us)
Async XLA Ops:
  7.2 65.0 %all-gather.6.cloned.1.call-start = ((), (), s32[]{:S(2)}) async-start(), calls=%async_computation.3 | async-start | bytes 2949120 | tf_op jit(solution)/shard_map/all_gather | solution.py:1107
  11.5 24.8 %copy-start.62 = (bf16[288]{0:T(512)(128)(2,1)S(1)}, bf16[288]{0:T(512)(128)(2,1)}, u32[]{:S(2)}) copy-start(bf16[288]{0:T(512)(128)(2,1)} %param.19) | copy-start | bytes 1732
  11.5 24.9 %copy-start.63 = (bf16[288]{0:T(512)(128)(2,1)S(1)}, bf16[288]{0:T(512)(128)(2,1)}, u32[]{:S(2)}) copy-start(bf16[288]{0:T(512)(128)(2,1)} %param.20) | copy-start | bytes 1732
  11.5 24.9 %copy-start.64 = (bf16[288]{0:T(512)(128)(2,1)S(1)}, bf16[288]{0:T(512)(128)(2,1)}, u32[]{:S(2)}) copy-start(bf16[288]{0:T(512)(128)(2,1)} %param.21) | copy-start | bytes 1732
  11.5 24.9 %copy-start.65 = (bf16[288]{0:T(512)(128)(2,1)S(1)}, bf16[288]{0:T(512)(128)(2,1)}, u32[]{:S(2)}) copy-start(bf16[288]{0:T(512)(128)(2,1)} %param.22) | copy-start | bytes 1732
  11.6 39.2 %copy-start.61 = (s32[1,1024]{1,0:T(1,128)S(1)}, s32[1,1024]{1,0:T(1,128)}, u32[]{:S(2)}) copy-start(s32[1,1024]{1,0:T(1,128)} %param.26) | copy-start | bytes 12292
  35.6 128.9 %all-gather.4.cloned.1.call-start = ((), (), s32[]{:S(2)}) async-start(), calls=%async_computation.2 | async-start | bytes 10616832 | tf_op jit(solution)/shard_map/all_gather | solution.py:1107
  177.6 12.3 %collective-permute-start = (bf16[2048,256]{1,0:T(8,128)(2,1)S(1)}, bf16[2048,256]{1,0:T(8,128)(2,1)}, u32[]{:S(2)}, u32[]{:S(2)}) collective-permute-start(bf16[2048,256]{1,0:T(8,128)(2,1)S(1)} %get-tuple-element.61), channel_id=1, source_target_pairs={{0,1},{1,0},{2,3},{3,2},{4,5},{5,4},{6,7},{7,6},{8,9},{9,8},{10,11... | collective-permute-start | bytes 3145736 | tf_op jit(solution)/shard_map/ppermute | solution.py:1103
  191.6 24.4 %copy-start.2 = (bf16[2048,256]{1,0:T(8,128)(2,1)}, bf16[2048,256]{1,0:T(8,128)(2,1)S(1)}, u32[]{:S(2)}) copy-start(bf16[2048,256]{1,0:T(8,128)(2,1)S(1)} %pad_maximum_fusion.8.v_ref) | copy-start | bytes 3145732
  267.9 58.0 %copy-start.16 = (f32[128,2304]{1,0:T(8,128)}, f32[128,2304]{1,0:T(8,128)S(1)}, u32[]{:S(2)}) copy-start(f32[128,2304]{1,0:T(8,128)S(1)} %get-tuple-element.225) | copy-start | bytes 3538948
  793.5 35.6 %collective-permute-start.1 = (bf16[2048,256]{1,0:T(8,128)(2,1)S(1)}, bf16[2048,256]{1,0:T(8,128)(2,1)S(1)}, u32[]{:S(2)}, u32[]{:S(2)}) collective-permute-start(bf16[2048,256]{1,0:T(8,128)(2,1)S(1)} %broadcast_select_fusion.10), channel_id=1, source_target_pairs={{0,1},{1,0},{2,3},{3,2},{4,5},{5,4},{6,7},{7,6},{8,9},{9,8},{10,11... | collective-permute-start | bytes 3145736 | tf_op jit(solution)/shard_map/ppermute | solution.py:1103
  794.6 12.6 %collective-permute-start.14 = (bf16[64,2304]{1,0:T(8,128)(2,1)S(1)}, bf16[64,2304]{1,0:T(8,128)(2,1)S(1)}, u32[]{:S(2)}, u32[]{:S(2)}) collective-permute-start(bf16[64,2304]{1,0:T(8,128)(2,1)S(1)} %constant_dynamic-slice_fusion.1), channel_id=1, source_target_pairs={{0,16},{8,24},{16,0},{24,8},{1,17},{9,25},{17,1},{25,9},{2,18},{10... | collective-permute-start | bytes 884744 | tf_op jit(solution)/shard_map/ppermute | solution.py:1116
  795.8 12.6 %collective-permute-start.10 = (bf16[64,2304]{1,0:T(8,128)(2,1)S(1)}, bf16[64,2304]{1,0:T(8,128)(2,1)S(1)}, u32[]{:S(2)}, u32[]{:S(2)}) collective-permute-start(bf16[64,2304]{1,0:T(8,128)(2,1)S(1)} %constant_dynamic-slice_fusion.3), channel_id=1, source_target_pairs={{0,8},{8,0},{16,24},{24,16},{1,9},{9,1},{17,25},{25,17},{2,10},{10... | collective-permute-start | bytes 884744 | tf_op jit(solution)/shard_map/ppermute | solution.py:1116
  807.3 5.2 collective-permute-start.15
  808.6 5.2 collective-permute-start.11
  812.5 5.2 collective-permute-start.16
  813.8 6.8 collective-permute-start.12
  817.8 7.4 collective-permute-start.17
  820.7 6.8 collective-permute-start.13
  850.5 115.9 %collective-permute-start.4 = (bf16[8,144,256]{2,1,0:T(8,128)(2,1)}, bf16[8,144,256]{2,1,0:T(8,128)(2,1)S(1)}, u32[]{:S(2)}, u32[]{:S(2)}) collective-permute-start(bf16[8,144,256]{2,1,0:T(8,128)(2,1)} %fusion.11), channel_id=1, source_target_pairs={{0,16},{8,24},{16,0},{24,8},{1,17},{9,25},{17,1},{25,9},{2,18},{10... | collective-permute-start | bytes 1769480 | tf_op jit(solution)/shard_map/ppermute | solution.py:1116
  852.4 102.7 %copy-start.26 = (bf16[432,2304]{1,0:T(8,128)(2,1)S(1)}, bf16[432,2304]{1,0:T(8,128)(2,1)}, u32[]{:S(2)}) copy-start(bf16[432,2304]{1,0:T(8,128)(2,1)} %copy-done.25) | copy-start | bytes 5971972
  852.4 102.7 %copy-start.28 = (bf16[432,2304]{1,0:T(8,128)(2,1)S(1)}, bf16[432,2304]{1,0:T(8,128)(2,1)}, u32[]{:S(2)}) copy-start(bf16[432,2304]{1,0:T(8,128)(2,1)} %copy-done.27) | copy-start | bytes 5971972
  852.4 115.3 %collective-permute-start.2 = (bf16[8,144,384]{2,1,0:T(8,128)(2,1)}, bf16[8,144,384]{2,1,0:T(8,128)(2,1)S(1)}, u32[]{:S(2)}, u32[]{:S(2)}) collective-permute-start(bf16[8,144,384]{2,1,0:T(8,128)(2,1)} %constant_dynamic-slice_fusion.6), channel_id=1, source_target_pairs={{0,8},{8,0},{16,24},{24,16},{1,9},{9,1},{17,25},{25,17},{2,10},{10... | collective-permute-start | bytes 2654216 | tf_op jit(solution)/shard_map/ppermute | solution.py:1116
  966.7 10.8 %collective-permute-start.5 = (bf16[8,72,256]{2,1,0:T(8,128)(2,1)S(1)}, bf16[8,72,256]{2,1,0:T(8,128)(2,1)S(1)}, u32[]{:S(2)}, u32[]{:S(2)}) collective-permute-start(bf16[8,72,256]{2,1,0:T(8,128)(2,1)S(1)} %constant_dynamic-slice_fusion.4), channel_id=1, source_target_pairs={{0,8},{8,0},{16,24},{24,16},{1,9},{9,1},{17,25},{25,17},{2,10},{10... | collective-permute-start | bytes 884744 | tf_op jit(solution)/shard_map/ppermute | solution.py:1116
  968.2 9.4 collective-permute-start.3
  978.6 24.4 %all-to-all-start.1 = ((bf16[8,72,640]{2,1,0:T(8,128)(2,1)}), bf16[8,72,640]{2,1,0:T(8,128)(2,1)}, u32[]{:S(2)}, u32[]{:S(2)}) async-start(bf16[8,72,640]{2,1,0:T(8,128)(2,1)} %pad_maximum_fusion.11), calls=%async_computation.1 | async-start | bytes 1474560 | tf_op jit(solution)/shard_map/all_to_all | solution.py:1206
  983.1 22.0 %copy-start.19 = (bf16[256,2304]{1,0:T(8,128)(2,1)S(1)}, bf16[256,2304]{1,0:T(8,128)(2,1)}, u32[]{:S(2)}) copy-start(bf16[256,2304]{1,0:T(8,128)(2,1)} %param.14) | copy-start | bytes 3538948
  983.1 22.0 %copy-start.42 = (f32[256,2304]{1,0:T(8,128)S(1)}, f32[256,2304]{1,0:T(8,128)}, u32[]{:S(2)}) copy-start(f32[256,2304]{1,0:T(8,128)} %get-tuple-element.101) | copy-start | bytes 7077892
  1004.0 8.6 collective-permute-start.8
  1007.7 13.4 %collective-permute-start.6 = (bf16[8,72,384]{2,1,0:T(8,128)(2,1)}, bf16[8,72,384]{2,1,0:T(8,128)(2,1)}, u32[]{:S(2)}, u32[]{:S(2)}) collective-permute-start(bf16[8,72,384]{2,1,0:T(8,128)(2,1)} %slice.234), channel_id=1, source_target_pairs={{0,16},{8,24},{16,0},{24,8},{1,17},{9,25},{17,1},{25,9},{2,18},{10... | collective-permute-start | bytes 1327112 | tf_op jit(solution)/shard_map/ppermute | solution.py:1116
  1015.2 16.9 %collective-permute-start.9 = (bf16[8,144,256]{2,1,0:T(8,128)(2,1)}, bf16[8,144,256]{2,1,0:T(8,128)(2,1)}, u32[]{:S(2)}, u32[]{:S(2)}) collective-permute-start(bf16[8,144,256]{2,1,0:T(8,128)(2,1)} %pad_maximum_fusion.12), channel_id=1, source_target_pairs={{0,16},{8,24},{16,0},{24,8},{1,17},{9,25},{17,1},{25,9},{2,18},{10... | collective-permute-start | bytes 1769480 | tf_op jit(solution)/shard_map/ppermute | solution.py:1116
  1024.8 19.0 %collective-permute-start.7 = (bf16[8,144,384]{2,1,0:T(8,128)(2,1)}, bf16[8,144,384]{2,1,0:T(8,128)(2,1)}, u32[]{:S(2)}, u32[]{:S(2)}) collective-permute-start(bf16[8,144,384]{2,1,0:T(8,128)(2,1)} %copy.141), channel_id=1, source_target_pairs={{0,8},{8,0},{16,24},{24,16},{1,9},{9,1},{17,25},{25,17},{2,10},{10... | collective-permute-start | bytes 2654216 | tf_op jit(solution)/shard_map/ppermute | solution.py:1116
  (61 other events, 296.7 us)
Sparse Core Ops, SparseCore 0:
  35.7 36.3 all-gather.5
  73.8 90.7 all-gather.3

commit v3 on v2

--- a/solution.py
+++ b/solution.py
@@ -350,27 +350,13 @@
 
 
 def attend_back_kernel(
-    bits,
     q_ref, k_ref, v_ref, low_ref, lse_ref, att_ref, top_ref, end_ref, wo_ref, tab_ref,
-    swap_a, swap_b,
-    dq_ref, dk_ref, dv_ref, go_ref, got_a, got_b, dk_acc, dv_acc, go_acc, swap_sem,
+    dq_ref, dk_ref, dv_ref, go_ref, dk_acc, dv_acc, go_acc,
 ):
     i = pl.program_id(0)
-    swaps = swap_copies((swap_a, swap_b), (got_a, got_b), bits, swap_sem)
 
     @pl.when(i == 0)
     def _():
-        barrier = pltpu.get_barrier_semaphore()
-        for bit in bits:
-            pl.semaphore_signal(
-                barrier,
-                inc=1,
-                device_id={"replica": flipped(bit)},
-                device_id_type=pl.DeviceIdType.MESH,
-            )
-        pl.semaphore_wait(barrier, len(bits))
-        for swap in swaps:
-            swap.start()
         dk_acc[...] = jnp.zeros_like(dk_acc)
         dv_acc[...] = jnp.zeros_like(dv_acc)
         go_acc[...] = jnp.zeros_like(go_acc)
@@ -413,8 +399,6 @@
         dk_ref[...] = dk_acc[...].astype(BF16)
         dv_ref[...] = dv_acc[...].astype(BF16)
         go_ref[...] = go_acc[...].astype(BF16)
-        for swap in swaps:
-            swap.wait()
 
 
 ANYWHERE = pl.BlockSpec(memory_space=pl.ANY)
@@ -490,49 +474,39 @@
     )(q, k, v, low_row, wo)
 
 
-def attend_back_call(number, q, k, v, low_row, lse, att, top, end, wo, table, swaps):
+def attend_back_call(q, k, v, low_row, lse, att, top, end, wo, table):
     rows = q.shape[0]
     width = wo.shape[1]
-    bits = tuple(bit for _, bit in swaps)
-    sent = [x for x, _ in swaps]
     return pl.pallas_call(
-        functools.partial(attend_back_kernel, bits),
+        attend_back_kernel,
         grid=(rows // BLOCK,),
         in_specs=[
             rows_spec(HD), whole_spec(rows, HD), whole_spec(rows, HD), lane_spec(), lane_spec(),
             rows_spec(HD), half_spec(width), half_spec(width), whole_spec(HD, width),
-            rows_spec(4 * HALF), ANYWHERE, ANYWHERE,
+            rows_spec(4 * HALF),
         ],
         out_specs=[
             rows_spec(HD), whole_spec(rows, HD), whole_spec(rows, HD), whole_spec(HD, width),
-            ANYWHERE, ANYWHERE,
         ],
         out_shape=[
             jax.ShapeDtypeStruct((rows, HD), BF16),
             jax.ShapeDtypeStruct((rows, HD), BF16),
             jax.ShapeDtypeStruct((rows, HD), BF16),
             jax.ShapeDtypeStruct((HD, width), BF16),
-        ]
-        + [jax.ShapeDtypeStruct(x.shape, x.dtype) for x in sent],
+        ],
         scratch_shapes=[
             pltpu.VMEM((rows, HD), F32),
             pltpu.VMEM((rows, HD), F32),
             pltpu.VMEM((HD, width), F32),
-            pltpu.SemaphoreType.DMA((2, len(bits))),
         ],
-        compiler_params=pltpu.CompilerParams(
-            dimension_semantics=("arbitrary",),
-            vmem_limit_bytes=48 * 1024 * 1024,
-            collective_id=number,
-            has_side_effects=True,
-        ),
+        compiler_params=kernel_params(),
         cost_estimate=pl.CostEstimate(
             flops=6 * rows * rows * HD + 4 * rows * width * HD,
             bytes_accessed=2 * rows * width,
             transcendentals=rows * rows,
         ),
         name="attend_back",
-    )(q, k, v, low_row, lse, att, top, end, wo, table, *sent)
+    )(q, k, v, low_row, lse, att, top, end, wo, table)
 
 
 def gelu_parts(v):
@@ -1055,6 +1029,374 @@
     )(*ins)
 
 
+class Stream:
+    def __init__(self, src, final, axis, bits, bufs, sems, dealt=None):
+        self.src, self.final, self.axis, self.bits = src, final, axis, bits
+        self.kept, self.first, self.half_sum, self.second, self.quarter_sum = bufs
+        self.send, self.got, self.local = sems
+        self.dealt = self.quarter_sum if dealt is None else dealt
+        r = lax.axis_index("replica")
+        self.b1, self.b2 = (lax.rem(r // bit, 2) for bit in bits)
+        self.half = src.shape[axis] // 2
+        self.quarter = self.half // 2
+
+    def cut(self, ref, start, size):
+        return ref.at[(slice(None),) * self.axis + (pl.ds(start, size),)]
+
+    def copy(self, n, src, dst, bit):
+        return pltpu.make_async_remote_copy(
+            src_ref=src,
+            dst_ref=dst,
+            send_sem=self.send.at[n],
+            recv_sem=self.got.at[n],
+            device_id={"replica": flipped(bit)},
+            device_id_type=pl.DeviceIdType.MESH,
+        )
+
+    def exchange(self, n):
+        half, quarter = self.half, self.quarter
+        own = self.b1 * half + self.b2 * quarter
+        if n == 0:
+            return self.copy(0, self.cut(self.src, (1 - self.b1) * half, half), self.first, self.bits[0])
+        if n == 1:
+            part = self.cut(self.half_sum, (1 - self.b2) * quarter, quarter)
+            return self.copy(1, part, self.second, self.bits[1])
+        if n == 2:
+            return self.copy(2, self.dealt, self.cut(self.final, own, quarter), self.bits[1])
+        part = self.cut(self.final, self.b1 * half, half)
+        return self.copy(3, part, part, self.bits[0])
+
+    def arrived(self, n):
+        if n < 2:
+            return self.exchange(n)
+        other = 1 - self.b2 if n == 2 else self.b2
+        if n == 2:
+            place = self.cut(self.final, self.b1 * self.half + other * self.quarter, self.quarter)
+            return self.copy(2, self.dealt, place, self.bits[1])
+        place = self.cut(self.final, (1 - self.b1) * self.half, self.half)
+        return self.copy(3, place, place, self.bits[0])
+
+    def load(self):
+        return pltpu.make_async_copy(
+            self.cut(self.src, self.b1 * self.half, self.half), self.kept, self.local.at[0]
+        )
+
+    def settle(self):
+        own = self.b1 * self.half + self.b2 * self.quarter
+        return pltpu.make_async_copy(
+            self.dealt, self.cut(self.final, own, self.quarter), self.local.at[1]
+        )
+
+    def start(self):
+        self.exchange(0).start()
+        self.load().start()
+
+    def add_first(self):
+        self.load().wait()
+        self.exchange(0).wait_recv()
+        add_into(self.half_sum, self.kept, self.first)
+        self.exchange(1).start()
+
+    def add_second(self):
+        self.exchange(1).wait_recv()
+        add_into(
+            self.quarter_sum, self.cut(self.half_sum, self.b2 * self.quarter, self.quarter), self.second
+        )
+
+    def give_back(self):
+        self.exchange(2).start()
+        self.settle().start()
+
+    def give_half(self):
+        self.settle().wait()
+        self.arrived(2).wait_recv()
+        self.exchange(3).start()
+
+    def finish(self):
+        self.arrived(3).wait_recv()
+        for n in range(4):
+            self.exchange(n).wait_send()
+
+
+def add_into(dst, a, b):
+    size = 1 if len(dst.shape) == 4 else 32
+
+    def some(n, carry):
+        rows = pl.ds(pl.multiple_of(n * size, size), size)
+        dst[rows] = (a[rows].astype(F32) + b[rows].astype(F32)).astype(BF16)
+        return carry
+
+    lax.fori_loop(0, dst.shape[0] // size, some, 0)
+
+
+def tail_kernel(
+    part_in, head_a, head_b, out_a, out_b,
+    total_hbm, final_a, final_b, final_c, final_d,
+    *refs,
+):
+    refs = list(refs)
+
+    def take(n):
+        out = refs[:n]
+        del refs[:n]
+        return out
+
+    (total,) = take(1)
+    chain_bufs = take(5)
+    stream_bufs = [take(5) for _ in range(4)]
+    dealt = take(2)
+    chain_sems = take(7)
+    stream_sems = [take(3) for _ in range(4)]
+    deal_send, deal_got, deal_local = take(3)
+    shards = lax.axis_size("shard")
+    chips = shards // 2
+    me = lax.axis_index("shard")
+    barrier = pltpu.get_barrier_semaphore()
+    peers = [lax.rem(me + n, shards) for n in range(1, shards)]
+    for peer in peers:
+        pl.semaphore_signal(
+            barrier, inc=1, device_id={"shard": peer}, device_id_type=pl.DeviceIdType.MESH
+        )
+    for bit in (1, 2):
+        pl.semaphore_signal(
+            barrier,
+            inc=1,
+            device_id={"replica": flipped(bit)},
+            device_id_type=pl.DeviceIdType.MESH,
+        )
+    pl.semaphore_wait(barrier, shards - 1 + 2)
+    streams = [
+        Stream(src, final, axis, bits, bufs, sems, target)
+        for src, final, axis, bits, bufs, sems, target in zip(
+            (head_a, head_b, out_a, out_b),
+            (final_a, final_b, final_c, final_d),
+            (1, 1, 0, 0),
+            ((1, 2), (2, 1), (2, 1), (1, 2)),
+            stream_bufs,
+            stream_sems,
+            (dealt[0], dealt[1], None, None),
+        )
+    ]
+    for stream in streams:
+        stream.start()
+    chain = Chain(part_in, total, total_hbm, chain_bufs, chain_sems, chips)
+    chain.start()
+
+    def deal(k, peer, src, n):
+        return pltpu.make_async_remote_copy(
+            src_ref=streams[k].quarter_sum.at[peer],
+            dst_ref=dealt[k].at[src],
+            send_sem=deal_send.at[k, n],
+            recv_sem=deal_got.at[k, src],
+            device_id={"shard": peer},
+            device_id_type=pl.DeviceIdType.MESH,
+        )
+
+    def own_deal(k):
+        return pltpu.make_async_copy(
+            streams[k].quarter_sum.at[me], dealt[k].at[me], deal_local.at[k]
+        )
+
+    chain.step(0)
+    for stream in streams:
+        stream.add_first()
+    chain.step(1)
+    for stream in streams:
+        stream.add_second()
+    for k in range(2):
+        for n, peer in enumerate(peers):
+            deal(k, peer, me, n).start()
+        own_deal(k).start()
+    for stream in streams[2:]:
+        stream.give_back()
+    chain.step(2)
+    for k in range(2):
+        own_deal(k).wait()
+        for n, peer in enumerate(peers):
+            deal(k, me, peer, n).wait_recv()
+        streams[k].give_back()
+    for stream in streams[2:]:
+        stream.give_half()
+    for stream in streams[:2]:
+        stream.give_half()
+    chain.step(3)
+    chain.finish()
+    for stream in streams:
+        stream.finish()
+    for k in range(2):
+        for n, peer in enumerate(peers):
+            deal(k, peer, me, n).wait_send()
+
+
+def tail_call(number, part, head_a, head_b, out_a, out_b):
+    shards = lax.axis_size("shard")
+    chips = shards // 2
+    width = part.shape[1]
+    size = part.shape[0] // shards
+    dma = pltpu.SemaphoreType.DMA
+    streams = (head_a, head_b, out_a, out_b)
+    scratch = [pltpu.VMEM((size, width), F32)] + [pltpu.VMEM((chips, size, width), BF16)] * 5
+
+    def scaled(x, axis, by):
+        shape = list(x.shape)
+        shape[axis] //= by
+        return pltpu.VMEM(tuple(shape), BF16)
+
+    for x, axis in zip(streams, (1, 1, 0, 0)):
+        scratch += [scaled(x, axis, 2)] * 3 + [scaled(x, axis, 4)] * 2
+    scratch += [scaled(head_a, 1, 4), scaled(head_b, 1, 4)]
+    sems = [dma((chips,))] * 6 + [dma]
+    for _ in streams:
+        sems += [dma((4,)), dma((4,)), dma((2,))]
+    sems += [dma((2, shards - 1)), dma((2, shards)), dma((2,))]
+    return pl.pallas_call(
+        tail_kernel,
+        in_specs=[ANYWHERE] * 5,
+        out_specs=[ANYWHERE] * 5,
+        out_shape=[jax.ShapeDtypeStruct((size, width), F32)]
+        + [jax.ShapeDtypeStruct(x.shape, BF16) for x in streams],
+        scratch_shapes=scratch + sems,
+        compiler_params=pltpu.CompilerParams(
+            collective_id=number, has_side_effects=True, vmem_limit_bytes=56 * 1024 * 1024
+        ),
+        cost_estimate=pl.CostEstimate(
+            flops=0, bytes_accessed=30 * part.shape[0] * width, transcendentals=0
+        ),
+        name="tail",
+    )(part, *streams)
+
+
+ROW_TILE = 8
+
+
+def head_kernel(
+    own_hbm, sent_hbm, all_hbm, weights_hbm, gains_hbm, buf, got,
+    right, left, side, got_line, got_side, keep_sem,
+    deal_send, deal_got, spread_send, spread_got, out_sem, local,
+):
+    shards = lax.axis_size("shard")
+    replicas = lax.axis_size("replica")
+    chips = shards // 2
+    me, r = lax.axis_index("shard"), lax.axis_index("replica")
+    tiles = got.shape[1] - 1
+    barrier = pltpu.get_barrier_semaphore()
+    shard_peers = [lax.rem(me + n, shards) for n in range(1, shards)]
+    replica_peers = [lax.rem(r + n, replicas) for n in range(1, replicas)]
+    for peer in shard_peers:
+        pl.semaphore_signal(
+            barrier, inc=1, device_id={"shard": peer}, device_id_type=pl.DeviceIdType.MESH
+        )
+    for peer in replica_peers:
+        pl.semaphore_signal(
+            barrier, inc=1, device_id={"replica": peer}, device_id_type=pl.DeviceIdType.MESH
+        )
+    pl.semaphore_wait(barrier, shards + replicas - 2)
+
+    def deal(peer, src, n):
+        return pltpu.make_async_remote_copy(
+            src_ref=sent_hbm.at[peer],
+            dst_ref=got.at[src],
+            send_sem=deal_send.at[n],
+            recv_sem=deal_got.at[src],
+            device_id={"shard": peer},
+            device_id_type=pl.DeviceIdType.MESH,
+        )
+
+    for n, peer in enumerate(shard_peers):
+        deal(peer, me, n).start()
+    mine = pltpu.make_async_copy(sent_hbm.at[me], got.at[me], local.at[0])
+    mine.start()
+    line = Line(own_hbm, buf, (right, left, side, got_line, got_side), chips)
+    line.start()
+    keep = pltpu.make_async_copy(own_hbm, line.place(line.z, line.core), keep_sem)
+    keep.start()
+    mine.wait()
+    for n, peer in enumerate(shard_peers):
+        deal(me, peer, n).wait_recv()
+
+    def spread(peer, src, n):
+        return pltpu.make_async_remote_copy(
+            src_ref=got.at[:, pl.ds(0, tiles)],
+            dst_ref=weights_hbm.at[:, pl.ds(src * tiles, tiles)],
+            send_sem=spread_send.at[n],
+            recv_sem=spread_got.at[src],
+            device_id={"replica": peer},
+            device_id_type=pl.DeviceIdType.MESH,
+        )
+
+    for n, peer in enumerate(replica_peers):
+        spread(peer, r, n).start()
+    own_part = pltpu.make_async_copy(
+        got.at[:, pl.ds(0, tiles)], weights_hbm.at[:, pl.ds(r * tiles, tiles)], local.at[1]
+    )
+    own_part.start()
+    gain_part = pltpu.make_async_copy(got.at[:, tiles], gains_hbm, local.at[2])
+    gain_part.start()
+    keep.wait()
+    pair = 2 * own_hbm.shape[0]
+
+    def out(chip):
+        rows = pl.ds(pl.multiple_of(chip * pair, pair), pair)
+        return pltpu.make_async_copy(buf.at[rows], all_hbm.at[rows], out_sem.at[chip])
+
+    def step(n, carry):
+        line.pass_on(n)
+        chip = line.chip_at(n)
+        line.wait_side(chip)
+        out(chip).start()
+        return carry
+
+    lax.fori_loop(0, chips, step, 0)
+    line.finish()
+    for n, peer in enumerate(shard_peers):
+        deal(peer, me, n).wait_send()
+    for n, peer in enumerate(replica_peers):
+        spread(peer, r, n).wait_send()
+        spread(r, peer, n).wait_recv()
+    own_part.wait()
+    gain_part.wait()
+
+    def drain(chip, carry):
+        out(chip).wait()
+        return carry
+
+    lax.fori_loop(0, chips, drain, 0)
+
+
+def head_call(number, own, sent):
+    shards = lax.axis_size("shard")
+    replicas = lax.axis_size("replica")
+    chips = shards // 2
+    size, width = own.shape
+    tiles, cols = sent.shape[1] - 1, sent.shape[3]
+    dma = pltpu.SemaphoreType.DMA
+    return pl.pallas_call(
+        head_kernel,
+        in_specs=[ANYWHERE] * 2,
+        out_specs=[ANYWHERE] * 3,
+        out_shape=[
+            jax.ShapeDtypeStruct((size * shards, width), BF16),
+            jax.ShapeDtypeStruct((shards, tiles * replicas, ROW_TILE, cols), BF16),
+            jax.ShapeDtypeStruct((shards, ROW_TILE, cols), BF16),
+        ],
+        scratch_shapes=[
+            pltpu.VMEM((size * shards, width), BF16),
+            pltpu.VMEM(sent.shape, BF16),
+        ]
+        + [dma((chips,))] * 5
+        + [dma]
+        + [dma((shards - 1,)), dma((shards,)), dma((replicas - 1,)), dma((replicas,))]
+        + [dma((chips,)), dma((3,))],
+        compiler_params=pltpu.CompilerParams(
+            collective_id=number, has_side_effects=True, vmem_limit_bytes=32 * 1024 * 1024
+        ),
+        cost_estimate=pl.CostEstimate(
+            flops=0, bytes_accessed=100 * size * shards * width, transcendentals=0
+        ),
+        name="head",
+    )(own, sent)
+
+
 def over_tokens_kernel(a0, a1, b0, b1, c0, c1, x0, x1, g0, g1, out_ref):
     i = pl.program_id(0)
     tiles = pl.num_programs(0) // 3
@@ -1231,10 +1573,6 @@
     first_core = lax.rem(shard_index, 2) == 0
     piece = w_rows // replicas
 
-    x_group = gather(tokens, "shard", 0)
-    gain_stack = jnp.stack([gain_attn_in, gain_attn_out, gain_ffn_in, gain_ffn_out])
-    gains = gather(gain_stack, "shard", 1).astype(F32)
-
     start = lax.axis_index("replica") * piece
     wq = lax.dynamic_slice_in_dim(w_query, start, piece)
     wk = lax.dynamic_slice_in_dim(w_key, start, piece)
@@ -1247,7 +1585,20 @@
         ],
         axis=2,
     ).swapaxes(0, 1)
-    head_w = gather(exchange(sent), "replica", 1).reshape(width, 2 * HD)
+    cols = 2 * HD
+    gain_stack = jnp.stack([gain_attn_in, gain_attn_out, gain_ffn_in, gain_ffn_out])
+    own_gains = jnp.pad(gain_stack.reshape(-1), (0, ROW_TILE * cols - gain_stack.size))
+    sent = jnp.concatenate(
+        [
+            sent.reshape(shards, piece // ROW_TILE, ROW_TILE, cols),
+            jnp.broadcast_to(own_gains.reshape(1, 1, ROW_TILE, cols), (shards, 1, ROW_TILE, cols)),
+        ],
+        axis=1,
+    )
+    x_group, head_w, all_gains = head_call(7, tokens, sent)
+    head_w = head_w.reshape(width, cols)
+    gains = all_gains.reshape(shards, -1)[:, : gain_stack.size].reshape(shards, 4, w_rows)
+    gains = gains.swapaxes(0, 1).reshape(4, width).astype(F32)
 
     segment_row = segment_ids[0]
     smaller = jnp.sum((segment_row[:, None] < segment_row[None, :]).astype(jnp.int32), axis=0)
@@ -1313,7 +1664,8 @@
     hidden_parts, raw_parts = (hidden_first, hidden_second), (raw_first, raw_second)
     outs, gain_four = (out_first, out_second), (g4_first, g4_second)
 
-    sums = [ReplicaSum(over_tokens(d_gates, d_ups, glus, normed_groups, d_groups))]
+    ffn_part = over_tokens(d_gates, d_ups, glus, normed_groups, d_groups)
+    ffn_sum = lax.psum(ffn_part, "replica")
 
     def back(d_normed, c):
         rows = slice(c * size, (c + 1) * size)
@@ -1325,20 +1677,15 @@
         return d_hidden, d_raw.astype(BF16), g2, g3
 
     d_hidden_first, d_attn_first, g2_first, g3_first = back(d_normed_first, 0)
-    d_attn_0, d_normed_second, *got = comm_call(
-        3, d_attn_first, d_part_1, swaps=all_sends(sums)
-    )
-    all_receive(sums, got)
+    ffn_part, d_attn_first = lax.optimization_barrier((ffn_part, d_attn_first))
+    d_attn_0, d_normed_second = comm_call(3, d_attn_first, d_part_1)
     d_hidden_second, d_attn_second, g2_second, g3_second = back(d_normed_second, 1)
-    d_attn_1, *got = comm_call(4, d_attn_second, swaps=all_sends(sums))
-    all_receive(sums, got)
+    (d_attn_1,) = comm_call(4, d_attn_second)
     d_hidden = jnp.concatenate([d_hidden_first, d_hidden_second])
     gain_two, gain_three = (g2_first, g2_second), (g3_first, g3_second)
-    dq, dk, dv, grad_out, *got = attend_back_call(
-        6, queries, keys, values, low_row, lse, attended, d_attn_0, d_attn_1, w_output, table,
-        all_sends(sums),
-    )
-    all_receive(sums, got)
+    dq, dk, dv, grad_out = attend_back_call(
+        queries, keys, values, low_row, lse, attended, d_attn_0, d_attn_1, w_output, table
+    )
     dkv_low = jnp.concatenate([dk[:, :HALF], dv[:, :HALF]], axis=1)
     dkv_high = jnp.concatenate([dk[:, HALF:], dv[:, HALF:]], axis=1)
     dkv_mine = jnp.where(first_core, dkv_low, dkv_high).astype(F32)
@@ -1348,24 +1695,22 @@
     turned = jnp.concatenate([dk_half[:, QUARTER:], dk_half[:, :QUARTER]], axis=1)
     dk_lin = dk_half * own[:, :HALF] - turned * own[:, HALF:]
     d_lin = jnp.concatenate([dq, dk_lin.astype(BF16), dkv[:, HALF:].astype(BF16)], axis=1)
-    part, d_lin = lax.optimization_barrier((dot(d_lin, head_w, NT).astype(BF16), d_lin))
-    d_normed, *got = comm_call(5, part=part, swaps=all_sends(sums))
-    all_receive(sums, got)
+    part = dot(d_lin, head_w, NT).astype(BF16)
     grad_head = dot(normed, d_lin, TN)
     gain_one = jnp.sum(grad_head * head_w.astype(F32), axis=1) / gains[0]
+    gain_terms = jnp.stack([gain_one, sum(gain_two), sum(gain_three), sum(gain_four)], axis=1)
+    padded = jnp.pad(gain_terms, ((0, 0), (0, HALF - gain_terms.shape[1])))
+    cut = HD + HALF
+    moved = (shards, w_rows // ROW_TILE, ROW_TILE)
+    head_a = grad_head[:, :cut].astype(BF16).reshape(*moved, cut)
+    head_b = jnp.concatenate([grad_head[:, cut:], padded], axis=1).astype(BF16).reshape(*moved, HD)
+    d_normed, left, right, out_left, out_right = tail_call(
+        5, part, head_a, head_b, grad_out[:, : width // 2], grad_out[:, width // 2 :]
+    )
+    left = left.reshape(shards, w_rows, cut).astype(F32)
+    right = right.reshape(shards, w_rows, HD).astype(F32)
     _, pull = jax.vjp(rms_scaled, x_float, gains[0])
     input_grad = d_hidden + pull(d_normed)[0]
-
-    gain_terms = jnp.stack([gain_one, sum(gain_two), sum(gain_three), sum(gain_four)], axis=1)
-    padded = jnp.pad(gain_terms, ((0, 0), (0, HALF - gain_terms.shape[1])))
-    moved = jnp.concatenate([grad_head, padded], axis=1).astype(BF16)
-    moved = moved.reshape(shards, w_rows, moved.shape[1])
-    cut = HD + HALF
-    left = halve(halve(moved[:, :, :cut], 1, 1), 1, 2)
-    right = halve(halve(moved[:, :, cut:], 1, 2), 1, 1)
-    traded = exchange(jnp.concatenate([left, right], axis=2))
-    left = double(double(traded[:, :, :cut], 1, 2), 1, 1).astype(F32)
-    right = double(double(traded[:, :, cut:], 1, 1), 1, 2).astype(F32)
     grad_query = (
         left[:, :, :HD].reshape(H, w_rows, 2, 2, QUARTER).transpose(1, 0, 3, 2, 4)
     ).reshape(w_rows, H * HD)
@@ -1376,8 +1721,11 @@
         .reshape(w_rows, KV * HD)
     )
     grad_value = right[:, :, :HALF].transpose(1, 0, 2).reshape(w_rows, KV * HD)
-    grad_out_proj = sum_replicas(grad_out)
-    grad_gate, grad_up, grad_down = sums[0].thirds()
+    grad_out_proj = jnp.concatenate([out_left, out_right], axis=1).astype(F32)
+    units = w_gate.shape[0]
+    grad_gate, grad_up, grad_down = (
+        ffn_sum[n * units : (n + 1) * units].astype(F32) for n in range(3)
+    )
     gain_shares = jnp.sum(right[:, :, HALF : HALF + gain_terms.shape[1]], axis=0).T
     return (
         jnp.concatenate(outs),

time: 1070 us -> 937 us (0.88); the launches traced: 1070 us -> 922 us
  waiting for transfers between devices: 142 us -> 0.02 us
  Pallas kernels: 647 us -> 752 us
  other arithmetic: 112 us -> 72 us
  blocking collectives: 37.2 us -> 0 us
  starting transfers between devices: 21.7 us -> 2.33 us
  local copies, waits for them, and re-layouts: 75.9 us -> 62.7 us
    pallas_call x1 -> x3, Pallas kernels: 48.4 us -> 290 us  [the longest x1 155 us: tail_call(): pl.pallas_call(tail_kernel, in_specs=[ANYWHERE] * 5, out_specs=[ANYWHERE]...]
    pallas_call x8 -> x7, Pallas kernels: 519 us -> 383 us  [comm_call(): pl.pallas_call(kernel, in_specs=[ANYWHERE] * len(ins), out_specs=[ANYWHER...]
    all_gather x2 -> x0, waiting for transfers between devices: 96.4 us -> none  [gather(): return lax.all_gather(x, axis_name, axis=axis, tiled=True)]
    ppermute x16 -> x0, waiting for transfers between devices: 32.9 us -> none  [partner(): return lax.ppermute(x, 'replica', [(r, r ^ bit) for r in range(n)])]
    all_to_all x1 -> x0, blocking collectives: 23 us -> none  [exchange(): return lax.all_to_all(x, 'shard', 0, 0, tiled=True)]
    convert_element_type x19 -> x5, other arithmetic: 37.3 us -> 20.1 us  [the longest x1 15.2 us: fast_on_device(): ffn_sum[n * units:(n + 1) * units].astype(F32)]
    ppermute x16 -> x0, starting transfers between devices: 16.8 us -> none  [partner(): return lax.ppermute(x, 'replica', [(r, r ^ bit) for r in range(n)])]
    all_gather x1 -> x0, blocking collectives: 14.2 us -> none  [gather(): return lax.all_gather(x, axis_name, axis=axis, tiled=True)]
  transfers between devices with their start and end apart: 21 -> 3, of which waited for: 13 -> 0; matrix products, arithmetic and copies ran while one was open for 8% -> 7% of each run, Pallas kernels for 10% -> 32%
where the time goes in v3:
time: 937 us; the launch traced here: 922 us
  Pallas kernels  752 us (80%)
  other arithmetic  72 us (8%)
  local copies, waits for them, and re-layouts  62.7 us (7%)
  matrix products  17.3 us (2%)
  between operations  15.2 us (2%)
    pallas_call x7, Pallas kernels, comm_call(): pl.pallas_call(kernel, in_specs=[ANYWHERE] * len(ins), out_specs=[ANYWHER...  383 us
    pallas_call x1, Pallas kernels, tail_call(): pl.pallas_call(tail_kernel, in_specs=[ANYWHERE] * 5, out_specs=[ANYWHERE]...  155 us
    pallas_call x1, Pallas kernels, head_call(): pl.pallas_call(head_kernel, in_specs=[ANYWHERE] * 2, out_specs=[ANYWHERE]...  101 us
    pallas_call x1, Pallas kernels, over_tokens(): pl.pallas_call(over_tokens_kernel, grid=(3 * tiles,), in_specs=[some(0),...  44.4 us
    unnamed x100, local copies, waits for them, and re-layouts  34 us
    pallas_call x1, Pallas kernels, attend_back_call(): pl.pallas_call(attend_back_kernel, grid=(rows // BLOCK,), in_specs=[rows_...  33.2 us
    pallas_call x1, Pallas kernels, attend_call(): pl.pallas_call(attend_kernel, grid=(rows // BLOCK,), in_specs=[rows_spec(...  22.6 us
  transfers between devices with their start and end apart: 3, of which 0 were waited for; matrix products, arithmetic and copies ran while one was open for 7% of the time, Pallas kernels for 32%

profile of v3, /device:TPU:0, one launch (start us, length us, event | category | flops | bytes accessed | tf_op | source)
XLA Modules:
  0.0 921.8 jit_solution(8179412947696747718)
XLA Ops:
  16.8 101.4 %head.1 = (bf16[2048,2304]{1,0:T(8,128)(2,1)S(1)}, bf16[8,36,8,512]{3,2,1,0:T(8,128)(2,1)S(1)}, bf16[8,8,512]{2,1,0:T(8,128)(2,1)S(1)}) custom-call(bf16[256,2304]{1,0:T(8,128)(2,1)S(1)} %copy-done.2, bf16[8,10,8,512]{3,2,1,0:T(8,128)(2,1)S(1)} %pad_maximum_fusion.9.sent_hbm), custom_call_target="tpu_custom_call" | custom-call | bytes 471859200 | tf_op jit(solution)/shard_map/head/pallas_call | solution.py:1373
  118.2 3.7 copy-done.5
  123.7 3.7 multiply_sine_fusion
  127.4 2.7 fusion.28
  130.1 8.5 concatenate.57.tab_ref
  140.2 12.1 %qkv.1 = (bf16[2048,2304]{1,0:T(8,128)(2,1)}, bf16[2048,256]{1,0:T(8,128)(2,1)S(1)}, bf16[2048,256]{1,0:T(8,128)(2,1)S(1)}) custom-call(bf16[2048,2304]{1,0:T(8,128)(2,1)} %copy-done.5, f32[1,2304]{1,0:T(1,128)S(1)} %slice.161.gain_ref, bf16[2304,512]{1,0:T(8,128)(2,1)S(1)} %bitcast.46, f32[2048,512]{1,0:T(8,128)} %concatenate.57.tab_ref), custom_call_target="tpu_custom_call" | custom-call | flops 4831838208 | bytes 18874368 | tf_op jit(solution)/shard_map/qkv/pallas_call | solution.py:432
  160.9 22.6 %attend.1 = (bf16[2048,256]{1,0:T(8,128)(2,1)S(1)}, f32[1,2048]{1,0:T(1,128)S(1)}, bf16[1024,2304]{1,0:T(8,128)(2,1)}, bf16[1024,2304]{1,0:T(8,128)(2,1)}) custom-call(bf16[2048,256]{1,0:T(8,128)(2,1)S(1)} %copy-done.11, bf16[2048,256]{1,0:T(8,128)(2,1)S(1)} %pad_maximum_fusion.3.k_ref, bf16[2048,256]{1,0:T(8,128)(2,1)S(1)} %pad_maximum_fusion.4.v_ref, ...), custom_call_target="tpu_custom_call" | custom-call | flops 5637144576 | bytes 9437184 | tf_op jit(solution)/shard_map/attend/pallas_call | solution.py:453
  184.6 45.8 %comm0.1 = f32[128,2304]{1,0:T(8,128)} custom-call(bf16[1024,2304]{1,0:T(8,128)(2,1)} %get-tuple-element.62.refs_0_), custom_call_target="tpu_custom_call" | custom-call | bytes 70778880 | tf_op jit(solution)/shard_map/comm0/pallas_call | solution.py:1018
  233.3 2.3 multiply_convert_fusion.1.refs_0_
  235.6 58.7 %comm1.2 = (bf16[1024,2304]{1,0:T(8,128)(2,1)}, bf16[1024,1152]{1,0:T(8,128)(2,1)}, bf16[1024,1152]{1,0:T(8,128)(2,1)}, bf16[1024,1152]{1,0:T(8,128)(2,1)}, bf16...) custom-call(bf16[128,2304]{1,0:T(8,128)(2,1)} %multiply_convert_fusion.1.refs_0_, bf16[1152,2304]{1,0:T(8,128)(2,1)} %refs_1_.7, ...), custom_call_target="tpu_custom_call" | custom-call | flops 16307453952 | bytes 141557760 | tf_op jit(solution)/shard_map/comm1/pallas_call | solution.py:1018
  297.2 57.7 %comm1.3 = (bf16[1024,2304]{1,0:T(8,128)(2,1)}, bf16[1024,1152]{1,0:T(8,128)(2,1)}, bf16[1024,1152]{1,0:T(8,128)(2,1)}, bf16[1024,1152]{1,0:T(8,128)(2,1)}, bf16...) custom-call(bf16[128,2304]{1,0:T(8,128)(2,1)} %multiply_convert_fusion.refs_0_, bf16[1152,2304]{1,0:T(8,128)(2,1)} %refs_1_.7, ...), custom_call_target="tpu_custom_call" | custom-call | flops 16307453952 | bytes 141557760 | tf_op jit(solution)/shard_map/comm1/pallas_call | solution.py:1018
  357.0 3.0 add_convert_fusion.1
  360.0 59.4 %comm2.2 = (bf16[1024,2304]{1,0:T(8,128)(2,1)}, bf16[1024,1152]{1,0:T(8,128)(2,1)}, bf16[1024,1152]{1,0:T(8,128)(2,1)}, bf16[1024,2304]{1,0:T(8,128)(2,1)}, f32[128,2304]{1,0:T(8,128)}) custom-call(bf16[128,2304]{1,0:T(8,128)(2,1)} %get-tuple-element.180.refs_0_, bf16[1152,2304]{1,0:T(8,128)(2,1)} %refs_1_.7, bf16[1152,2304]{1,0:T(8,128)(2,1)} %refs_2_.7, ...), custom_call_target="tpu_custom_call" | custom-call | flops 16307453952 | bytes 141557760 | tf_op jit(solution)/shard_map/comm2/pallas_call | solution.py:1018
  423.4 58.0 %comm2.3 = (bf16[1024,2304]{1,0:T(8,128)(2,1)}, bf16[1024,1152]{1,0:T(8,128)(2,1)}, bf16[1024,1152]{1,0:T(8,128)(2,1)}, bf16[1024,2304]{1,0:T(8,128)(2,1)}, f32[128,2304]{1,0:T(8,128)}) custom-call(bf16[128,2304]{1,0:T(8,128)(2,1)} %get-tuple-element.177.refs_0_, bf16[1152,2304]{1,0:T(8,128)(2,1)} %refs_1_.7, bf16[1152,2304]{1,0:T(8,128)(2,1)} %refs_2_.7, ...), custom_call_target="tpu_custom_call" | custom-call | flops 16307453952 | bytes 141557760 | tf_op jit(solution)/shard_map/comm2/pallas_call | solution.py:1018
  483.5 2.1 multiply_reduce_fusion.8
  487.9 44.4 %over_tokens.1 = bf16[3456,2304]{1,0:T(8,128)(2,1)} custom-call(bf16[1024,1152]{1,0:T(8,128)(2,1)S(1)} %copy-done.14, bf16[1024,1152]{1,0:T(8,128)(2,1)S(1)} %copy-done.15, bf16[1024,1152]{1,0:T(8,128)(2,1)} %get-tuple-element.77.b0, bf16[1024,1152]{1,0:T(8,128)(2,1)} %get-tuple-element.78.b1, bf16[1024,1152]{1,0:T(8,128)(2,1)} %get-tuple-element.79.c0, ...), custom_call_target="tpu_custom_call" | custom-call | flops 32614907904 | bytes 37748736 | tf_op jit(solution)/shard_map/over_tokens/pallas_call | solution.py:1429
  533.5 5.9 maximum_select_fusion
  539.4 60.4 %comm3.1 = (bf16[1024,2304]{1,0:T(8,128)(2,1)}, f32[128,2304]{1,0:T(8,128)}) custom-call(bf16[128,2304]{1,0:T(8,128)(2,1)} %fusion.4.refs_0_, bf16[1024,2304]{1,0:T(8,128)(2,1)} %get-tuple-element.86.refs_1_), custom_call_target="tpu_custom_call" | custom-call | bytes 141557760 | tf_op jit(solution)/shard_map/comm3/pallas_call | solution.py:1018
  601.8 2.1 multiply_reduce_fusion.7
  605.1 43.3 %comm4.1.end_ref = bf16[1024,2304]{1,0:T(8,128)(2,1)} custom-call(bf16[128,2304]{1,0:T(8,128)(2,1)} %fusion.6.refs_0_), custom_call_target="tpu_custom_call" | custom-call | bytes 70778880 | tf_op jit(solution)/shard_map/comm4/pallas_call | solution.py:1018
  648.5 33.2 %attend_back.1 = (bf16[2048,256]{1,0:T(8,128)(2,1)S(1)}, bf16[2048,256]{1,0:T(8,128)(2,1)S(1)}, bf16[2048,256]{1,0:T(8,128)(2,1)S(1)}, bf16[256,2304]{1,0:T(8,128)(2,1)}) custom-call(bf16[2048,256]{1,0:T(8,128)(2,1)S(1)} %copy-done.12, bf16[2048,256]{1,0:T(8,128)(2,1)S(1)} %pad_maximum_fusion.3.k_ref, bf16[2048,256]{1,0:T(8,128)(2,1)} %copy-done.4, ...), custom_call_target="tpu_custom_call" | custom-call | flops 11274289152 | bytes 9437184 | tf_op jit(solution)/shard_map/attend_back/pallas_call | solution.py:480
  691.3 9.8 %multiply_reduce_fusion = (f32[2304]{0:T(1024)S(1)}, bf16[2304,512]{1,0:T(8,128)(2,1)S(1)}) fusion(bf16[8,36,8,512]{3,2,1,0:T(8,128)(2,1)S(1)} %copy-done.8, bf16[2048,2304]{1,0:T(8,128)(2,1)} %get-tuple-element.94, bf16[2048,128]{1,0:T(8,128)(2,1)S(1)} %slice.273, bf16[2048,128]{1,0:T(8,128)(2,1)S(1)} %fusion.8, bf16[2048,256]{1,0:T(8,128)(2,1)S(1)} %get-tuple-element.91), kind=kOutput, calls=%fused_computation.4 | convolution fusion | flops 4842846208 | bytes 16262144 | tf_op jit(solution)/shard_map/dot_general | solution.py:273
  707.5 7.5 convolution_convert_fusion.part_in
  715.0 155.2 %tail.1 = (f32[256,2304]{1,0:T(8,128)}, bf16[8,36,8,384]{3,2,1,0:T(8,128)(2,1)}, bf16[8,36,8,256]{3,2,1,0:T(8,128)(2,1)}, bf16[256,1152]{1,0:T(8,128)(2,1)}, bf16[256,1152]{1,0:T(8,128)(2,1)}) custom-call(bf16[2048,2304]{1,0:T(8,128)(2,1)} %convolution_convert_fusion.part_in, bf16[8,36,8,384]{3,2,1,0:T(8,128)(2,1)} %bitcast.50, ...), custom_call_target="tpu_custom_call" | custom-call | bytes 141557760 | tf_op jit(solution)/shard_map/tail/pallas_call | solution.py:1252
  874.2 2.9 copy.64
  877.0 2.7 copy.59
  879.7 3.0 copy.62
  882.8 2.3 copy.63
  885.1 2.1 copy.57
  887.2 2.1 copy.61
  897.1 2.1 fusion
  899.2 15.2 %slice_convert_fusion = (f32[1152,2304]{1,0:T(8,128)}, f32[1152,2304]{1,0:T(8,128)}, f32[1152,2304]{1,0:T(8,128)}) fusion(bf16[3456,2304]{1,0:T(8,128)(2,1)} %all-reduce.5.cloned.1.call-done), kind=kLoop, calls=%fused_computation.1 | loop fusion | flops 7962624 | bytes 47775744 | tf_op jit(solution)/shard_map/convert_element_type | solution.py:1727
  (200 shorter events, 70.6 us)
Async XLA Ops:
  7.2 6.8 copy-start
  7.2 892.0 %all-reduce.5.cloned.1.call-start = ((), (), s32[]{:S(2)}) async-start(), calls=%async_computation | async-start | bytes 31850496 | tf_op jit(solution)/shard_map/psum | solution.py:1668
  118.2 3.7 copy-start.5
  130.1 8.5 copy-start.21
  130.1 8.5 copy-start.23
  138.6 1.7 copy-start.7
  153.3 4.1 collective-permute-start
  153.9 1.7 copy-start.38
  159.1 24.5 %copy-start.4 = (bf16[2048,256]{1,0:T(8,128)(2,1)}, bf16[2048,256]{1,0:T(8,128)(2,1)S(1)}, u32[]{:S(2)}) copy-start(bf16[2048,256]{1,0:T(8,128)(2,1)S(1)} %pad_maximum_fusion.4.v_ref) | copy-start | bytes 3145732
  159.1 1.8 copy-start.9
  184.5 47.4 %copy-start.31 = (f32[256,2304]{1,0:T(8,128)S(1)}, f32[256,2304]{1,0:T(8,128)}, u32[]{:S(2)}) copy-start(f32[256,2304]{1,0:T(8,128)} %convert_element_type.93) | copy-start | bytes 7077892
  297.2 59.2 %copy-start.16 = (f32[256,2304]{1,0:T(8,128)S(1)}, f32[256,2304]{1,0:T(8,128)}, u32[]{:S(2)}) copy-start(f32[256,2304]{1,0:T(8,128)} %convert_element_type.102) | copy-start | bytes 7077892
  481.4 2.1 copy-start.34
  483.5 3.3 copy-start.15
  485.6 2.3 copy-start.14
  539.4 62.2 %copy-start.20 = (f32[128,2304]{1,0:T(8,128)S(1)}, f32[128,2304]{1,0:T(8,128)}, u32[]{:S(2)}) copy-start(f32[128,2304]{1,0:T(8,128)} %get-tuple-element.64) | copy-start | bytes 3538948
  599.8 2.0 copy-start.17
  605.1 43.4 %copy-start.12 = (bf16[2048,256]{1,0:T(8,128)(2,1)S(1)}, bf16[2048,256]{1,0:T(8,128)(2,1)}, u32[]{:S(2)}) copy-start(bf16[2048,256]{1,0:T(8,128)(2,1)} %copy-done.10) | copy-start | bytes 3145732
  681.8 2.1 copy-start.35
  681.8 2.1 copy-start.36
  682.2 4.6 collective-permute-start.1
  683.9 1.7 copy-start.39
  687.2 2.5 copy-start.42
  687.3 2.1 copy-start.33
  689.4 2.0 copy-start.8
  689.8 11.4 %copy-start.44 = (bf16[2048,128]{1,0:T(8,128)(2,1)}, bf16[2048,128]{1,0:T(8,128)(2,1)S(1)}, u32[]{:S(2)}) copy-start(bf16[2048,128]{1,0:T(8,128)(2,1)S(1)} %fusion.8) | copy-start | bytes 1572868
  872.0 2.2 copy-start.24
  879.7 3.0 slice-start
  889.3 2.7 copy-start.32
  894.6 1.7 copy-start.26
  894.6 2.5 copy-start.28
  899.2 15.2 %copy-start.1 = (bf16[288,2048]{1,0:T(8,128)(2,1)S(1)}, bf16[288,2048]{1,0:T(8,128)(2,1)}, u32[]{:S(2)}) copy-start(bf16[288,2048]{1,0:T(8,128)(2,1)} %param.15) | copy-start | bytes 3538948
  (18 other events, 24.8 us)
Sparse Core Ops, SparseCore 0:
  532.4 354.4 all-reduce.4
